TPU v7x, 32 devices: a whole 2x2x4 slice. The times are simulated.
32 devices in a mesh: tile: 16 (over z, x, core), group: 2 (over y).
Axes of the slice: x: 2, y: 2, z: 4, core: 2. Of those that a mesh axis runs over, the one named last changes fastest.
Arguments:
- state: float32 [8, 5, 16, 128, 128], P('group', None, 'tile'), may hold values from -6 to 6
- courant_x: float32 [8], P('group'), may hold values from -0.35 to 0.35
- courant_y: float32 [8], P('group'), may hold values from -0.35 to 0.35
- diffusion: float32 [5], replicated, may hold values from 0.02 to 0.07
- neighbours: int32 [9, 16, 128, 128], P(None, 'tile'), may hold values from 0 to 16899, as said below
- w_in: bfloat16 [360, 256], replicated, may hold values from -0.3125 to 0.3125
- w_mid: bfloat16 [256, 256], replicated, may hold values from -0.375 to 0.375
- w_out: bfloat16 [256, 40], replicated, may hold values from -0.375 to 0.375
Outputs:
- updated: float32 [8, 5, 16, 128, 128], P('group', None, 'tile')
Inputs may be any that keep to these rules, and one draw needn't show every extreme that they name: `neighbours`: for each column the nine entries name the cells of its 3 x 3 neighbourhood, each once, in one of eight rotated or mirrored orders; cells are numbered in the tile extended by one cell on every side, row by row with 130 cells a row.
All inputs are finite; a program needn't handle non-finite values.
Results may differ from a plain program's by a relative error of at most 0.0016.
Values may be sent and summed in bfloat16 or wider, within the bound.
No kernel may reach another device: no remote copies, remote signals or barrier semaphores. Data moves between devices by JAX's collectives and lax.ppermute only.
A program may use at most 128 MiB of HBM per device.

v0:
```python
import functools

import jax
import jax.numpy as jnp
from jax import lax
from jax.experimental import pallas as pl
from jax.experimental.pallas import tpu as pltpu
from jax.sharding import PartitionSpec as P

TILE_ROWS = 8
DEEP = 3
EXTRA = 16
ROW_UNROLL = 2

F32 = jnp.float32
BF16 = jnp.bfloat16
VMEM_SPEC = pl.BlockSpec(memory_space=pltpu.VMEM)
ANY_SPEC = pl.BlockSpec(memory_space=pl.ANY)
PARAMS = pltpu.CompilerParams(vmem_limit_bytes=56 << 20)


def whole(ref):
    return ref[...]


def lanes_of(shape):
    return lax.broadcasted_iota(jnp.int32, shape, len(shape) - 1)


def edge_kernel(state_ref, east_ref, west_ref, rows_ref):
    chans, cells_x, cells_y = state_ref.shape
    slot = lax.broadcasted_iota(jnp.int32, (16, cells_y), 0)
    lane = lanes_of((16, cells_y))
    wanted = jnp.where(slot < 8, slot + cells_y - DEEP, slot - 8)
    valid = (slot % 8) < DEEP
    pick = jnp.where(valid & (lane == wanted), 1.0, 0.0).astype(BF16)
    for c in range(chans):
        block = state_ref[c].astype(BF16)
        strips = lax.dot_general(
            pick, block, (((1,), (1,)), ((), ())), preferred_element_type=F32
        ).astype(BF16)
        east_ref[c] = strips[0:8]
        west_ref[c] = strips[8:16]
        rows_ref[c] = jnp.concatenate(
            [state_ref[c, 0:8], state_ref[c, cells_x - 8 : cells_x]], axis=0
        ).astype(BF16)


def transport_kernel(
    state_ref, coef_ref, west_ref, east_ref, up_ref, upw_ref, upe_ref,
    down_ref, downw_ref, downe_ref, *rest, cells_x,
):
    moved_ref, mine0, mine1, theirs0, theirs1 = rest[:5]
    raw, once, twice, strips, border, extra = rest[5:]
    chans = state_ref.shape[0] // cells_x
    width = state_ref.shape[1]
    half = cells_x // 2
    part = half // 2
    own = lax.axis_index("group")
    place = lax.axis_index("tile") % TILE_ROWS
    lane = lanes_of((chans, width))
    is_east = lane < width // 2
    keep = jnp.where(
        is_east,
        jnp.where(place == TILE_ROWS - 1, 0.0, 1.0),
        jnp.where(place == 0, 0.0, 1.0),
    )
    for s, refs in enumerate(
        ((west_ref, east_ref), (upw_ref, upe_ref), (downw_ref, downe_ref))
    ):
        for side in range(2):
            strips[s, side] = refs[side][...].astype(F32)
    border[0] = up_ref[...].astype(F32)
    border[1] = down_ref[...].astype(F32)

    def edge_slab(source, row):
        slab = jnp.zeros((chans, width), F32)
        for k in range(DEEP):
            wk = strips[source, 0, pl.ds(k, chans, stride=8), :]
            ek = strips[source, 1, pl.ds(k, chans, stride=8), :]
            at = width - DEEP + k
            slab = jnp.where(lane == at, pltpu.roll(wk, lax.rem(at - row + width, width), 1), slab)
            slab = jnp.where(lane == k, pltpu.roll(ek, lax.rem(k - row + width, width), 1), slab)
        return slab

    def fill(i, _):
        raw[i + DEEP, 0] = state_ref[pl.ds(i, chans, stride=cells_x), :]
        raw[i + DEEP, 1] = edge_slab(0, i)
        return 0

    lax.fori_loop(0, cells_x, fill, 0, unroll=4)
    for k in range(DEEP):
        raw[k, 0] = border[0, pl.ds(16 - DEEP + k, chans, stride=16), :]
        raw[k, 1] = edge_slab(1, jnp.int32(cells_x - DEEP + k))
        raw[cells_x + DEEP + k, 0] = border[1, pl.ds(k, chans, stride=16), :]
        raw[cells_x + DEEP + k, 1] = edge_slab(2, jnp.int32(k))

    def sweep(src, r):
        c0, cxl, cxu, cyl, cyu = [coef_ref[n] for n in range(5)]
        q, e = src[r, 0], src[r, 1]
        ql, el = pltpu.roll(q, 1, 1), pltpu.roll(e, 1, 1)
        qu, eu = pltpu.roll(q, width - 1, 1), pltpu.roll(e, width - 1, 1)
        first, last = lane == 0, lane == width - 1
        ql, el = jnp.where(first, el, ql), jnp.where(first, ql, el)
        qu, eu = jnp.where(last, eu, qu), jnp.where(last, qu, eu)
        q2 = c0 * q + cxl * src[r - 1, 0] + cxu * src[r + 1, 0] + cyl * ql + cyu * qu
        e2 = c0 * e + cxl * src[r - 1, 1] + cxu * src[r + 1, 1] + cyl * el + cyu * eu
        return q2, e2 * keep

    def first_sweep(r, _):
        q2, e2 = sweep(raw, r)
        once[r, 0] = q2
        once[r, 1] = e2
        return 0

    lax.fori_loop(1, cells_x + 2 * DEEP - 1, first_sweep, 0, unroll=ROW_UNROLL)

    def second_sweep(i, _):
        q2, e2 = sweep(once, i + DEEP)
        moved_ref[pl.ds(i, chans, stride=cells_x), :] = q2
        twice[i + 1] = e2
        return 0

    lax.fori_loop(0, cells_x, second_sweep, 0, unroll=ROW_UNROLL)
    above, twice[0] = sweep(once, DEEP - 1)
    below, twice[cells_x + 1] = sweep(once, cells_x + DEEP)

    def row(i):
        if i < 0:
            return above
        if i >= cells_x:
            return below
        return moved_ref[pl.ds(i, chans, stride=cells_x), :]

    for q in range(2):
        base = q * half

        def gather(l, carry):
            aw, ae = carry
            e2 = twice[base + l]
            aw = jnp.where(lane == l, pltpu.roll(e2, lax.rem(l + 1, width), 1), aw)
            ae = jnp.where(lane == l, pltpu.roll(e2, l, 1), ae)
            return aw, ae

        zero = jnp.zeros((chans, width), F32)
        aw, ae = lax.fori_loop(0, half + 2, gather, (zero, zero), unroll=2)
        items = (row(base - 1), row(base + half), aw, ae, row(base + part))
        for k in range(EXTRA):
            extra[q, pl.ds(k, chans, stride=EXTRA), :] = items[k] if k < len(items) else zero

    for c in range(chans):
        for dst0, dst1, q in ((mine0, mine1, own), (theirs0, theirs1, 1 - own)):
            start = pl.multiple_of(c * cells_x + q * half, 8)
            dst0[c, 0:EXTRA] = extra[q, pl.ds(c * EXTRA, EXTRA), :].astype(BF16)
            dst0[c, EXTRA : EXTRA + part] = moved_ref[pl.ds(start, part), :].astype(BF16)
            dst1[c] = moved_ref[pl.ds(start + part, part), :].astype(BF16)


def physics_kernel(chunk, table_ref, w1_ref, w2_ref, w3_ref, *rest):
    count = 2 if chunk == 0 else 4
    ins, rest = rest[:count], rest[count:]
    own_out, other_out, wide0, wide1, slab, packed, mask, table, stacked, terms, sem = rest
    chans, part, width = own_out.shape
    half = 2 * part
    pad = slab.shape[1] // 2
    both = 2 * pad
    own = lax.axis_index("group")
    top = own * half + chunk * part
    copies = []
    for n, k in enumerate((5, 7)):
        copies.append(
            pltpu.make_async_copy(table_ref.at[k, 0, pl.ds(top, part)], table.at[n], sem.at[n])
        )
        copies[-1].start()
    height0 = EXTRA + part
    for s in range(2):
        wide0[s] = ins[s][...].reshape(chans * height0, width).astype(F32)
        if chunk:
            wide1[s] = ins[2 + s][...].reshape(chans * part, width).astype(F32)

    slab[...] = jnp.zeros_like(slab)

    def source(s, l):
        if chunk == 0:
            if l < 0:
                return wide0[s, pl.ds(0, chans, stride=height0), :]
            if l >= part:
                return wide0[s, pl.ds(4, chans, stride=height0), :]
            return wide0[s, pl.ds(EXTRA + l, chans, stride=height0), :]
        if l < 0:
            return wide0[s, pl.ds(height0 - 1, chans, stride=height0), :]
        if l >= part:
            return wide0[s, pl.ds(1, chans, stride=height0), :]
        return wide1[s, pl.ds(l, chans, stride=part), :]

    for s in range(2):
        for l in range(-1, part + 1):
            slab[l + 1, pl.ds(s * pad, chans)] = source(s, l)
        for k in range(2):
            slab[part + 2 + k, pl.ds(s * pad, chans)] = wide0[s, pl.ds(2 + k, chans, stride=height0), :]

    lane = lanes_of((both, width))

    def shift(r, _):
        q = slab[r]
        idx = r + chunk * part
        low = jnp.where(lane == 0, pltpu.roll(slab[part + 2], lax.rem(width - idx, width), 1), pltpu.roll(q, 1, 1))
        high = jnp.where(lane == width - 1, pltpu.roll(slab[part + 3], lax.rem(2 * width - 1 - idx, width), 1), pltpu.roll(q, width - 1, 1))
        packed[0, r] = low.astype(BF16)
        packed[1, r] = q.astype(BF16)
        packed[2, r] = high.astype(BF16)
        return 0

    lax.fori_loop(0, part + 2, shift, 0, unroll=2)
    for copy in copies:
        copy.wait()
    rows_i = lax.broadcasted_iota(jnp.int32, (part, width), 0) + top
    centre = (rows_i + 1) * (width + 2) + lanes_of((part, width)) + 1
    along_y = table[0] - centre
    along_x = table[1] - centre
    turned = jnp.abs(along_x) == 1
    mask[0] = jnp.where(jnp.where(turned, along_y, along_x) < 0, 1.0, 0.0)
    mask[1] = jnp.where(jnp.where(turned, along_x, along_y) < 0, 1.0, 0.0)
    mask[2] = jnp.where(turned, 1.0, 0.0)

    rows_step = stacked.shape[1] // width

    def choose(m, a, b):
        return jnp.where(m, a, b), jnp.where(m, b, a)

    def block(b, _):
        for u in range(rows_step):
            l = b * rows_step + u
            m = []
            for n in range(3):
                line = jnp.broadcast_to(mask[n, pl.ds(l, 1), :], (16, width)).astype(BF16)
                m.append(jnp.concatenate([line] * (both // 16), axis=0) > 0.5)
            x = [[packed[bb, l + aa] for bb in range(3)] for aa in range(3)]
            for bb in range(3):
                x[0][bb], x[2][bb] = choose(m[0], x[2][bb], x[0][bb])
            for aa in range(3):
                x[aa][0], x[aa][2] = choose(m[1], x[aa][2], x[aa][0])
            for aa, bb in ((0, 1), (0, 2), (1, 2)):
                x[aa][bb], x[bb][aa] = choose(m[2], x[bb][aa], x[aa][bb])
            for k in range(9):
                stacked[pl.ds(k * both, both), pl.ds(u * width, width)] = x[k // 3][k % 3]
        dot = functools.partial(
            lax.dot_general,
            dimension_numbers=(((1,), (0,)), ((), ())),
            preferred_element_type=F32,
        )

        def silu(v):
            h = v * 0.5
            return (h * jnp.tanh(h) + h).astype(BF16)

        first = silu(dot(w1_ref[...], stacked[...]))
        second = silu(dot(w2_ref[...], first))
        tend = dot(w3_ref[...], second)
        for u in range(rows_step):
            l = b * rows_step + u
            cols = slice(u * width, (u + 1) * width)
            terms[0, pl.ds(l, chans, stride=part), :] = tend[0:chans, cols]
            terms[1, pl.ds(l, chans, stride=part), :] = tend[pad : pad + chans, cols]
        return 0

    lax.fori_loop(0, part // rows_step, block, 0)
    own_out[...] = terms[0].reshape(chans, part, width).astype(BF16)
    other_out[...] = terms[1].reshape(chans, part, width).astype(BF16)


def finish_kernel(moved_ref, a0, a1, b0, b1, out_ref):
    chans, part, width = a0.shape
    own = lax.axis_index("group")
    for q, pair in ((own, (a0, a1)), (1 - own, (b0, b1))):
        for n in range(2):
            rows = pl.ds(pl.multiple_of(q * 2 * part + n * part, 8), part)
            out_ref[:, rows, :] = moved_ref[:, rows, :] + pair[n][...].astype(F32)


def call(kernel, name, outs, ins, scratch=(), **cost):
    return pl.pallas_call(
        kernel,
        out_shape=outs,
        in_specs=ins,
        out_specs=jax.tree.map(lambda _: VMEM_SPEC, outs),
        scratch_shapes=list(scratch),
        compiler_params=PARAMS,
        name=name,
    )


def shards(state, courant_x, courant_y, diffusion, neighbours, w_in, w_mid, w_out):
    levels, fields, single, cells_x, cells_y = state.shape
    chans = levels * fields
    hidden = w_mid.shape[0]
    tiles = lax.axis_size("tile")
    half, part = cells_x // 2, cells_x // 4
    pad = -(-chans // 8) * 8
    block = state.reshape(chans, cells_x, cells_y)
    sds = jax.ShapeDtypeStruct

    strip = sds((chans, 8, cells_y), BF16)
    to_east, to_west, rows = call(
        edge_kernel, "edges", (strip, strip, sds((chans, 16, cells_y), BF16)), [VMEM_SPEC]
    )(block)

    def beside(by):
        return [(i, i + by) for i in range(tiles) if 0 <= i % TILE_ROWS + by < TILE_ROWS]

    from_west = lax.ppermute(to_east, "tile", beside(1))
    from_east = lax.ppermute(to_west, "tile", beside(-1))
    message = jnp.concatenate([rows, from_west, from_east], axis=1)

    def across(x, by):
        return lax.ppermute(x, "tile", [(i, (i + by) % tiles) for i in range(tiles)])

    up = across(message, TILE_ROWS)
    down = up if tiles == 2 * TILE_ROWS else across(message, -TILE_ROWS)

    ax = jnp.repeat(courant_x, fields)
    ay = jnp.repeat(courant_y, fields)
    nu = jnp.tile(diffusion, levels)
    coef = jnp.stack(
        [
            1.0 - jnp.abs(ax) - jnp.abs(ay) - 4.0 * nu,
            jnp.maximum(ax, 0.0) + nu,
            nu - jnp.minimum(ax, 0.0),
            jnp.maximum(ay, 0.0) + nu,
            nu - jnp.minimum(ay, 0.0),
        ]
    )
    coef = jnp.broadcast_to(coef[:, :, None], (5, chans, cells_y))

    def flat(x):
        return x.reshape(-1, cells_y)

    def split(x):
        return flat(x[:, 0:16]), flat(x[:, 16:24]), flat(x[:, 24:32])

    win0 = sds((chans, EXTRA + part, cells_y), BF16)
    win1 = sds((chans, part, cells_y), BF16)
    slabs = pltpu.VMEM((cells_x + 2 * DEEP, 2, chans, cells_y), F32)
    moved, mine0, mine1, theirs0, theirs1 = call(
        functools.partial(transport_kernel, cells_x=cells_x),
        "transport",
        (sds((chans * cells_x, cells_y), F32), win0, win1, win0, win1),
        [VMEM_SPEC] * 10,
        [
            slabs,
            slabs,
            pltpu.VMEM((cells_x + 2, chans, cells_y), F32),
            pltpu.VMEM((3, 2, chans * 8, cells_y), F32),
            pltpu.VMEM((2, chans * 16, cells_y), F32),
            pltpu.VMEM((2, chans * EXTRA, cells_y), F32),
        ],
    )(block.reshape(chans * cells_x, cells_y), coef, flat(from_west), flat(from_east), *split(up), *split(down))

    def swap(x):
        return lax.ppermute(x, "group", [(0, 1), (1, 0)])

    got0 = swap(theirs0)
    got1 = swap(theirs1)

    own = lax.axis_index("group")
    both = 2 * pad

    def ordered(w):
        return jnp.where(own == 0, w, w[::-1])

    w1 = ordered(w_in.reshape(2, chans, 9, hidden)).transpose(3, 2, 0, 1)
    w1 = jnp.pad(w1, ((0, 0), (0, 0), (0, 0), (0, pad - chans))).reshape(hidden, 9 * both)
    w3 = ordered(w_out.T.reshape(2, chans, hidden))
    w3 = jnp.pad(w3, ((0, 0), (0, pad - chans), (0, 0))).reshape(both, hidden)
    w2 = w_mid.T

    def physics(chunk, *windows):
        return call(
            functools.partial(physics_kernel, chunk),
            f"physics{chunk}",
            (win1, win1),
            [ANY_SPEC] + [VMEM_SPEC] * (3 + len(windows)),
            [
                pltpu.VMEM((2, chans * (EXTRA + part), cells_y), F32),
                pltpu.VMEM((2, chans * part, cells_y), F32),
                pltpu.VMEM((part + 4, both, cells_y), F32),
                pltpu.VMEM((3, part + 2, both, cells_y), BF16),
                pltpu.VMEM((3, part, cells_y), F32),
                pltpu.VMEM((2, part, cells_y), jnp.int32),
                pltpu.VMEM((9 * both, 16 * cells_y), BF16),
                pltpu.VMEM((2, chans * part, cells_y), F32),
                pltpu.SemaphoreType.DMA((2,)),
            ],
        )(neighbours, w1, w2, w3, *windows)

    own0, other0 = physics(0, mine0, got0)
    back0 = swap(other0)
    own1, other1 = physics(1, mine0, got0, mine1, got1)
    back1 = swap(other1)
    updated = call(
        finish_kernel, "finish", sds((chans, cells_x, cells_y), F32), [VMEM_SPEC] * 5
    )(moved.reshape(chans, cells_x, cells_y), own0, own1, back0, back1)
    return updated.reshape(levels, fields, single, cells_x, cells_y)


def solution(mesh):
    return jax.shard_map(
        shards,
        mesh=mesh,
        in_specs=(
            P("group", None, "tile", None, None),
            P("group"),
            P("group"),
            P(),
            P(None, "tile", None, None),
            P(),
            P(),
            P(),
        ),
        out_specs=P("group", None, "tile", None, None),
        check_vma=False,
    )
```

profile of v0, /device:TPU:24, one launch (start us, length us, event | category | flops | bytes accessed | tf_op | source)
XLA Modules:
  0.0 88.7 jit_solution(6474982487638929632)
XLA Ops:
  0.0 0.0 copy-start.10
  0.0 0.0 copy-start.11
  0.0 0.0 copy-start.9
  0.0 0.0 copy-start.1
  0.0 2.5 %edges.1 = (bf16[20,8,128]{2,1,0:T(8,128)(2,1)}, bf16[20,8,128]{2,1,0:T(8,128)(2,1)}, bf16[20,16,128]{2,1,0:T(8,128)(2,1)}) custom-call(f32[20,128,128]{2,1,0:T(8,128)} %bitcast.19), custom_call_target="tpu_custom_call" | custom-call | tf_op jit(solution)/shard_map/edges/pallas_call | solution.py:304
  2.5 1.9 %collective-permute-start = (bf16[20,8,128]{2,1,0:T(8,128)(2,1)}, bf16[20,8,128]{2,1,0:T(8,128)(2,1)S(1)}, u32[]{:S(2)}, u32[]{:S(2)}) collective-permute-start(bf16[20,8,128]{2,1,0:T(8,128)(2,1)} %get-tuple-element.17), channel_id=1, source_target_pairs={{0,2},{2,4},{4,6},{6,8},{8,10},{10,12},{12,14},{16,18},{18,20},{20... | collective-permute-start | bytes 122888 | tf_op jit(solution)/shard_map/ppermute | solution.py:311
  4.4 4.5 %collective-permute-start.1 = (bf16[20,8,128]{2,1,0:T(8,128)(2,1)}, bf16[20,8,128]{2,1,0:T(8,128)(2,1)S(1)}, u32[]{:S(2)}, u32[]{:S(2)}) collective-permute-start(bf16[20,8,128]{2,1,0:T(8,128)(2,1)} %get-tuple-element.18), channel_id=1, source_target_pairs={{2,0},{4,2},{6,4},{8,6},{10,8},{12,10},{14,12},{18,16},{20,18},{22... | collective-permute-start | bytes 122888 | tf_op jit(solution)/shard_map/ppermute | solution.py:312
  9.0 0.0 copy-done.10
  9.0 0.0 copy-done.11
  9.0 0.0 copy-done.9
  9.0 0.0 collective-permute-done
  9.0 0.0 copy-start.2
  9.1 1.9 %collective-permute-done.1 = bf16[20,8,128]{2,1,0:T(8,128)(2,1)S(1)} collective-permute-done((bf16[20,8,128]{2,1,0:T(8,128)(2,1)}, bf16[20,8,128]{2,1,0:T(8,128)(2,1)S(1)}, u32[]{:S(2)}, u32[]{:S(2)}) %collective-permute-start.1) | collective-permute-done | bytes 40992 | tf_op jit(solution)/shard_map/ppermute | solution.py:312
  10.9 0.0 copy-start.3
  10.9 0.9 %pad_maximum_fusion = bf16[20,32,128]{2,1,0:T(8,128)(2,1)S(1)} fusion(bf16[20,8,128]{2,1,0:T(8,128)(2,1)S(1)} %collective-permute-done.1, bf16[20,8,128]{2,1,0:T(8,128)(2,1)S(1)} %collective-permute-done, bf16[20,16,128]{2,1,0:T(8,128)(2,1)} %get-tuple-element.19), kind=kLoop, calls=%fused_computation.2 | loop fusion | flops 491520 | bytes 327680 | tf_op jit(solution)/shard_map/concatenate | solution.py:313
  11.9 0.4 collective-permute-start.2
  12.3 0.1 broadcast_subtract_fusion
  12.3 0.1 sub.70
  12.4 0.1 sub.68
  12.5 0.1 add.33
  12.6 0.1 add.31
  12.7 0.1 sub.66
  12.8 0.0 copy-done.1
  12.8 0.1 reshape.189
  12.9 8.3 %collective-permute-done.2 = bf16[20,32,128]{2,1,0:T(8,128)(2,1)S(1)} collective-permute-done((bf16[20,32,128]{2,1,0:T(8,128)(2,1)S(1)}, bf16[20,32,128]{2,1,0:T(8,128)(2,1)S(1)}, u32[]{:S(2)}, u32[]{:S(2)}) %collective-permute-start.2) | collective-permute-done | bytes 163872 | tf_op jit(solution)/shard_map/ppermute | solution.py:316
  21.2 0.6 slice.15
  21.8 0.0 copy-start.8
  21.8 0.6 slice_bitcast_fusion
  22.5 0.0 copy-start.7
  22.5 0.7 broadcast_in_dim.23.coef_ref
  23.2 0.0 copy-done.2
  23.2 0.0 copy-done.3
  23.2 27.2 %transport.1 = (f32[2560,128]{1,0:T(8,128)}, bf16[20,48,128]{2,1,0:T(8,128)(2,1)}, bf16[20,32,128]{2,1,0:T(8,128)(2,1)}, bf16[20,48,128]{2,1,0:T(8,128)(2,1)}, bf16[20,32,128]{2,1,0:T(8,128)(2,1)}) custom-call(f32[2560,128]{1,0:T(8,128)} %bitcast.20, f32[5,20,128]{2,1,0:T(8,128)} %broadcast_in_dim.23.coef_ref, bf16[160,128]{1,0:T(8,128)(2,1)} %bitcast.29, ...), custom_call_target="tpu_custom_call" | custom-call | tf_op jit(solution)/shard_map/transport/pallas_call | solution.py:344
  50.4 0.0 copy-start.12
  50.4 1.6 %collective-permute-start.3 = (bf16[20,48,128]{2,1,0:T(8,128)(2,1)}, bf16[20,48,128]{2,1,0:T(8,128)(2,1)S(1)}, u32[]{:S(2)}, u32[]{:S(2)}) collective-permute-start(bf16[20,48,128]{2,1,0:T(8,128)(2,1)} %get-tuple-element.22), channel_id=1, source_target_pairs={{0,1},{1,0},{2,3},{3,2},{4,5},{5,4},{6,7},{7,6},{8,9},{9,8},{10,11... | collective-permute-start | bytes 737288 | tf_op jit(solution)/shard_map/ppermute | solution.py:360
  51.9 0.1 fusion
  52.0 0.0 copy-done.8
  52.0 0.0 copy-done.7
  52.0 0.7 copy.14
  52.8 0.1 copy.18
  52.9 0.0 copy-done.12
  52.9 0.6 collective-permute-start.4
  53.4 0.6 pad.9
  54.1 0.8 copy.15.w1_ref
  54.9 7.2 %collective-permute-done.4.rest_3_ = bf16[20,32,128]{2,1,0:T(8,128)(2,1)S(1)} collective-permute-done((bf16[20,32,128]{2,1,0:T(8,128)(2,1)S(1)}, bf16[20,32,128]{2,1,0:T(8,128)(2,1)S(1)}, u32[]{:S(2)}, u32[]{:S(2)}) %collective-permute-start.4) | collective-permute-done | bytes 163872 | tf_op jit(solution)/shard_map/ppermute | solution.py:360
  62.1 0.0 copy-start.6
  62.1 0.0 collective-permute-done.3.rest_1_
  62.1 0.0 copy-start
  62.1 0.7 copy-done.6
  62.8 0.1 copy-done
  62.9 7.8 %physics1.1 = (bf16[20,32,128]{2,1,0:T(8,128)(2,1)}, bf16[20,32,128]{2,1,0:T(8,128)(2,1)}) custom-call(s32[9,1,128,128]{3,2,1,0:T(8,128)} %table_ref.3, bf16[256,432]{1,0:T(8,128)(2,1)} %copy.15.w1_ref, bf16[256,256]{1,0:T(8,128)(2,1)} %bitcast.22, bf16[48,256]{1,0:T(8,128)(2,1)} %bitcast.27, bf16[20,48,128]{2,1,0:T(8,128)(2,1)} %get-tuple-element.21.rest_0_, ...), custom_call_target="tpu_custom_call" | custom-call | tf_op jit(solution)/shard_map/physics1/pallas_call | solution.py:378
  70.7 1.6 %collective-permute-start.6 = (bf16[20,32,128]{2,1,0:T(8,128)(2,1)}, bf16[20,32,128]{2,1,0:T(8,128)(2,1)S(1)}, u32[]{:S(2)}, u32[]{:S(2)}) collective-permute-start(bf16[20,32,128]{2,1,0:T(8,128)(2,1)} %get-tuple-element.28), channel_id=1, source_target_pairs={{0,1},{1,0},{2,3},{3,2},{4,5},{5,4},{6,7},{7,6},{8,9},{9,8},{10,11... | collective-permute-start | bytes 491528 | tf_op jit(solution)/shard_map/ppermute | solution.py:360
  72.3 7.5 %physics0.1 = (bf16[20,32,128]{2,1,0:T(8,128)(2,1)}, bf16[20,32,128]{2,1,0:T(8,128)(2,1)}) custom-call(s32[9,1,128,128]{3,2,1,0:T(8,128)} %table_ref.3, bf16[256,432]{1,0:T(8,128)(2,1)} %copy.15.w1_ref, bf16[256,256]{1,0:T(8,128)(2,1)} %bitcast.23, bf16[48,256]{1,0:T(8,128)(2,1)} %bitcast.28, bf16[20,48,128]{2,1,0:T(8,128)(2,1)} %get-tuple-element.21.rest_0_, ...), custom_call_target="tpu_custom_call" | custom-call | tf_op jit(solution)/shard_map/physics0/pallas_call | solution.py:378
  79.8 0.6 collective-permute-start.5
  80.3 0.0 collective-permute-done.6.b1
  80.3 0.0 copy-start.4
  80.3 5.0 %collective-permute-done.5.b0 = bf16[20,32,128]{2,1,0:T(8,128)(2,1)S(1)} collective-permute-done((bf16[20,32,128]{2,1,0:T(8,128)(2,1)}, bf16[20,32,128]{2,1,0:T(8,128)(2,1)S(1)}, u32[]{:S(2)}, u32[]{:S(2)}) %collective-permute-start.5) | collective-permute-done | bytes 163872 | tf_op jit(solution)/shard_map/ppermute | solution.py:360
  85.4 0.0 copy-start.5
  85.4 0.0 copy-done.4
  85.4 0.7 copy-done.5
  86.0 2.7 %finish.1 = f32[20,128,128]{2,1,0:T(8,128)} custom-call(f32[20,128,128]{2,1,0:T(8,128)} %bitcast.21, bf16[20,32,128]{2,1,0:T(8,128)(2,1)} %get-tuple-element.23.a0, bf16[20,32,128]{2,1,0:T(8,128)(2,1)} %get-tuple-element.26.a1, bf16[20,32,128]{2,1,0:T(8,128)(2,1)} %copy-done.5, bf16[20,32,128]{2,1,0:T(8,128)(2,1)} %copy-done.4), custom_call_target="tpu_custom_call" | custom-call | tf_op jit(solution)/shard_map/finish/pallas_call | solution.py:400
  (6 shorter events, 0.1 us)
Async XLA Ops:
  0.0 9.0 %copy-start.10 = (f32[4]{0:T(128)S(1)}, f32[4]{0:T(128)}, u32[]{:S(2)}) copy-start(f32[4]{0:T(128)} %param.10) | copy-start | bytes 52
  0.0 9.0 %copy-start.11 = (f32[4]{0:T(128)S(1)}, f32[4]{0:T(128)}, u32[]{:S(2)}) copy-start(f32[4]{0:T(128)} %param.9) | copy-start | bytes 52
  0.0 9.0 %copy-start.9 = (f32[5]{0:T(128)S(1)}, f32[5]{0:T(128)}, u32[]{:S(2)}) copy-start(f32[5]{0:T(128)} %param.11) | copy-start | bytes 64
  0.0 12.8 %copy-start.1 = (bf16[360,256]{1,0:T(8,128)(2,1)S(1)}, bf16[360,256]{1,0:T(8,128)(2,1)}, u32[]{:S(2)}) copy-start(bf16[360,256]{1,0:T(8,128)(2,1)} %param.13) | copy-start | bytes 552964
  2.5 6.5 %collective-permute-start = (bf16[20,8,128]{2,1,0:T(8,128)(2,1)}, bf16[20,8,128]{2,1,0:T(8,128)(2,1)S(1)}, u32[]{:S(2)}, u32[]{:S(2)}) collective-permute-start(bf16[20,8,128]{2,1,0:T(8,128)(2,1)} %get-tuple-element.17), channel_id=1, source_target_pairs={{0,2},{2,4},{4,6},{6,8},{8,10},{10,12},{12,14},{16,18},{18,20},{20... | collective-permute-start | bytes 122888 | tf_op jit(solution)/shard_map/ppermute | solution.py:311
  4.4 6.5 %collective-permute-start.1 = (bf16[20,8,128]{2,1,0:T(8,128)(2,1)}, bf16[20,8,128]{2,1,0:T(8,128)(2,1)S(1)}, u32[]{:S(2)}, u32[]{:S(2)}) collective-permute-start(bf16[20,8,128]{2,1,0:T(8,128)(2,1)} %get-tuple-element.18), channel_id=1, source_target_pairs={{2,0},{4,2},{6,4},{8,6},{10,8},{12,10},{14,12},{18,16},{20,18},{22... | collective-permute-start | bytes 122888 | tf_op jit(solution)/shard_map/ppermute | solution.py:312
  9.0 14.1 %copy-start.2 = (bf16[20,8,128]{2,1,0:T(8,128)(2,1)}, bf16[20,8,128]{2,1,0:T(8,128)(2,1)S(1)}, u32[]{:S(2)}) copy-start(bf16[20,8,128]{2,1,0:T(8,128)(2,1)S(1)} %collective-permute-done) | copy-start | bytes 122884
  10.9 12.2 %copy-start.3 = (bf16[20,8,128]{2,1,0:T(8,128)(2,1)}, bf16[20,8,128]{2,1,0:T(8,128)(2,1)S(1)}, u32[]{:S(2)}) copy-start(bf16[20,8,128]{2,1,0:T(8,128)(2,1)S(1)} %collective-permute-done.1) | copy-start | bytes 122884
  11.9 9.3 %collective-permute-start.2 = (bf16[20,32,128]{2,1,0:T(8,128)(2,1)S(1)}, bf16[20,32,128]{2,1,0:T(8,128)(2,1)S(1)}, u32[]{:S(2)}, u32[]{:S(2)}) collective-permute-start(bf16[20,32,128]{2,1,0:T(8,128)(2,1)S(1)} %pad_maximum_fusion), channel_id=1, source_target_pairs={{0,16},{2,18},{4,20},{6,22},{8,24},{10,26},{12,28},{14,30},{16,0},... | collective-permute-start | bytes 491528 | tf_op jit(solution)/shard_map/ppermute | solution.py:316
  21.8 30.2 %copy-start.8 = (bf16[256,40]{0,1:T(8,128)(2,1)S(1)}, bf16[256,40]{0,1:T(8,128)(2,1)}, u32[]{:S(2)}) copy-start(bf16[256,40]{0,1:T(8,128)(2,1)} %param.15) | copy-start | bytes 61444
  22.5 29.5 %copy-start.7 = (bf16[256,256]{1,0:T(8,128)(2,1)S(1)}, bf16[256,256]{1,0:T(8,128)(2,1)}, u32[]{:S(2)}) copy-start(bf16[256,256]{1,0:T(8,128)(2,1)} %param.14) | copy-start | bytes 393220
  50.4 2.5 %copy-start.12 = (bf16[20,32,128]{2,1,0:T(8,128)(2,1)S(1)}, bf16[20,32,128]{2,1,0:T(8,128)(2,1)}, u32[]{:S(2)}) copy-start(bf16[20,32,128]{2,1,0:T(8,128)(2,1)} %get-tuple-element.25) | copy-start | bytes 491524
  50.4 11.7 %collective-permute-start.3 = (bf16[20,48,128]{2,1,0:T(8,128)(2,1)}, bf16[20,48,128]{2,1,0:T(8,128)(2,1)S(1)}, u32[]{:S(2)}, u32[]{:S(2)}) collective-permute-start(bf16[20,48,128]{2,1,0:T(8,128)(2,1)} %get-tuple-element.22), channel_id=1, source_target_pairs={{0,1},{1,0},{2,3},{3,2},{4,5},{5,4},{6,7},{7,6},{8,9},{9,8},{10,11... | collective-permute-start | bytes 737288 | tf_op jit(solution)/shard_map/ppermute | solution.py:360
  52.9 9.2 %collective-permute-start.4 = (bf16[20,32,128]{2,1,0:T(8,128)(2,1)S(1)}, bf16[20,32,128]{2,1,0:T(8,128)(2,1)S(1)}, u32[]{:S(2)}, u32[]{:S(2)}) collective-permute-start(bf16[20,32,128]{2,1,0:T(8,128)(2,1)S(1)} %copy-done.12), channel_id=1, source_target_pairs={{0,1},{1,0},{2,3},{3,2},{4,5},{5,4},{6,7},{7,6},{8,9},{9,8},{10,11... | collective-permute-start | bytes 491528 | tf_op jit(solution)/shard_map/ppermute | solution.py:360
  62.1 0.7 copy-start.6
  62.1 0.8 copy-start
  70.7 9.7 %collective-permute-start.6 = (bf16[20,32,128]{2,1,0:T(8,128)(2,1)}, bf16[20,32,128]{2,1,0:T(8,128)(2,1)S(1)}, u32[]{:S(2)}, u32[]{:S(2)}) collective-permute-start(bf16[20,32,128]{2,1,0:T(8,128)(2,1)} %get-tuple-element.28), channel_id=1, source_target_pairs={{0,1},{1,0},{2,3},{3,2},{4,5},{5,4},{6,7},{7,6},{8,9},{9,8},{10,11... | collective-permute-start | bytes 491528 | tf_op jit(solution)/shard_map/ppermute | solution.py:360
  79.8 5.6 %collective-permute-start.5 = (bf16[20,32,128]{2,1,0:T(8,128)(2,1)}, bf16[20,32,128]{2,1,0:T(8,128)(2,1)S(1)}, u32[]{:S(2)}, u32[]{:S(2)}) collective-permute-start(bf16[20,32,128]{2,1,0:T(8,128)(2,1)} %get-tuple-element.27), channel_id=1, source_target_pairs={{0,1},{1,0},{2,3},{3,2},{4,5},{5,4},{6,7},{7,6},{8,9},{9,8},{10,11... | collective-permute-start | bytes 491528 | tf_op jit(solution)/shard_map/ppermute | solution.py:360
  80.3 5.0 %copy-start.4 = (bf16[20,32,128]{2,1,0:T(8,128)(2,1)}, bf16[20,32,128]{2,1,0:T(8,128)(2,1)S(1)}, u32[]{:S(2)}) copy-start(bf16[20,32,128]{2,1,0:T(8,128)(2,1)S(1)} %collective-permute-done.6.b1) | copy-start | bytes 491524
  85.4 0.7 copy-start.5
where the time goes:
time: 89.1 us; the launch traced here: 88.7 us
  Pallas kernels  47.7 us (54%)
  waiting for transfers between devices  22.4 us (25%)
  starting transfers between devices  11.1 us (12%)
  local copies, waits for them, and re-layouts  6.25 us (7%)
  other arithmetic  1.07 us (1%)
    pallas_call x1, Pallas kernels, shards(): call(functools.partial(transport_kernel, cells_x=cells_x), 'transport', (...  27.2 us
    pallas_call x2, Pallas kernels, physics(): call(functools.partial(physics_kernel, chunk), f'physics{chunk}', (win1,...  15.3 us
    ppermute x4, waiting for transfers between devices, swap(): return lax.ppermute(x, 'group', [(0, 1), (1, 0)])  12.2 us
    ppermute x1, waiting for transfers between devices, across(): lax.ppermute(x, 'tile', [(i, (i + by) % tiles) for i in range(tiles)])  8.32 us
    ppermute x1, starting transfers between devices, shards(): from_east = lax.ppermute(to_west, 'tile', beside(-1))  4.54 us
    ppermute x4, starting transfers between devices, swap(): return lax.ppermute(x, 'group', [(0, 1), (1, 0)])  4.28 us
    pallas_call x1, Pallas kernels, shards(): call(finish_kernel, 'finish', sds((chans, cells_x, cells_y), F32), [VMEM_...  2.69 us
    pallas_call x1, Pallas kernels, shards(): call(edge_kernel, 'edges', (strip, strip, sds((chans, 16, cells_y), BF16)...  2.49 us
  transfers between devices with their start and end apart: 7, of which 4 were waited for; matrix products, arithmetic and copies ran while one was open for 3% of the time, Pallas kernels for 8%

commit v1 on v0

--- a/solution.py
+++ b/solution.py
@@ -10,7 +10,7 @@
 TILE_ROWS = 8
 DEEP = 3
 EXTRA = 16
-ROW_UNROLL = 2
+ROW_UNROLL = 7
 
 F32 = jnp.float32
 BF16 = jnp.bfloat16
@@ -47,83 +47,121 @@
 
 
 def transport_kernel(
-    state_ref, coef_ref, west_ref, east_ref, up_ref, upw_ref, upe_ref,
-    down_ref, downw_ref, downe_ref, *rest, cells_x,
+    state_ref, coef_ref, here_ref, up_ref, down_ref,
+    moved_ref, mine0, mine1, theirs0, theirs1, border, extra, *, cells_x,
 ):
-    moved_ref, mine0, mine1, theirs0, theirs1 = rest[:5]
-    raw, once, twice, strips, border, extra = rest[5:]
     chans = state_ref.shape[0] // cells_x
     width = state_ref.shape[1]
     half = cells_x // 2
     part = half // 2
+    message = here_ref.shape[0] // chans
     own = lax.axis_index("group")
     place = lax.axis_index("tile") % TILE_ROWS
     lane = lanes_of((chans, width))
-    is_east = lane < width // 2
-    keep = jnp.where(
-        is_east,
+    first, last = lane == 0, lane == width - 1
+    low_lanes = lane < width // 2
+    for s, ref in enumerate((here_ref, up_ref, down_ref)):
+        border[s] = ref[...].astype(F32)
+    coefs = [coef_ref[n] for n in range(5)]
+
+    def line(s, k):
+        return border[s, pl.ds(k, chans, stride=message), :]
+
+    def pair(k):
+        return line(0, k), jnp.where(low_lanes, line(2, k), line(1, k))
+
+    def roll(x, by):
+        return pltpu.roll(x, by, 1)
+
+    def both_ways(main, aux):
+        ml, al = roll(main, 1), roll(aux, 1)
+        mu, au = roll(main, width - 1), roll(aux, width - 1)
+        lower = jnp.where(first, al, ml), jnp.where(first, ml, al)
+        upper = jnp.where(last, au, mu), jnp.where(last, mu, au)
+        return lower, upper
+
+    def stencil(q, xl, xu, yl, yu):
+        c0, cxl, cxu, cyl, cyu = coefs
+        return c0 * q + cxl * xl + cxu * xu + cyl * yl + cyu * yu
+
+    def column(west, mid, east, keep):
+        lower, upper = both_ways(*mid)
+        return tuple(
+            stencil(mid[n], lower[n], upper[n], west[n], east[n]) * keep for n in range(2)
+        )
+
+    keeps = (
+        jnp.where(place == 0, 0.0, 1.0),
         jnp.where(place == TILE_ROWS - 1, 0.0, 1.0),
-        jnp.where(place == 0, 0.0, 1.0),
     )
-    for s, refs in enumerate(
-        ((west_ref, east_ref), (upw_ref, upe_ref), (downw_ref, downe_ref))
-    ):
+    edges = []
+    for side in range(2):
+        raw = [pair(16 + 8 * side + k) for k in range(5)]
+        keep = keeps[side]
+        inside = 3 if side == 0 else 1
+        once = [
+            column(raw[k - 1], raw[k], raw[k + 1], 1.0 if k == inside else keep)
+            for k in (1, 2, 3)
+        ]
+        edges.append((raw[2], once[1], column(once[0], once[1], once[2], keep)))
+
+    for q in range(2):
         for side in range(2):
-            strips[s, side] = refs[side][...].astype(F32)
-    border[0] = up_ref[...].astype(F32)
-    border[1] = down_ref[...].astype(F32)
-
-    def edge_slab(source, row):
-        slab = jnp.zeros((chans, width), F32)
-        for k in range(DEEP):
-            wk = strips[source, 0, pl.ds(k, chans, stride=8), :]
-            ek = strips[source, 1, pl.ds(k, chans, stride=8), :]
-            at = width - DEEP + k
-            slab = jnp.where(lane == at, pltpu.roll(wk, lax.rem(at - row + width, width), 1), slab)
-            slab = jnp.where(lane == k, pltpu.roll(ek, lax.rem(k - row + width, width), 1), slab)
-        return slab
-
-    def fill(i, _):
-        raw[i + DEEP, 0] = state_ref[pl.ds(i, chans, stride=cells_x), :]
-        raw[i + DEEP, 1] = edge_slab(0, i)
-        return 0
-
-    lax.fori_loop(0, cells_x, fill, 0, unroll=4)
-    for k in range(DEEP):
-        raw[k, 0] = border[0, pl.ds(16 - DEEP + k, chans, stride=16), :]
-        raw[k, 1] = edge_slab(1, jnp.int32(cells_x - DEEP + k))
-        raw[cells_x + DEEP + k, 0] = border[1, pl.ds(k, chans, stride=16), :]
-        raw[cells_x + DEEP + k, 1] = edge_slab(2, jnp.int32(k))
-
-    def sweep(src, r):
-        c0, cxl, cxu, cyl, cyu = [coef_ref[n] for n in range(5)]
-        q, e = src[r, 0], src[r, 1]
-        ql, el = pltpu.roll(q, 1, 1), pltpu.roll(e, 1, 1)
-        qu, eu = pltpu.roll(q, width - 1, 1), pltpu.roll(e, width - 1, 1)
-        first, last = lane == 0, lane == width - 1
-        ql, el = jnp.where(first, el, ql), jnp.where(first, ql, el)
-        qu, eu = jnp.where(last, eu, qu), jnp.where(last, qu, eu)
-        q2 = c0 * q + cxl * src[r - 1, 0] + cxu * src[r + 1, 0] + cyl * ql + cyu * qu
-        e2 = c0 * e + cxl * src[r - 1, 1] + cxu * src[r + 1, 1] + cyl * el + cyu * eu
-        return q2, e2 * keep
-
-    def first_sweep(r, _):
-        q2, e2 = sweep(raw, r)
-        once[r, 0] = q2
-        once[r, 1] = e2
-        return 0
-
-    lax.fori_loop(1, cells_x + 2 * DEEP - 1, first_sweep, 0, unroll=ROW_UNROLL)
-
-    def second_sweep(i, _):
-        q2, e2 = sweep(once, i + DEEP)
-        moved_ref[pl.ds(i, chans, stride=cells_x), :] = q2
-        twice[i + 1] = e2
-        return 0
-
-    lax.fori_loop(0, cells_x, second_sweep, 0, unroll=ROW_UNROLL)
-    above, twice[0] = sweep(once, DEEP - 1)
-    below, twice[cells_x + 1] = sweep(once, cells_x + DEEP)
+            main, aux = edges[side][2]
+            if q == 0:
+                lineup = jnp.where(first, roll(aux, 1), roll(main, 1))
+            else:
+                by = width - half + 1
+                lineup = jnp.where(lane <= half, roll(main, by), roll(aux, by))
+            extra[q, pl.ds(2 + side, chans, stride=EXTRA), :] = lineup
+
+    def sweep(level, i, q, xl, xu, aux=False):
+        west, east = edges[0][level][int(aux)], edges[1][level][int(aux)]
+        if isinstance(i, int):
+            to_first, to_last = -i % width, (width - 1 - i) % width
+        else:
+            to_first, to_last = lax.rem(width - i, width), width - 1 - i
+        yl = jnp.where(first, roll(west, to_first), roll(q, 1))
+        yu = jnp.where(last, roll(east, to_last), roll(q, width - 1))
+        return stencil(q, xl, xu, yl, yu)
+
+    def raw(i):
+        if isinstance(i, int) and i < 0:
+            return line(1, 16 + i)
+        if isinstance(i, int) and i >= cells_x:
+            return line(2, i - cells_x)
+        return state_ref[pl.ds(i, chans, stride=cells_x), :]
+
+    def outside(i):
+        return isinstance(i, int) and not 0 <= i < cells_x
+
+    def step(i, carry):
+        r0, r1, o0, o1 = carry
+        r2 = raw(i + 2)
+        o2 = sweep(0, i + 1, r1, r0, r2, outside(i + 1))
+        moved = sweep(1, i, o1, o0, o2, outside(i))
+        return moved, (r1, r2, o1, o2)
+
+    def put(i, moved):
+        moved_ref[pl.ds(i, chans, stride=cells_x), :] = moved
+
+    ra, rb, rc, rd = raw(-3), raw(-2), raw(-1), raw(0)
+    carry = (rc, rd, sweep(0, -2, rb, ra, rc, True), sweep(0, -1, rc, rb, rd, True))
+    above, carry = step(-1, carry)
+
+    def rows(n, carry):
+        for u in range(ROW_UNROLL):
+            i = n * ROW_UNROLL + u
+            moved, carry = step(i, carry)
+            put(i, moved)
+        return carry
+
+    steps = (cells_x - 2) // ROW_UNROLL
+    carry = lax.fori_loop(0, steps, rows, carry)
+    for i in range(steps * ROW_UNROLL, cells_x):
+        moved, carry = step(i, carry)
+        put(i, moved)
+    below, _ = step(cells_x, carry)
 
     def row(i):
         if i < 0:
@@ -132,21 +170,13 @@
             return below
         return moved_ref[pl.ds(i, chans, stride=cells_x), :]
 
+    zero = jnp.zeros((chans, width), F32)
     for q in range(2):
         base = q * half
-
-        def gather(l, carry):
-            aw, ae = carry
-            e2 = twice[base + l]
-            aw = jnp.where(lane == l, pltpu.roll(e2, lax.rem(l + 1, width), 1), aw)
-            ae = jnp.where(lane == l, pltpu.roll(e2, l, 1), ae)
-            return aw, ae
-
-        zero = jnp.zeros((chans, width), F32)
-        aw, ae = lax.fori_loop(0, half + 2, gather, (zero, zero), unroll=2)
-        items = (row(base - 1), row(base + half), aw, ae, row(base + part))
+        items = {0: row(base - 1), 1: row(base + half), 4: row(base + part)}
         for k in range(EXTRA):
-            extra[q, pl.ds(k, chans, stride=EXTRA), :] = items[k] if k < len(items) else zero
+            if k not in (2, 3):
+                extra[q, pl.ds(k, chans, stride=EXTRA), :] = items.get(k, zero)
 
     for c in range(chans):
         for dst0, dst1, q in ((mine0, mine1, own), (theirs0, theirs1, 1 - own)):
@@ -158,7 +188,7 @@
 
 def physics_kernel(chunk, table_ref, w1_ref, w2_ref, w3_ref, *rest):
     count = 2 if chunk == 0 else 4
-    ins, rest = rest[:count], rest[count:]
+    ins, rest = rest[:count], rest[count + (chunk > 0) :]
     own_out, other_out, wide0, wide1, slab, packed, mask, table, stacked, terms, sem = rest
     chans, part, width = own_out.shape
     half = 2 * part
@@ -310,7 +340,11 @@
 
     from_west = lax.ppermute(to_east, "tile", beside(1))
     from_east = lax.ppermute(to_west, "tile", beside(-1))
-    message = jnp.concatenate([rows, from_west, from_east], axis=1)
+    spare = jnp.zeros((chans, 3, cells_y), BF16)
+    message = jnp.concatenate(
+        [rows, from_west[:, :3], to_west[:, :2], spare, to_east[:, 1:3], from_east[:, :3], spare],
+        axis=1,
+    )
 
     def across(x, by):
         return lax.ppermute(x, "tile", [(i, (i + by) % tiles) for i in range(tiles)])
@@ -335,26 +369,18 @@
     def flat(x):
         return x.reshape(-1, cells_y)
 
-    def split(x):
-        return flat(x[:, 0:16]), flat(x[:, 16:24]), flat(x[:, 24:32])
-
     win0 = sds((chans, EXTRA + part, cells_y), BF16)
     win1 = sds((chans, part, cells_y), BF16)
-    slabs = pltpu.VMEM((cells_x + 2 * DEEP, 2, chans, cells_y), F32)
     moved, mine0, mine1, theirs0, theirs1 = call(
         functools.partial(transport_kernel, cells_x=cells_x),
         "transport",
         (sds((chans * cells_x, cells_y), F32), win0, win1, win0, win1),
-        [VMEM_SPEC] * 10,
+        [VMEM_SPEC] * 5,
         [
-            slabs,
-            slabs,
-            pltpu.VMEM((cells_x + 2, chans, cells_y), F32),
-            pltpu.VMEM((3, 2, chans * 8, cells_y), F32),
-            pltpu.VMEM((2, chans * 16, cells_y), F32),
+            pltpu.VMEM((3, chans * message.shape[1], cells_y), F32),
             pltpu.VMEM((2, chans * EXTRA, cells_y), F32),
         ],
-    )(block.reshape(chans * cells_x, cells_y), coef, flat(from_west), flat(from_east), *split(up), *split(down))
+    )(flat(block), coef, flat(message), flat(up), flat(down))
 
     def swap(x):
         return lax.ppermute(x, "group", [(0, 1), (1, 0)])
@@ -379,7 +405,7 @@
             functools.partial(physics_kernel, chunk),
             f"physics{chunk}",
             (win1, win1),
-            [ANY_SPEC] + [VMEM_SPEC] * (3 + len(windows)),
+            [ANY_SPEC] + [VMEM_SPEC] * (3 + 2 + 2 * chunk) + [ANY_SPEC] * chunk,
             [
                 pltpu.VMEM((2, chans * (EXTRA + part), cells_y), F32),
                 pltpu.VMEM((2, chans * part, cells_y), F32),
@@ -395,7 +421,7 @@
 
     own0, other0 = physics(0, mine0, got0)
     back0 = swap(other0)
-    own1, other1 = physics(1, mine0, got0, mine1, got1)
+    own1, other1 = physics(1, mine0, got0, mine1, got1, own0)
     back1 = swap(other1)
     updated = call(
         finish_kernel, "finish", sds((chans, cells_x, cells_y), F32), [VMEM_SPEC] * 5

time: 89.1 us -> 69.5 us (0.78)
  Pallas kernels: 47.7 us -> 30.1 us
  waiting for transfers between devices: 22.4 us -> 19.3 us
  local copies, waits for them, and re-layouts: 6.25 us -> 8.26 us
  other arithmetic: 1.07 us -> 0.15 us
    pallas_call x1, Pallas kernels: 27.2 us -> 9.58 us  [shards(): call(functools.partial(transport_kernel, cells_x=cells_x), 'transport', (...]
    ppermute x1, waiting for transfers between devices: 1.89 us -> 0.26 us  [shards(): from_east = lax.ppermute(to_west, 'tile', beside(-1))]
    ppermute x4, waiting for transfers between devices: 12.2 us -> 10.6 us  [swap(): return lax.ppermute(x, 'group', [(0, 1), (1, 0)])]
    concatenate x0 -> x1, local copies, waits for them, and re-layouts: none -> 1.05 us  [shards(): jnp.concatenate([rows, from_west[:, :3], to_west[:, :2], spare, to_east[:...]
    slice x1 -> x4, local copies, waits for them, and re-layouts: 0.63 us -> 1.63 us  [the longest x1 0.82 us: shards(): to_west[:, :2]]
    concatenate x1 -> x0, other arithmetic: 0.92 us -> none  [shards(): message = jnp.concatenate([rows, from_west, from_east], axis=1)]
  transfers between devices with their start and end apart: 7 -> 7, of which waited for: 4 -> 5; matrix products, arithmetic and copies ran while one was open for 3% -> 7% of each run, Pallas kernels for 8% -> 11%
where the time goes in v1:
time: 69.5 us; the launch traced here: 69 us
  Pallas kernels  30.1 us (43%)
  waiting for transfers between devices  19.3 us (28%)
  starting transfers between devices  11 us (16%)
  local copies, waits for them, and re-layouts  8.26 us (12%)
    pallas_call x2, Pallas kernels, physics(): call(functools.partial(physics_kernel, chunk), f'physics{chunk}', (win1,...  15.3 us
    ppermute x4, waiting for transfers between devices, swap(): return lax.ppermute(x, 'group', [(0, 1), (1, 0)])  10.6 us
    pallas_call x1, Pallas kernels, shards(): call(functools.partial(transport_kernel, cells_x=cells_x), 'transport', (...  9.58 us
    ppermute x1, waiting for transfers between devices, across(): lax.ppermute(x, 'tile', [(i, (i + by) % tiles) for i in range(tiles)])  8.4 us
    ppermute x1, starting transfers between devices, shards(): from_east = lax.ppermute(to_west, 'tile', beside(-1))  4.54 us
    ppermute x4, starting transfers between devices, swap(): return lax.ppermute(x, 'group', [(0, 1), (1, 0)])  4.18 us
    unnamed x28, local copies, waits for them, and re-layouts  2.86 us
    pallas_call x1, Pallas kernels, shards(): call(finish_kernel, 'finish', sds((chans, cells_x, cells_y), F32), [VMEM_...  2.69 us
  transfers between devices with their start and end apart: 7, of which 5 were waited for; matrix products, arithmetic and copies ran while one was open for 7% of the time, Pallas kernels for 11%

profile of v1, /device:TPU:24, one launch (start us, length us, event | category | flops | bytes accessed | tf_op | source)
XLA Modules:
  0.0 69.0 jit_solution(12041846741881039942)
XLA Ops:
  0.0 0.0 copy-start.10
  0.0 0.0 copy-start.11
  0.0 0.0 copy-start.9
  0.0 0.0 copy-start.8
  0.0 2.5 %edges.1 = (bf16[20,8,128]{2,1,0:T(8,128)(2,1)}, bf16[20,8,128]{2,1,0:T(8,128)(2,1)}, bf16[20,16,128]{2,1,0:T(8,128)(2,1)}) custom-call(f32[20,128,128]{2,1,0:T(8,128)} %bitcast.14), custom_call_target="tpu_custom_call" | custom-call | tf_op jit(solution)/shard_map/edges/pallas_call | solution.py:334
  2.5 1.9 %collective-permute-start = (bf16[20,8,128]{2,1,0:T(8,128)(2,1)}, bf16[20,8,128]{2,1,0:T(8,128)(2,1)S(1)}, u32[]{:S(2)}, u32[]{:S(2)}) collective-permute-start(bf16[20,8,128]{2,1,0:T(8,128)(2,1)} %get-tuple-element.18), channel_id=1, source_target_pairs={{0,2},{2,4},{4,6},{6,8},{8,10},{10,12},{12,14},{16,18},{18,20},{20... | collective-permute-start | bytes 122888 | tf_op jit(solution)/shard_map/ppermute | solution.py:341
  4.4 4.5 %collective-permute-start.1 = (bf16[20,8,128]{2,1,0:T(8,128)(2,1)}, bf16[20,8,128]{2,1,0:T(8,128)(2,1)S(1)}, u32[]{:S(2)}, u32[]{:S(2)}) collective-permute-start(bf16[20,8,128]{2,1,0:T(8,128)(2,1)} %get-tuple-element.19), channel_id=1, source_target_pairs={{2,0},{4,2},{6,4},{8,6},{10,8},{12,10},{14,12},{18,16},{20,18},{22... | collective-permute-start | bytes 122888 | tf_op jit(solution)/shard_map/ppermute | solution.py:342
  9.0 0.0 copy-done.10
  9.0 0.0 copy-done.11
  9.0 0.0 copy-done.9
  9.0 0.8 %slice.14 = bf16[20,2,128]{2,1,0:T(2,128)(2,1)S(1)} slice(bf16[20,8,128]{2,1,0:T(8,128)(2,1)} %get-tuple-element.18), slice={[0:20], [1:3], [0:128]} | slice | bytes 20480 | tf_op jit(solution)/shard_map/slice | solution.py:345
  9.8 0.0 copy-start.7
  9.8 0.8 %slice.13 = bf16[20,2,128]{2,1,0:T(2,128)(2,1)S(1)} slice(bf16[20,8,128]{2,1,0:T(8,128)(2,1)} %get-tuple-element.19), slice={[0:20], [0:2], [0:128]} | slice | bytes 20480 | tf_op jit(solution)/shard_map/slice | solution.py:345
  10.7 0.0 collective-permute-done
  10.7 0.3 collective-permute-done.1
  11.0 0.0 copy-start.3
  11.0 1.1 %concatenate.3 = bf16[20,32,128]{2,1,0:T(8,128)(2,1)S(1)} concatenate(bf16[20,16,128]{2,1,0:T(8,128)(2,1)} %get-tuple-element.17, bf16[20,3,128]{2,1,0:T(4,128)(2,1)S(1)} %slice.16, bf16[20,2,128]{2,1,0:T(2,128)(2,1)S(1)} %slice.13, bf16[20,3,128]{2,1,0:T(4,128)(2,1)S(1)} %broadcast_in_dim.27, bf16[20,2,128]{2,1,0:T(2,128)(2,1)S(1)} %slice.14, bf16[20,3,128]{2,1,0:T(4,128)(2,1)S(1)} %slice.17, ...), dimensions={1} | concatenate | bytes 327680 | tf_op jit(solution)/shard_map/concatenate | solution.py:344
  12.0 0.0 copy-start.2
  12.0 0.4 collective-permute-start.2
  12.4 0.1 broadcast_subtract_fusion
  12.5 0.1 sub.70
  12.6 0.1 sub.68
  12.7 0.1 add.33
  12.8 0.1 add.31
  12.8 0.1 sub.66
  12.9 0.0 copy-done.8
  13.0 8.4 %collective-permute-done.2 = bf16[20,32,128]{2,1,0:T(8,128)(2,1)S(1)} collective-permute-done((bf16[20,32,128]{2,1,0:T(8,128)(2,1)S(1)}, bf16[20,32,128]{2,1,0:T(8,128)(2,1)S(1)}, u32[]{:S(2)}, u32[]{:S(2)}) %collective-permute-start.2) | collective-permute-done | bytes 163872 | tf_op jit(solution)/shard_map/ppermute | solution.py:350
  21.4 0.0 copy-start.1
  21.4 0.7 %broadcast_in_dim.26.coef_ref = f32[5,20,128]{2,1,0:T(8,128)} broadcast(f32[5,20]{1,0:T(8,128)S(1)} %stack.2), dimensions={0,1} | broadcast | bytes 51600 | tf_op jit(solution)/shard_map/broadcast_in_dim | solution.py:367
  22.1 0.0 copy-done.2
  22.1 0.0 copy-done.1
  22.1 9.6 %transport.1 = (f32[2560,128]{1,0:T(8,128)}, bf16[20,48,128]{2,1,0:T(8,128)(2,1)}, bf16[20,32,128]{2,1,0:T(8,128)(2,1)}, bf16[20,48,128]{2,1,0:T(8,128)(2,1)}, bf16[20,32,128]{2,1,0:T(8,128)(2,1)}) custom-call(f32[2560,128]{1,0:T(8,128)} %bitcast.15, f32[5,20,128]{2,1,0:T(8,128)} %broadcast_in_dim.26.coef_ref, bf16[640,128]{1,0:T(8,128)(2,1)} %bitcast.22, ...), custom_call_target="tpu_custom_call" | custom-call | tf_op jit(solution)/shard_map/transport/pallas_call | solution.py:374
  31.7 1.5 %collective-permute-start.3 = (bf16[20,48,128]{2,1,0:T(8,128)(2,1)}, bf16[20,48,128]{2,1,0:T(8,128)(2,1)S(1)}, u32[]{:S(2)}, u32[]{:S(2)}) collective-permute-start(bf16[20,48,128]{2,1,0:T(8,128)(2,1)} %get-tuple-element.22), channel_id=1, source_target_pairs={{0,1},{1,0},{2,3},{3,2},{4,5},{5,4},{6,7},{7,6},{8,9},{9,8},{10,11... | collective-permute-start | bytes 737288 | tf_op jit(solution)/shard_map/ppermute | solution.py:386
  33.2 0.6 pad.9
  33.8 0.0 copy-done.7
  33.8 0.7 %copy.14 = bf16[256,256]{0,1:T(8,128)(2,1)} copy(bf16[256,256]{1,0:T(8,128)(2,1)S(1)} %copy-done.7) | data formatting | bytes 262144 | tf_op args[6]
  34.6 0.0 copy-done.3
  34.6 0.1 reshape.175
  34.6 0.6 collective-permute-start.4
  35.2 0.1 fusion
  35.3 0.1 copy.18
  35.4 0.8 %copy.15.w1_ref = bf16[256,432]{1,0:T(8,128)(2,1)} copy(bf16[256,432]{0,1:T(8,128)(2,1)S(1)} %bitcast.19) | data formatting | bytes 442368 | tf_op jit(solution)/shard_map/reshape | solution.py:398
  36.2 4.5 %collective-permute-done.3.rest_1_ = bf16[20,48,128]{2,1,0:T(8,128)(2,1)S(1)} collective-permute-done((bf16[20,48,128]{2,1,0:T(8,128)(2,1)}, bf16[20,48,128]{2,1,0:T(8,128)(2,1)S(1)}, u32[]{:S(2)}, u32[]{:S(2)}) %collective-permute-start.3) | collective-permute-done | bytes 245792 | tf_op jit(solution)/shard_map/ppermute | solution.py:386
  40.7 0.0 copy-start
  40.7 0.7 %copy-done = bf16[20,48,128]{2,1,0:T(8,128)(2,1)} copy-done((bf16[20,48,128]{2,1,0:T(8,128)(2,1)}, bf16[20,48,128]{2,1,0:T(8,128)(2,1)S(1)}, u32[]{:S(2)}) %copy-start) | copy-done | bytes 245784
  41.4 7.5 %physics0.1 = (bf16[20,32,128]{2,1,0:T(8,128)(2,1)}, bf16[20,32,128]{2,1,0:T(8,128)(2,1)}) custom-call(s32[9,1,128,128]{3,2,1,0:T(8,128)} %table_ref.3, bf16[256,432]{1,0:T(8,128)(2,1)} %copy.15.w1_ref, bf16[256,256]{1,0:T(8,128)(2,1)} %bitcast.17, bf16[48,256]{1,0:T(8,128)(2,1)} %bitcast.23, bf16[20,48,128]{2,1,0:T(8,128)(2,1)} %get-tuple-element.21.rest_0_, ...), custom_call_target="tpu_custom_call" | custom-call | tf_op jit(solution)/shard_map/physics0/pallas_call | solution.py:404
  48.9 0.0 copy-start.12
  48.9 0.0 collective-permute-done.4.rest_3_
  48.9 0.0 copy-start.6
  48.9 0.7 copy-done.6
  49.6 7.8 %physics1.1 = (bf16[20,32,128]{2,1,0:T(8,128)(2,1)}, bf16[20,32,128]{2,1,0:T(8,128)(2,1)}) custom-call(s32[9,1,128,128]{3,2,1,0:T(8,128)} %table_ref.3, bf16[256,432]{1,0:T(8,128)(2,1)} %copy.15.w1_ref, bf16[256,256]{1,0:T(8,128)(2,1)} %bitcast.18, bf16[48,256]{1,0:T(8,128)(2,1)} %bitcast.24, bf16[20,48,128]{2,1,0:T(8,128)(2,1)} %get-tuple-element.21.rest_0_, ...), custom_call_target="tpu_custom_call" | custom-call | tf_op jit(solution)/shard_map/physics1/pallas_call | solution.py:404
  57.4 1.6 %collective-permute-start.6 = (bf16[20,32,128]{2,1,0:T(8,128)(2,1)}, bf16[20,32,128]{2,1,0:T(8,128)(2,1)S(1)}, u32[]{:S(2)}, u32[]{:S(2)}) collective-permute-start(bf16[20,32,128]{2,1,0:T(8,128)(2,1)} %get-tuple-element.28), channel_id=1, source_target_pairs={{0,1},{1,0},{2,3},{3,2},{4,5},{5,4},{6,7},{7,6},{8,9},{9,8},{10,11... | collective-permute-start | bytes 491528 | tf_op jit(solution)/shard_map/ppermute | solution.py:386
  59.0 0.0 copy-done.12
  59.0 0.5 collective-permute-start.5
  59.5 4.4 %collective-permute-done.6.b1 = bf16[20,32,128]{2,1,0:T(8,128)(2,1)S(1)} collective-permute-done((bf16[20,32,128]{2,1,0:T(8,128)(2,1)}, bf16[20,32,128]{2,1,0:T(8,128)(2,1)S(1)}, u32[]{:S(2)}, u32[]{:S(2)}) %collective-permute-start.6) | collective-permute-done | bytes 163872 | tf_op jit(solution)/shard_map/ppermute | solution.py:386
  63.9 0.0 copy-start.4
  63.9 1.8 %collective-permute-done.5.b0 = bf16[20,32,128]{2,1,0:T(8,128)(2,1)S(1)} collective-permute-done((bf16[20,32,128]{2,1,0:T(8,128)(2,1)S(1)}, bf16[20,32,128]{2,1,0:T(8,128)(2,1)S(1)}, u32[]{:S(2)}, u32[]{:S(2)}) %collective-permute-start.5) | collective-permute-done | bytes 163872 | tf_op jit(solution)/shard_map/ppermute | solution.py:386
  65.6 0.0 copy-start.5
  65.6 0.0 copy-done.4
  65.7 0.7 copy-done.5
  66.3 2.7 %finish.1 = f32[20,128,128]{2,1,0:T(8,128)} custom-call(f32[20,128,128]{2,1,0:T(8,128)} %bitcast.16, bf16[20,32,128]{2,1,0:T(8,128)(2,1)} %get-tuple-element.23.rest_4_.a0, bf16[20,32,128]{2,1,0:T(8,128)(2,1)} %get-tuple-element.26.a1, bf16[20,32,128]{2,1,0:T(8,128)(2,1)} %copy-done.5, bf16[20,32,128]{2,1,0:T(8,128)(2,1)} %copy-done.4), custom_call_target="tpu_custom_call" | custom-call | tf_op jit(solution)/shard_map/finish/pallas_call | solution.py:426
  (9 shorter events, 0.1 us)
Async XLA Ops:
  0.0 9.0 %copy-start.10 = (f32[4]{0:T(128)S(1)}, f32[4]{0:T(128)}, u32[]{:S(2)}) copy-start(f32[4]{0:T(128)} %param.10) | copy-start | bytes 52
  0.0 9.0 %copy-start.11 = (f32[4]{0:T(128)S(1)}, f32[4]{0:T(128)}, u32[]{:S(2)}) copy-start(f32[4]{0:T(128)} %param.9) | copy-start | bytes 52
  0.0 9.0 %copy-start.9 = (f32[5]{0:T(128)S(1)}, f32[5]{0:T(128)}, u32[]{:S(2)}) copy-start(f32[5]{0:T(128)} %param.11) | copy-start | bytes 64
  0.0 12.9 %copy-start.8 = (bf16[256,40]{0,1:T(8,128)(2,1)S(1)}, bf16[256,40]{0,1:T(8,128)(2,1)}, u32[]{:S(2)}) copy-start(bf16[256,40]{0,1:T(8,128)(2,1)} %param.15) | copy-start | bytes 61444
  2.5 8.2 %collective-permute-start = (bf16[20,8,128]{2,1,0:T(8,128)(2,1)}, bf16[20,8,128]{2,1,0:T(8,128)(2,1)S(1)}, u32[]{:S(2)}, u32[]{:S(2)}) collective-permute-start(bf16[20,8,128]{2,1,0:T(8,128)(2,1)} %get-tuple-element.18), channel_id=1, source_target_pairs={{0,2},{2,4},{4,6},{6,8},{8,10},{10,12},{12,14},{16,18},{18,20},{20... | collective-permute-start | bytes 122888 | tf_op jit(solution)/shard_map/ppermute | solution.py:341
  4.4 6.5 %collective-permute-start.1 = (bf16[20,8,128]{2,1,0:T(8,128)(2,1)}, bf16[20,8,128]{2,1,0:T(8,128)(2,1)S(1)}, u32[]{:S(2)}, u32[]{:S(2)}) collective-permute-start(bf16[20,8,128]{2,1,0:T(8,128)(2,1)} %get-tuple-element.19), channel_id=1, source_target_pairs={{2,0},{4,2},{6,4},{8,6},{10,8},{12,10},{14,12},{18,16},{20,18},{22... | collective-permute-start | bytes 122888 | tf_op jit(solution)/shard_map/ppermute | solution.py:342
  9.8 24.0 %copy-start.7 = (bf16[256,256]{1,0:T(8,128)(2,1)S(1)}, bf16[256,256]{1,0:T(8,128)(2,1)}, u32[]{:S(2)}) copy-start(bf16[256,256]{1,0:T(8,128)(2,1)} %param.14) | copy-start | bytes 393220
  11.0 23.6 %copy-start.3 = (bf16[360,256]{1,0:T(8,128)(2,1)S(1)}, bf16[360,256]{1,0:T(8,128)(2,1)}, u32[]{:S(2)}) copy-start(bf16[360,256]{1,0:T(8,128)(2,1)} %param.13) | copy-start | bytes 552964
  12.0 10.1 %copy-start.2 = (bf16[20,32,128]{2,1,0:T(8,128)(2,1)}, bf16[20,32,128]{2,1,0:T(8,128)(2,1)S(1)}, u32[]{:S(2)}) copy-start(bf16[20,32,128]{2,1,0:T(8,128)(2,1)S(1)} %concatenate.3) | copy-start | bytes 491524
  12.0 9.3 %collective-permute-start.2 = (bf16[20,32,128]{2,1,0:T(8,128)(2,1)S(1)}, bf16[20,32,128]{2,1,0:T(8,128)(2,1)S(1)}, u32[]{:S(2)}, u32[]{:S(2)}) collective-permute-start(bf16[20,32,128]{2,1,0:T(8,128)(2,1)S(1)} %concatenate.3), channel_id=1, source_target_pairs={{0,16},{2,18},{4,20},{6,22},{8,24},{10,26},{12,28},{14,30},{16,0},... | collective-permute-start | bytes 491528 | tf_op jit(solution)/shard_map/ppermute | solution.py:350
  21.4 0.7 %copy-start.1 = (bf16[20,32,128]{2,1,0:T(8,128)(2,1)}, bf16[20,32,128]{2,1,0:T(8,128)(2,1)S(1)}, u32[]{:S(2)}) copy-start(bf16[20,32,128]{2,1,0:T(8,128)(2,1)S(1)} %collective-permute-done.2) | copy-start | bytes 491524
  31.7 9.0 %collective-permute-start.3 = (bf16[20,48,128]{2,1,0:T(8,128)(2,1)}, bf16[20,48,128]{2,1,0:T(8,128)(2,1)S(1)}, u32[]{:S(2)}, u32[]{:S(2)}) collective-permute-start(bf16[20,48,128]{2,1,0:T(8,128)(2,1)} %get-tuple-element.22), channel_id=1, source_target_pairs={{0,1},{1,0},{2,3},{3,2},{4,5},{5,4},{6,7},{7,6},{8,9},{9,8},{10,11... | collective-permute-start | bytes 737288 | tf_op jit(solution)/shard_map/ppermute | solution.py:386
  34.6 14.3 %collective-permute-start.4 = (bf16[20,32,128]{2,1,0:T(8,128)(2,1)}, bf16[20,32,128]{2,1,0:T(8,128)(2,1)S(1)}, u32[]{:S(2)}, u32[]{:S(2)}) collective-permute-start(bf16[20,32,128]{2,1,0:T(8,128)(2,1)} %get-tuple-element.25), channel_id=1, source_target_pairs={{0,1},{1,0},{2,3},{3,2},{4,5},{5,4},{6,7},{7,6},{8,9},{9,8},{10,11... | collective-permute-start | bytes 491528 | tf_op jit(solution)/shard_map/ppermute | solution.py:386
  40.7 0.7 %copy-start = (bf16[20,48,128]{2,1,0:T(8,128)(2,1)}, bf16[20,48,128]{2,1,0:T(8,128)(2,1)S(1)}, u32[]{:S(2)}) copy-start(bf16[20,48,128]{2,1,0:T(8,128)(2,1)S(1)} %collective-permute-done.3.rest_1_) | copy-start | bytes 737284
  48.9 10.1 %copy-start.12 = (bf16[20,32,128]{2,1,0:T(8,128)(2,1)S(1)}, bf16[20,32,128]{2,1,0:T(8,128)(2,1)}, u32[]{:S(2)}) copy-start(bf16[20,32,128]{2,1,0:T(8,128)(2,1)} %get-tuple-element.27) | copy-start | bytes 491524
  48.9 0.7 copy-start.6
  57.4 6.5 %collective-permute-start.6 = (bf16[20,32,128]{2,1,0:T(8,128)(2,1)}, bf16[20,32,128]{2,1,0:T(8,128)(2,1)S(1)}, u32[]{:S(2)}, u32[]{:S(2)}) collective-permute-start(bf16[20,32,128]{2,1,0:T(8,128)(2,1)} %get-tuple-element.28), channel_id=1, source_target_pairs={{0,1},{1,0},{2,3},{3,2},{4,5},{5,4},{6,7},{7,6},{8,9},{9,8},{10,11... | collective-permute-start | bytes 491528 | tf_op jit(solution)/shard_map/ppermute | solution.py:386
  59.0 6.6 %collective-permute-start.5 = (bf16[20,32,128]{2,1,0:T(8,128)(2,1)S(1)}, bf16[20,32,128]{2,1,0:T(8,128)(2,1)S(1)}, u32[]{:S(2)}, u32[]{:S(2)}) collective-permute-start(bf16[20,32,128]{2,1,0:T(8,128)(2,1)S(1)} %copy-done.12), channel_id=1, source_target_pairs={{0,1},{1,0},{2,3},{3,2},{4,5},{5,4},{6,7},{7,6},{8,9},{9,8},{10,11... | collective-permute-start | bytes 491528 | tf_op jit(solution)/shard_map/ppermute | solution.py:386
  63.9 1.8 %copy-start.4 = (bf16[20,32,128]{2,1,0:T(8,128)(2,1)}, bf16[20,32,128]{2,1,0:T(8,128)(2,1)S(1)}, u32[]{:S(2)}) copy-start(bf16[20,32,128]{2,1,0:T(8,128)(2,1)S(1)} %collective-permute-done.6.b1) | copy-start | bytes 491524
  65.6 0.7 copy-start.5

commit v2 on v1

--- a/solution.py
+++ b/solution.py
@@ -10,7 +10,8 @@
 TILE_ROWS = 8
 DEEP = 3
 EXTRA = 16
-ROW_UNROLL = 7
+MARGIN = 16
+GROUP = 4
 
 F32 = jnp.float32
 BF16 = jnp.bfloat16
@@ -46,23 +47,37 @@
         ).astype(BF16)
 
 
+def shift_matrix(width):
+    k = lax.broadcasted_iota(jnp.int32, (4 * width, 2 * width), 0)
+    n = lax.broadcasted_iota(jnp.int32, (4 * width, 2 * width), 1)
+    m = k % width
+    lower = (n < width) & (n == m + 1)
+    upper = (n >= width) & (n - width == m - 1)
+    west = (k >= 2 * width) & (k < 3 * width) & (n == 0)
+    east = (k >= 3 * width) & (n == 2 * width - 1)
+    return jnp.where(((k < 2 * width) & (lower | upper)) | west | east, 1.0, 0.0).astype(BF16)
+
+
 def transport_kernel(
-    state_ref, coef_ref, here_ref, up_ref, down_ref,
-    moved_ref, mine0, mine1, theirs0, theirs1, border, extra, *, cells_x,
+    state_ref, speed_ref, coef_ref, here_ref, up_ref, down_ref,
+    moved_ref, mine0, mine1, theirs0, theirs1,
+    border, extra, raw_s, once_s, last_s, line_s, matrix, sem, *, chans,
 ):
-    chans = state_ref.shape[0] // cells_x
-    width = state_ref.shape[1]
+    cells_x, width = state_ref.shape[1:]
     half = cells_x // 2
     part = half // 2
     message = here_ref.shape[0] // chans
     own = lax.axis_index("group")
     place = lax.axis_index("tile") % TILE_ROWS
+    fetch = pltpu.make_async_copy(state_ref, raw_s.at[:, pl.ds(MARGIN, cells_x)], sem.at[0])
+    fetch.start()
     lane = lanes_of((chans, width))
     first, last = lane == 0, lane == width - 1
     low_lanes = lane < width // 2
     for s, ref in enumerate((here_ref, up_ref, down_ref)):
         border[s] = ref[...].astype(F32)
     coefs = [coef_ref[n] for n in range(5)]
+    matrix[...] = shift_matrix(width)
 
     def line(s, k):
         return border[s, pl.ds(k, chans, stride=message), :]
@@ -80,21 +95,18 @@
         upper = jnp.where(last, au, mu), jnp.where(last, mu, au)
         return lower, upper
 
-    def stencil(q, xl, xu, yl, yu):
+    def column(west, mid, east, keep):
         c0, cxl, cxu, cyl, cyu = coefs
-        return c0 * q + cxl * xl + cxu * xu + cyl * yl + cyu * yu
-
-    def column(west, mid, east, keep):
         lower, upper = both_ways(*mid)
         return tuple(
-            stencil(mid[n], lower[n], upper[n], west[n], east[n]) * keep for n in range(2)
+            (c0 * mid[n] + cxl * lower[n] + cxu * upper[n] + cyl * west[n] + cyu * east[n]) * keep
+            for n in range(2)
         )
 
     keeps = (
         jnp.where(place == 0, 0.0, 1.0),
         jnp.where(place == TILE_ROWS - 1, 0.0, 1.0),
     )
-    edges = []
     for side in range(2):
         raw = [pair(16 + 8 * side + k) for k in range(5)]
         keep = keeps[side]
@@ -103,11 +115,11 @@
             column(raw[k - 1], raw[k], raw[k + 1], 1.0 if k == inside else keep)
             for k in (1, 2, 3)
         ]
-        edges.append((raw[2], once[1], column(once[0], once[1], once[2], keep)))
-
-    for q in range(2):
-        for side in range(2):
-            main, aux = edges[side][2]
+        main, aux = column(once[0], once[1], once[2], keep)
+        for level, edge in enumerate((raw[2], once[1])):
+            for n in range(2):
+                line_s[level, side, n] = edge[n]
+        for q in range(2):
             if q == 0:
                 lineup = jnp.where(first, roll(aux, 1), roll(main, 1))
             else:
@@ -115,75 +127,74 @@
                 lineup = jnp.where(lane <= half, roll(main, by), roll(aux, by))
             extra[q, pl.ds(2 + side, chans, stride=EXTRA), :] = lineup
 
-    def sweep(level, i, q, xl, xu, aux=False):
-        west, east = edges[0][level][int(aux)], edges[1][level][int(aux)]
-        if isinstance(i, int):
-            to_first, to_last = -i % width, (width - 1 - i) % width
-        else:
-            to_first, to_last = lax.rem(width - i, width), width - 1 - i
-        yl = jnp.where(first, roll(west, to_first), roll(q, 1))
-        yu = jnp.where(last, roll(east, to_last), roll(q, width - 1))
-        return stencil(q, xl, xu, yl, yu)
-
-    def raw(i):
-        if isinstance(i, int) and i < 0:
-            return line(1, 16 + i)
-        if isinstance(i, int) and i >= cells_x:
-            return line(2, i - cells_x)
-        return state_ref[pl.ds(i, chans, stride=cells_x), :]
-
-    def outside(i):
-        return isinstance(i, int) and not 0 <= i < cells_x
-
-    def step(i, carry):
-        r0, r1, o0, o1 = carry
-        r2 = raw(i + 2)
-        o2 = sweep(0, i + 1, r1, r0, r2, outside(i + 1))
-        moved = sweep(1, i, o1, o0, o2, outside(i))
-        return moved, (r1, r2, o1, o2)
-
-    def put(i, moved):
-        moved_ref[pl.ds(i, chans, stride=cells_x), :] = moved
-
-    ra, rb, rc, rd = raw(-3), raw(-2), raw(-1), raw(0)
-    carry = (rc, rd, sweep(0, -2, rb, ra, rc, True), sweep(0, -1, rc, rb, rd, True))
-    above, carry = step(-1, carry)
-
-    def rows(n, carry):
-        for u in range(ROW_UNROLL):
-            i = n * ROW_UNROLL + u
-            moved, carry = step(i, carry)
-            put(i, moved)
-        return carry
-
-    steps = (cells_x - 2) // ROW_UNROLL
-    carry = lax.fori_loop(0, steps, rows, carry)
-    for i in range(steps * ROW_UNROLL, cells_x):
-        moved, carry = step(i, carry)
-        put(i, moved)
-    below, _ = step(cells_x, carry)
-
-    def row(i):
-        if i < 0:
-            return above
-        if i >= cells_x:
-            return below
-        return moved_ref[pl.ds(i, chans, stride=cells_x), :]
-
-    zero = jnp.zeros((chans, width), F32)
-    for q in range(2):
-        base = q * half
-        items = {0: row(base - 1), 1: row(base + half), 4: row(base + part)}
-        for k in range(EXTRA):
-            if k not in (2, 3):
-                extra[q, pl.ds(k, chans, stride=EXTRA), :] = items.get(k, zero)
+    rows = cells_x + 16
+    at = lax.broadcasted_iota(jnp.int32, (rows, width), 0) - 8
+    diagonal = (at + width) % width == lanes_of((rows, width))
+    fetch.wait()
+
+    group = next(n for n in (GROUP, 2, 1) if chans % n == 0)
+
+    def sweep(level, src, dst, base):
+        parts = []
+        for g in range(group):
+            c = base + g
+            q = src[c, pl.ds(8, rows), :]
+            hi = q.astype(BF16)
+            lo = (q - hi.astype(F32)).astype(BF16)
+            sides = []
+            for side in range(2):
+                main = line_s[level, side, 0, pl.ds(c, 1), :]
+                aux = line_s[level, side, 1, pl.ds(c, 1), :]
+                values = jnp.concatenate(
+                    [
+                        jnp.broadcast_to(aux, (8, width)),
+                        jnp.broadcast_to(main, (cells_x, width)),
+                        jnp.broadcast_to(aux, (8, width)),
+                    ],
+                    axis=0,
+                )
+                sides.append(jnp.where(diagonal, values, 0.0).astype(BF16))
+            parts.append(jnp.concatenate([hi, lo] + sides, axis=1))
+        near = lax.dot_general(
+            jnp.concatenate(parts, axis=0),
+            matrix[...],
+            (((1,), (0,)), ((), ())),
+            preferred_element_type=F32,
+        )
+        for g in range(group):
+            c = base + g
+            lower, upper = near[g * rows : (g + 1) * rows, :width], near[g * rows : (g + 1) * rows, width:]
+            c0, cxl, cxu, cyl, cyu = [speed_ref[n, c] for n in range(5)]
+            dst[c, pl.ds(8, rows), :] = (
+                c0 * src[c, pl.ds(8, rows), :]
+                + cxl * src[c, pl.ds(7, rows), :]
+                + cxu * src[c, pl.ds(9, rows), :]
+                + cyl * lower
+                + cyu * upper
+            )
+
+    def finish(base):
+        for g in range(group):
+            c = base + g
+            moved_ref[c] = last_s[c, pl.ds(MARGIN, cells_x), :]
+            for q in range(2):
+                for k, i in ((0, -1), (1, half), (4, part)):
+                    extra[q, pl.ds(c * EXTRA + k, 1), :] = last_s[c, pl.ds(MARGIN + q * half + i, 1), :]
+            for dst0, dst1, q in ((mine0, mine1, own), (theirs0, theirs1, 1 - own)):
+                start = pl.multiple_of(MARGIN + q * half, 8)
+                dst0[c, 0:EXTRA] = extra[q, pl.ds(c * EXTRA, EXTRA), :].astype(BF16)
+                dst0[c, EXTRA : EXTRA + part] = last_s[c, pl.ds(start, part), :].astype(BF16)
+                dst1[c] = last_s[c, pl.ds(start + part, part), :].astype(BF16)
 
     for c in range(chans):
-        for dst0, dst1, q in ((mine0, mine1, own), (theirs0, theirs1, 1 - own)):
-            start = pl.multiple_of(c * cells_x + q * half, 8)
-            dst0[c, 0:EXTRA] = extra[q, pl.ds(c * EXTRA, EXTRA), :].astype(BF16)
-            dst0[c, EXTRA : EXTRA + part] = moved_ref[pl.ds(start, part), :].astype(BF16)
-            dst1[c] = moved_ref[pl.ds(start + part, part), :].astype(BF16)
+        raw_s[c, pl.ds(MARGIN - DEEP, DEEP), :] = border[1, pl.ds(c * message + 16 - DEEP, DEEP), :]
+        raw_s[c, pl.ds(MARGIN + cells_x, DEEP), :] = border[2, pl.ds(c * message, DEEP), :]
+    for base in range(0, chans + group, group):
+        if base < chans:
+            sweep(0, raw_s, once_s, base)
+        if base:
+            sweep(1, once_s, last_s, base - group)
+            finish(base - group)
 
 
 def physics_kernel(chunk, table_ref, w1_ref, w2_ref, w3_ref, *rest):
@@ -364,23 +375,30 @@
             nu - jnp.minimum(ay, 0.0),
         ]
     )
-    coef = jnp.broadcast_to(coef[:, :, None], (5, chans, cells_y))
+    wide_coef = jnp.broadcast_to(coef[:, :, None], (5, chans, cells_y))
 
     def flat(x):
         return x.reshape(-1, cells_y)
 
     win0 = sds((chans, EXTRA + part, cells_y), BF16)
     win1 = sds((chans, part, cells_y), BF16)
+    tall = pltpu.VMEM((chans, cells_x + 2 * MARGIN, cells_y), F32)
     moved, mine0, mine1, theirs0, theirs1 = call(
-        functools.partial(transport_kernel, cells_x=cells_x),
+        functools.partial(transport_kernel, chans=chans),
         "transport",
-        (sds((chans * cells_x, cells_y), F32), win0, win1, win0, win1),
-        [VMEM_SPEC] * 5,
+        (sds((chans, cells_x, cells_y), F32), win0, win1, win0, win1),
+        [ANY_SPEC, pl.BlockSpec(memory_space=pltpu.SMEM)] + [VMEM_SPEC] * 4,
         [
             pltpu.VMEM((3, chans * message.shape[1], cells_y), F32),
             pltpu.VMEM((2, chans * EXTRA, cells_y), F32),
+            tall,
+            tall,
+            tall,
+            pltpu.VMEM((2, 2, 2, chans, cells_y), F32),
+            pltpu.VMEM((4 * cells_y, 2 * cells_y), BF16),
+            pltpu.SemaphoreType.DMA((1,)),
         ],
-    )(flat(block), coef, flat(message), flat(up), flat(down))
+    )(block, coef, wide_coef, flat(message), flat(up), flat(down))
 
     def swap(x):
         return lax.ppermute(x, "group", [(0, 1), (1, 0)])
@@ -425,7 +443,7 @@
     back1 = swap(other1)
     updated = call(
         finish_kernel, "finish", sds((chans, cells_x, cells_y), F32), [VMEM_SPEC] * 5
-    )(moved.reshape(chans, cells_x, cells_y), own0, own1, back0, back1)
+    )(moved, own0, own1, back0, back1)
     return updated.reshape(levels, fields, single, cells_x, cells_y)
 
 

time: 69.5 us -> 66 us (0.950)
  Pallas kernels: 30.1 us -> 26.4 us
    pallas_call x1, Pallas kernels: 9.58 us -> 5.9 us  [shards(): call(functools.partial(transport_kernel, chans=chans), 'transport', (sds(...]
    unnamed x28 -> x30, local copies, waits for them, and re-layouts: 2.86 us -> 2.9 us
  transfers between devices with their start and end apart: 7 -> 7, of which waited for: 5 -> 5; matrix products, arithmetic and copies ran while one was open for 7% -> 7% of each run, Pallas kernels for 11% -> 12%
where the time goes in v2:
time: 66 us; the launch traced here: 65.4 us
  Pallas kernels  26.4 us (40%)
  waiting for transfers between devices  19.2 us (29%)
  starting transfers between devices  11.1 us (17%)
  local copies, waits for them, and re-layouts  8.31 us (13%)
    pallas_call x2, Pallas kernels, physics(): call(functools.partial(physics_kernel, chunk), f'physics{chunk}', (win1,...  15.3 us
    ppermute x4, waiting for transfers between devices, swap(): return lax.ppermute(x, 'group', [(0, 1), (1, 0)])  10.6 us
    ppermute x1, waiting for transfers between devices, across(): lax.ppermute(x, 'tile', [(i, (i + by) % tiles) for i in range(tiles)])  8.39 us
    pallas_call x1, Pallas kernels, shards(): call(functools.partial(transport_kernel, chans=chans), 'transport', (sds(...  5.9 us
    ppermute x1, starting transfers between devices, shards(): from_east = lax.ppermute(to_west, 'tile', beside(-1))  4.54 us
    ppermute x4, starting transfers between devices, swap(): return lax.ppermute(x, 'group', [(0, 1), (1, 0)])  4.25 us
    unnamed x30, local copies, waits for them, and re-layouts  2.9 us
    pallas_call x1, Pallas kernels, shards(): call(finish_kernel, 'finish', sds((chans, cells_x, cells_y), F32), [VMEM_...  2.69 us
  transfers between devices with their start and end apart: 7, of which 5 were waited for; matrix products, arithmetic and copies ran while one was open for 7% of the time, Pallas kernels for 12%

profile of v2, /device:TPU:24, one launch (start us, length us, event | category | flops | bytes accessed | tf_op | source)
XLA Modules:
  0.0 65.4 jit_solution(13974674271598421968)
XLA Ops:
  0.0 0.0 copy-start.11
  0.0 0.0 copy-start.12
  0.0 0.0 copy-start.10
  0.0 0.0 copy-start.9
  0.0 2.5 %edges.1 = (bf16[20,8,128]{2,1,0:T(8,128)(2,1)}, bf16[20,8,128]{2,1,0:T(8,128)(2,1)}, bf16[20,16,128]{2,1,0:T(8,128)(2,1)}) custom-call(f32[20,128,128]{2,1,0:T(8,128)} %bitcast.12), custom_call_target="tpu_custom_call" | custom-call | tf_op jit(solution)/shard_map/edges/pallas_call | solution.py:345
  2.5 1.9 %collective-permute-start = (bf16[20,8,128]{2,1,0:T(8,128)(2,1)}, bf16[20,8,128]{2,1,0:T(8,128)(2,1)S(1)}, u32[]{:S(2)}, u32[]{:S(2)}) collective-permute-start(bf16[20,8,128]{2,1,0:T(8,128)(2,1)} %get-tuple-element.18), channel_id=1, source_target_pairs={{0,2},{2,4},{4,6},{6,8},{8,10},{10,12},{12,14},{16,18},{18,20},{20... | collective-permute-start | bytes 122888 | tf_op jit(solution)/shard_map/ppermute | solution.py:352
  4.4 4.5 %collective-permute-start.1 = (bf16[20,8,128]{2,1,0:T(8,128)(2,1)}, bf16[20,8,128]{2,1,0:T(8,128)(2,1)S(1)}, u32[]{:S(2)}, u32[]{:S(2)}) collective-permute-start(bf16[20,8,128]{2,1,0:T(8,128)(2,1)} %get-tuple-element.19), channel_id=1, source_target_pairs={{2,0},{4,2},{6,4},{8,6},{10,8},{12,10},{14,12},{18,16},{20,18},{22... | collective-permute-start | bytes 122888 | tf_op jit(solution)/shard_map/ppermute | solution.py:353
  9.0 0.0 copy-done.11
  9.0 0.0 copy-done.12
  9.0 0.0 copy-done.10
  9.0 0.8 %slice.14 = bf16[20,2,128]{2,1,0:T(2,128)(2,1)S(1)} slice(bf16[20,8,128]{2,1,0:T(8,128)(2,1)} %get-tuple-element.18), slice={[0:20], [1:3], [0:128]} | slice | bytes 20480 | tf_op jit(solution)/shard_map/slice | solution.py:356
  9.8 0.0 copy-start.7
  9.8 0.8 %slice.13 = bf16[20,2,128]{2,1,0:T(2,128)(2,1)S(1)} slice(bf16[20,8,128]{2,1,0:T(8,128)(2,1)} %get-tuple-element.19), slice={[0:20], [0:2], [0:128]} | slice | bytes 20480 | tf_op jit(solution)/shard_map/slice | solution.py:356
  10.7 0.0 collective-permute-done
  10.7 0.3 collective-permute-done.1
  11.0 0.0 copy-start.3
  11.0 1.1 %concatenate.3 = bf16[20,32,128]{2,1,0:T(8,128)(2,1)S(1)} concatenate(bf16[20,16,128]{2,1,0:T(8,128)(2,1)} %get-tuple-element.17, bf16[20,3,128]{2,1,0:T(4,128)(2,1)S(1)} %slice.16, bf16[20,2,128]{2,1,0:T(2,128)(2,1)S(1)} %slice.13, bf16[20,3,128]{2,1,0:T(4,128)(2,1)S(1)} %broadcast_in_dim.27, bf16[20,2,128]{2,1,0:T(2,128)(2,1)S(1)} %slice.14, bf16[20,3,128]{2,1,0:T(4,128)(2,1)S(1)} %slice.17, ...), dimensions={1} | concatenate | bytes 327680 | tf_op jit(solution)/shard_map/concatenate | solution.py:355
  12.0 0.0 copy-start.2
  12.0 0.4 collective-permute-start.2
  12.4 0.1 broadcast_subtract_fusion
  12.5 0.1 sub.70
  12.6 0.1 sub.68
  12.7 0.1 add.33
  12.8 0.1 add.31
  12.8 0.1 sub.66
  12.9 0.0 copy-done.9
  13.0 0.0 copy-start.8
  13.0 8.4 %collective-permute-done.2 = bf16[20,32,128]{2,1,0:T(8,128)(2,1)S(1)} collective-permute-done((bf16[20,32,128]{2,1,0:T(8,128)(2,1)S(1)}, bf16[20,32,128]{2,1,0:T(8,128)(2,1)S(1)}, u32[]{:S(2)}, u32[]{:S(2)}) %collective-permute-start.2) | collective-permute-done | bytes 163872 | tf_op jit(solution)/shard_map/ppermute | solution.py:361
  21.4 0.0 copy-start.1
  21.4 0.7 %broadcast_in_dim.26.coef_ref = f32[5,20,128]{2,1,0:T(8,128)} broadcast(f32[5,20]{1,0:T(8,128)S(1)} %stack.2.speed_ref), dimensions={0,1} | broadcast | bytes 51600 | tf_op jit(solution)/shard_map/broadcast_in_dim | solution.py:378
  22.1 0.0 copy-done.2
  22.1 0.0 copy-done.8
  22.1 0.0 copy-done.1
  22.1 5.9 %transport.1 = (f32[20,128,128]{2,1,0:T(8,128)}, bf16[20,48,128]{2,1,0:T(8,128)(2,1)}, bf16[20,32,128]{2,1,0:T(8,128)(2,1)}, bf16[20,48,128]{2,1,0:T(8,128)(2,1)}, bf16[20,32,128]{2,1,0:T(8,128)(2,1)}) custom-call(f32[20,128,128]{2,1,0:T(8,128)} %bitcast.13, f32[5,20]{1,0:T(8,128)} %copy-done.8, f32[5,20,128]{2,1,0:T(8,128)} %broadcast_in_dim.26.coef_ref, ...), custom_call_target="tpu_custom_call" | custom-call | tf_op jit(solution)/shard_map/transport/pallas_call | solution.py:386
  28.0 1.6 %collective-permute-start.3 = (bf16[20,48,128]{2,1,0:T(8,128)(2,1)}, bf16[20,48,128]{2,1,0:T(8,128)(2,1)S(1)}, u32[]{:S(2)}, u32[]{:S(2)}) collective-permute-start(bf16[20,48,128]{2,1,0:T(8,128)(2,1)} %get-tuple-element.22), channel_id=1, source_target_pairs={{0,1},{1,0},{2,3},{3,2},{4,5},{5,4},{6,7},{7,6},{8,9},{9,8},{10,11... | collective-permute-start | bytes 737288 | tf_op jit(solution)/shard_map/ppermute | solution.py:404
  29.6 0.6 pad.9
  30.2 0.0 copy-done.7
  30.2 0.8 %copy.14 = bf16[256,256]{0,1:T(8,128)(2,1)} copy(bf16[256,256]{1,0:T(8,128)(2,1)S(1)} %copy-done.7) | data formatting | bytes 262144 | tf_op args[6]
  31.0 0.0 copy-done.3
  31.0 0.1 reshape.171
  31.1 0.5 collective-permute-start.4
  31.6 0.1 fusion
  31.7 0.1 copy.18
  31.8 0.8 %copy.15.w1_ref = bf16[256,432]{1,0:T(8,128)(2,1)} copy(bf16[256,432]{0,1:T(8,128)(2,1)S(1)} %bitcast.16) | data formatting | bytes 442368 | tf_op jit(solution)/shard_map/reshape | solution.py:416
  32.6 4.5 %collective-permute-done.3.rest_1_ = bf16[20,48,128]{2,1,0:T(8,128)(2,1)S(1)} collective-permute-done((bf16[20,48,128]{2,1,0:T(8,128)(2,1)}, bf16[20,48,128]{2,1,0:T(8,128)(2,1)S(1)}, u32[]{:S(2)}, u32[]{:S(2)}) %collective-permute-start.3) | collective-permute-done | bytes 245792 | tf_op jit(solution)/shard_map/ppermute | solution.py:404
  37.1 0.0 copy-start
  37.1 0.7 %copy-done = bf16[20,48,128]{2,1,0:T(8,128)(2,1)} copy-done((bf16[20,48,128]{2,1,0:T(8,128)(2,1)}, bf16[20,48,128]{2,1,0:T(8,128)(2,1)S(1)}, u32[]{:S(2)}) %copy-start) | copy-done | bytes 245784
  37.8 7.5 %physics0.1 = (bf16[20,32,128]{2,1,0:T(8,128)(2,1)}, bf16[20,32,128]{2,1,0:T(8,128)(2,1)}) custom-call(s32[9,1,128,128]{3,2,1,0:T(8,128)} %table_ref.3, bf16[256,432]{1,0:T(8,128)(2,1)} %copy.15.w1_ref, bf16[256,256]{1,0:T(8,128)(2,1)} %bitcast.14, bf16[48,256]{1,0:T(8,128)(2,1)} %bitcast.20, bf16[20,48,128]{2,1,0:T(8,128)(2,1)} %get-tuple-element.21.rest_0_, ...), custom_call_target="tpu_custom_call" | custom-call | tf_op jit(solution)/shard_map/physics0/pallas_call | solution.py:422
  45.4 0.0 copy-start.13
  45.4 0.0 collective-permute-done.4.rest_3_
  45.4 0.0 copy-start.6
  45.4 0.7 %copy-done.6 = bf16[20,32,128]{2,1,0:T(8,128)(2,1)} copy-done((bf16[20,32,128]{2,1,0:T(8,128)(2,1)}, bf16[20,32,128]{2,1,0:T(8,128)(2,1)S(1)}, u32[]{:S(2)}) %copy-start.6) | copy-done | bytes 163864
  46.0 7.8 %physics1.1 = (bf16[20,32,128]{2,1,0:T(8,128)(2,1)}, bf16[20,32,128]{2,1,0:T(8,128)(2,1)}) custom-call(s32[9,1,128,128]{3,2,1,0:T(8,128)} %table_ref.3, bf16[256,432]{1,0:T(8,128)(2,1)} %copy.15.w1_ref, bf16[256,256]{1,0:T(8,128)(2,1)} %bitcast.15, bf16[48,256]{1,0:T(8,128)(2,1)} %bitcast.21, bf16[20,48,128]{2,1,0:T(8,128)(2,1)} %get-tuple-element.21.rest_0_, ...), custom_call_target="tpu_custom_call" | custom-call | tf_op jit(solution)/shard_map/physics1/pallas_call | solution.py:422
  53.9 1.6 %collective-permute-start.6 = (bf16[20,32,128]{2,1,0:T(8,128)(2,1)}, bf16[20,32,128]{2,1,0:T(8,128)(2,1)S(1)}, u32[]{:S(2)}, u32[]{:S(2)}) collective-permute-start(bf16[20,32,128]{2,1,0:T(8,128)(2,1)} %get-tuple-element.28), channel_id=1, source_target_pairs={{0,1},{1,0},{2,3},{3,2},{4,5},{5,4},{6,7},{7,6},{8,9},{9,8},{10,11... | collective-permute-start | bytes 491528 | tf_op jit(solution)/shard_map/ppermute | solution.py:404
  55.5 0.0 copy-done.13
  55.5 0.5 collective-permute-start.5
  56.0 4.4 %collective-permute-done.6.b1 = bf16[20,32,128]{2,1,0:T(8,128)(2,1)S(1)} collective-permute-done((bf16[20,32,128]{2,1,0:T(8,128)(2,1)}, bf16[20,32,128]{2,1,0:T(8,128)(2,1)S(1)}, u32[]{:S(2)}, u32[]{:S(2)}) %collective-permute-start.6) | collective-permute-done | bytes 163872 | tf_op jit(solution)/shard_map/ppermute | solution.py:404
  60.3 0.0 copy-start.4
  60.3 1.8 %collective-permute-done.5.b0 = bf16[20,32,128]{2,1,0:T(8,128)(2,1)S(1)} collective-permute-done((bf16[20,32,128]{2,1,0:T(8,128)(2,1)S(1)}, bf16[20,32,128]{2,1,0:T(8,128)(2,1)S(1)}, u32[]{:S(2)}, u32[]{:S(2)}) %collective-permute-start.5) | collective-permute-done | bytes 163872 | tf_op jit(solution)/shard_map/ppermute | solution.py:404
  62.1 0.0 copy-start.5
  62.1 0.0 copy-done.4
  62.1 0.7 %copy-done.5 = bf16[20,32,128]{2,1,0:T(8,128)(2,1)} copy-done((bf16[20,32,128]{2,1,0:T(8,128)(2,1)}, bf16[20,32,128]{2,1,0:T(8,128)(2,1)S(1)}, u32[]{:S(2)}) %copy-start.5) | copy-done | bytes 163864
  62.7 2.7 %finish.1 = f32[20,128,128]{2,1,0:T(8,128)} custom-call(f32[20,128,128]{2,1,0:T(8,128)} %get-tuple-element.20.moved_ref, bf16[20,32,128]{2,1,0:T(8,128)(2,1)} %get-tuple-element.23.rest_4_.a0, bf16[20,32,128]{2,1,0:T(8,128)(2,1)} %get-tuple-element.26.a1, bf16[20,32,128]{2,1,0:T(8,128)(2,1)} %copy-done.5, bf16[20,32,128]{2,1,0:T(8,128)(2,1)} %copy-done.4), custom_call_target="tpu_custom_call" | custom-call | tf_op jit(solution)/shard_map/finish/pallas_call | solution.py:444
  (9 shorter events, 0.1 us)
Async XLA Ops:
  0.0 9.0 %copy-start.11 = (f32[4]{0:T(128)S(1)}, f32[4]{0:T(128)}, u32[]{:S(2)}) copy-start(f32[4]{0:T(128)} %param.10) | copy-start | bytes 52
  0.0 9.0 %copy-start.12 = (f32[4]{0:T(128)S(1)}, f32[4]{0:T(128)}, u32[]{:S(2)}) copy-start(f32[4]{0:T(128)} %param.9) | copy-start | bytes 52
  0.0 9.0 %copy-start.10 = (f32[5]{0:T(128)S(1)}, f32[5]{0:T(128)}, u32[]{:S(2)}) copy-start(f32[5]{0:T(128)} %param.11) | copy-start | bytes 64
  0.0 12.9 %copy-start.9 = (bf16[256,40]{0,1:T(8,128)(2,1)S(1)}, bf16[256,40]{0,1:T(8,128)(2,1)}, u32[]{:S(2)}) copy-start(bf16[256,40]{0,1:T(8,128)(2,1)} %param.15) | copy-start | bytes 61444
  2.5 8.2 %collective-permute-start = (bf16[20,8,128]{2,1,0:T(8,128)(2,1)}, bf16[20,8,128]{2,1,0:T(8,128)(2,1)S(1)}, u32[]{:S(2)}, u32[]{:S(2)}) collective-permute-start(bf16[20,8,128]{2,1,0:T(8,128)(2,1)} %get-tuple-element.18), channel_id=1, source_target_pairs={{0,2},{2,4},{4,6},{6,8},{8,10},{10,12},{12,14},{16,18},{18,20},{20... | collective-permute-start | bytes 122888 | tf_op jit(solution)/shard_map/ppermute | solution.py:352
  4.4 6.5 %collective-permute-start.1 = (bf16[20,8,128]{2,1,0:T(8,128)(2,1)}, bf16[20,8,128]{2,1,0:T(8,128)(2,1)S(1)}, u32[]{:S(2)}, u32[]{:S(2)}) collective-permute-start(bf16[20,8,128]{2,1,0:T(8,128)(2,1)} %get-tuple-element.19), channel_id=1, source_target_pairs={{2,0},{4,2},{6,4},{8,6},{10,8},{12,10},{14,12},{18,16},{20,18},{22... | collective-permute-start | bytes 122888 | tf_op jit(solution)/shard_map/ppermute | solution.py:353
  9.8 20.4 %copy-start.7 = (bf16[256,256]{1,0:T(8,128)(2,1)S(1)}, bf16[256,256]{1,0:T(8,128)(2,1)}, u32[]{:S(2)}) copy-start(bf16[256,256]{1,0:T(8,128)(2,1)} %param.14) | copy-start | bytes 393220
  11.0 20.0 %copy-start.3 = (bf16[360,256]{1,0:T(8,128)(2,1)S(1)}, bf16[360,256]{1,0:T(8,128)(2,1)}, u32[]{:S(2)}) copy-start(bf16[360,256]{1,0:T(8,128)(2,1)} %param.13) | copy-start | bytes 552964
  12.0 10.1 %copy-start.2 = (bf16[20,32,128]{2,1,0:T(8,128)(2,1)}, bf16[20,32,128]{2,1,0:T(8,128)(2,1)S(1)}, u32[]{:S(2)}) copy-start(bf16[20,32,128]{2,1,0:T(8,128)(2,1)S(1)} %concatenate.3) | copy-start | bytes 491524
  12.0 9.3 %collective-permute-start.2 = (bf16[20,32,128]{2,1,0:T(8,128)(2,1)S(1)}, bf16[20,32,128]{2,1,0:T(8,128)(2,1)S(1)}, u32[]{:S(2)}, u32[]{:S(2)}) collective-permute-start(bf16[20,32,128]{2,1,0:T(8,128)(2,1)S(1)} %concatenate.3), channel_id=1, source_target_pairs={{0,16},{2,18},{4,20},{6,22},{8,24},{10,26},{12,28},{14,30},{16,0},... | collective-permute-start | bytes 491528 | tf_op jit(solution)/shard_map/ppermute | solution.py:361
  13.0 9.1 %copy-start.8 = (f32[5,20]{1,0:T(8,128)}, f32[5,20]{1,0:T(8,128)S(1)}, u32[]{:S(2)}) copy-start(f32[5,20]{1,0:T(8,128)S(1)} %stack.2.speed_ref) | copy-start | bytes 1204
  21.4 0.7 %copy-start.1 = (bf16[20,32,128]{2,1,0:T(8,128)(2,1)}, bf16[20,32,128]{2,1,0:T(8,128)(2,1)S(1)}, u32[]{:S(2)}) copy-start(bf16[20,32,128]{2,1,0:T(8,128)(2,1)S(1)} %collective-permute-done.2) | copy-start | bytes 491524
  28.0 9.1 %collective-permute-start.3 = (bf16[20,48,128]{2,1,0:T(8,128)(2,1)}, bf16[20,48,128]{2,1,0:T(8,128)(2,1)S(1)}, u32[]{:S(2)}, u32[]{:S(2)}) collective-permute-start(bf16[20,48,128]{2,1,0:T(8,128)(2,1)} %get-tuple-element.22), channel_id=1, source_target_pairs={{0,1},{1,0},{2,3},{3,2},{4,5},{5,4},{6,7},{7,6},{8,9},{9,8},{10,11... | collective-permute-start | bytes 737288 | tf_op jit(solution)/shard_map/ppermute | solution.py:404
  31.1 14.3 %collective-permute-start.4 = (bf16[20,32,128]{2,1,0:T(8,128)(2,1)}, bf16[20,32,128]{2,1,0:T(8,128)(2,1)S(1)}, u32[]{:S(2)}, u32[]{:S(2)}) collective-permute-start(bf16[20,32,128]{2,1,0:T(8,128)(2,1)} %get-tuple-element.25), channel_id=1, source_target_pairs={{0,1},{1,0},{2,3},{3,2},{4,5},{5,4},{6,7},{7,6},{8,9},{9,8},{10,11... | collective-permute-start | bytes 491528 | tf_op jit(solution)/shard_map/ppermute | solution.py:404
  37.1 0.7 %copy-start = (bf16[20,48,128]{2,1,0:T(8,128)(2,1)}, bf16[20,48,128]{2,1,0:T(8,128)(2,1)S(1)}, u32[]{:S(2)}) copy-start(bf16[20,48,128]{2,1,0:T(8,128)(2,1)S(1)} %collective-permute-done.3.rest_1_) | copy-start | bytes 737284
  45.4 10.1 %copy-start.13 = (bf16[20,32,128]{2,1,0:T(8,128)(2,1)S(1)}, bf16[20,32,128]{2,1,0:T(8,128)(2,1)}, u32[]{:S(2)}) copy-start(bf16[20,32,128]{2,1,0:T(8,128)(2,1)} %get-tuple-element.27) | copy-start | bytes 491524
  45.4 0.7 %copy-start.6 = (bf16[20,32,128]{2,1,0:T(8,128)(2,1)}, bf16[20,32,128]{2,1,0:T(8,128)(2,1)S(1)}, u32[]{:S(2)}) copy-start(bf16[20,32,128]{2,1,0:T(8,128)(2,1)S(1)} %collective-permute-done.4.rest_3_) | copy-start | bytes 491524
  53.9 6.5 %collective-permute-start.6 = (bf16[20,32,128]{2,1,0:T(8,128)(2,1)}, bf16[20,32,128]{2,1,0:T(8,128)(2,1)S(1)}, u32[]{:S(2)}, u32[]{:S(2)}) collective-permute-start(bf16[20,32,128]{2,1,0:T(8,128)(2,1)} %get-tuple-element.28), channel_id=1, source_target_pairs={{0,1},{1,0},{2,3},{3,2},{4,5},{5,4},{6,7},{7,6},{8,9},{9,8},{10,11... | collective-permute-start | bytes 491528 | tf_op jit(solution)/shard_map/ppermute | solution.py:404
  55.5 6.6 %collective-permute-start.5 = (bf16[20,32,128]{2,1,0:T(8,128)(2,1)S(1)}, bf16[20,32,128]{2,1,0:T(8,128)(2,1)S(1)}, u32[]{:S(2)}, u32[]{:S(2)}) collective-permute-start(bf16[20,32,128]{2,1,0:T(8,128)(2,1)S(1)} %copy-done.13), channel_id=1, source_target_pairs={{0,1},{1,0},{2,3},{3,2},{4,5},{5,4},{6,7},{7,6},{8,9},{9,8},{10,11... | collective-permute-start | bytes 491528 | tf_op jit(solution)/shard_map/ppermute | solution.py:404
  60.3 1.8 %copy-start.4 = (bf16[20,32,128]{2,1,0:T(8,128)(2,1)}, bf16[20,32,128]{2,1,0:T(8,128)(2,1)S(1)}, u32[]{:S(2)}) copy-start(bf16[20,32,128]{2,1,0:T(8,128)(2,1)S(1)} %collective-permute-done.6.b1) | copy-start | bytes 491524
  62.1 0.7 %copy-start.5 = (bf16[20,32,128]{2,1,0:T(8,128)(2,1)}, bf16[20,32,128]{2,1,0:T(8,128)(2,1)S(1)}, u32[]{:S(2)}) copy-start(bf16[20,32,128]{2,1,0:T(8,128)(2,1)S(1)} %collective-permute-done.5.b0) | copy-start | bytes 491524

commit v3 on v2

--- a/solution.py
+++ b/solution.py
@@ -7,6 +7,7 @@
 from jax.experimental.pallas import tpu as pltpu
 from jax.sharding import PartitionSpec as P
 
+
 TILE_ROWS = 8
 DEEP = 3
 EXTRA = 16
@@ -18,10 +19,6 @@
 VMEM_SPEC = pl.BlockSpec(memory_space=pltpu.VMEM)
 ANY_SPEC = pl.BlockSpec(memory_space=pl.ANY)
 PARAMS = pltpu.CompilerParams(vmem_limit_bytes=56 << 20)
-
-
-def whole(ref):
-    return ref[...]
 
 
 def lanes_of(shape):
@@ -43,8 +40,26 @@
         east_ref[c] = strips[0:8]
         west_ref[c] = strips[8:16]
         rows_ref[c] = jnp.concatenate(
-            [state_ref[c, 0:8], state_ref[c, cells_x - 8 : cells_x]], axis=0
+            [state_ref[c, 0:DEEP], state_ref[c, cells_x - DEEP : cells_x], state_ref[c, 0:2]], axis=0
         ).astype(BF16)
+
+
+def pack_kernel(rows_ref, west_in, east_in, west_own, east_own, out_ref, column_ref, wide, *, chans):
+    width = rows_ref.shape[1]
+    lane = lanes_of((chans, width))
+    for n, ref in enumerate((rows_ref, west_in, east_in, west_own, east_own)):
+        wide[n] = ref[...].astype(F32)
+    sources = [(1, 0), (1, 1), (1, 2), (3, 0), (3, 1), (4, 1), (4, 2), (2, 0), (2, 1), (2, 2)]
+    corner = jnp.zeros((chans, width), F32)
+    for k, (n, slot) in enumerate(sources):
+        line = wide[n, pl.ds(slot, chans, stride=8), :]
+        column_ref[k] = line
+        at = 2 * DEEP * k
+        corner = jnp.where(
+            (lane >= at) & (lane < at + 2 * DEEP), pltpu.roll(line, at + DEEP, 1), corner
+        )
+    wide[0, pl.ds(2 * DEEP, chans, stride=8), :] = corner
+    out_ref[...] = wide[0].astype(BF16)
 
 
 def shift_matrix(width):
@@ -59,31 +74,30 @@
 
 
 def transport_kernel(
-    state_ref, speed_ref, coef_ref, here_ref, up_ref, down_ref,
+    state_ref, speed_ref, coef_ref, column_ref, up_ref, down_ref,
     moved_ref, mine0, mine1, theirs0, theirs1,
     border, extra, raw_s, once_s, last_s, line_s, matrix, sem, *, chans,
 ):
     cells_x, width = state_ref.shape[1:]
     half = cells_x // 2
     part = half // 2
-    message = here_ref.shape[0] // chans
+    message = up_ref.shape[0] // chans
     own = lax.axis_index("group")
     place = lax.axis_index("tile") % TILE_ROWS
     fetch = pltpu.make_async_copy(state_ref, raw_s.at[:, pl.ds(MARGIN, cells_x)], sem.at[0])
     fetch.start()
     lane = lanes_of((chans, width))
     first, last = lane == 0, lane == width - 1
-    low_lanes = lane < width // 2
-    for s, ref in enumerate((here_ref, up_ref, down_ref)):
+    for s, ref in enumerate((up_ref, down_ref)):
         border[s] = ref[...].astype(F32)
-    coefs = [coef_ref[n] for n in range(5)]
+    coefs = [jnp.broadcast_to(coef_ref[:, n : n + 1], (chans, width)) for n in range(5)]
     matrix[...] = shift_matrix(width)
 
-    def line(s, k):
-        return border[s, pl.ds(k, chans, stride=message), :]
+    above, below = [border[s, pl.ds(2 * DEEP, chans, stride=message), :] for s in range(2)]
+    corners = jnp.where(lane % (2 * DEEP) < DEEP, above, below)
 
     def pair(k):
-        return line(0, k), jnp.where(low_lanes, line(2, k), line(1, k))
+        return column_ref[k], roll(corners, width - (2 * DEEP * k + DEEP))
 
     def roll(x, by):
         return pltpu.roll(x, by, 1)
@@ -108,7 +122,7 @@
         jnp.where(place == TILE_ROWS - 1, 0.0, 1.0),
     )
     for side in range(2):
-        raw = [pair(16 + 8 * side + k) for k in range(5)]
+        raw = [pair(5 * side + k) for k in range(5)]
         keep = keeps[side]
         inside = 3 if side == 0 else 1
         once = [
@@ -187,8 +201,8 @@
                 dst1[c] = last_s[c, pl.ds(start + part, part), :].astype(BF16)
 
     for c in range(chans):
-        raw_s[c, pl.ds(MARGIN - DEEP, DEEP), :] = border[1, pl.ds(c * message + 16 - DEEP, DEEP), :]
-        raw_s[c, pl.ds(MARGIN + cells_x, DEEP), :] = border[2, pl.ds(c * message, DEEP), :]
+        raw_s[c, pl.ds(MARGIN - DEEP, DEEP), :] = border[0, pl.ds(c * message + DEEP, DEEP), :]
+        raw_s[c, pl.ds(MARGIN + cells_x, DEEP), :] = border[1, pl.ds(c * message, DEEP), :]
     for base in range(0, chans + group, group):
         if base < chans:
             sweep(0, raw_s, once_s, base)
@@ -311,7 +325,7 @@
 
 
 def finish_kernel(moved_ref, a0, a1, b0, b1, out_ref):
-    chans, part, width = a0.shape
+    _, part, _ = a0.shape
     own = lax.axis_index("group")
     for q, pair in ((own, (a0, a1)), (1 - own, (b0, b1))):
         for n in range(2):
@@ -319,7 +333,7 @@
             out_ref[:, rows, :] = moved_ref[:, rows, :] + pair[n][...].astype(F32)
 
 
-def call(kernel, name, outs, ins, scratch=(), **cost):
+def call(kernel, outs, ins, scratch=(), flops=10**9):
     return pl.pallas_call(
         kernel,
         out_shape=outs,
@@ -327,7 +341,7 @@
         out_specs=jax.tree.map(lambda _: VMEM_SPEC, outs),
         scratch_shapes=list(scratch),
         compiler_params=PARAMS,
-        name=name,
+        cost_estimate=pl.CostEstimate(flops=flops, bytes_accessed=10**6, transcendentals=0),
     )
 
 
@@ -336,26 +350,29 @@
     chans = levels * fields
     hidden = w_mid.shape[0]
     tiles = lax.axis_size("tile")
-    half, part = cells_x // 2, cells_x // 4
+    part = cells_x // 4
     pad = -(-chans // 8) * 8
     block = state.reshape(chans, cells_x, cells_y)
     sds = jax.ShapeDtypeStruct
 
     strip = sds((chans, 8, cells_y), BF16)
-    to_east, to_west, rows = call(
-        edge_kernel, "edges", (strip, strip, sds((chans, 16, cells_y), BF16)), [VMEM_SPEC]
-    )(block)
+    to_east, to_west, rows = call(edge_kernel, (strip, strip, strip), [VMEM_SPEC])(block)
 
     def beside(by):
         return [(i, i + by) for i in range(tiles) if 0 <= i % TILE_ROWS + by < TILE_ROWS]
 
     from_west = lax.ppermute(to_east, "tile", beside(1))
     from_east = lax.ppermute(to_west, "tile", beside(-1))
-    spare = jnp.zeros((chans, 3, cells_y), BF16)
-    message = jnp.concatenate(
-        [rows, from_west[:, :3], to_west[:, :2], spare, to_east[:, 1:3], from_east[:, :3], spare],
-        axis=1,
-    )
+
+    def flat(x):
+        return x.reshape(-1, cells_y)
+
+    message, columns = call(
+        functools.partial(pack_kernel, chans=chans),
+        (sds((chans * 8, cells_y), BF16), sds((10, chans, cells_y), F32)),
+        [VMEM_SPEC] * 5,
+        [pltpu.VMEM((5, chans * 8, cells_y), F32)],
+    )(flat(rows), flat(from_west), flat(from_east), flat(to_west), flat(to_east))
 
     def across(x, by):
         return lax.ppermute(x, "tile", [(i, (i + by) % tiles) for i in range(tiles)])
@@ -375,21 +392,16 @@
             nu - jnp.minimum(ay, 0.0),
         ]
     )
-    wide_coef = jnp.broadcast_to(coef[:, :, None], (5, chans, cells_y))
-
-    def flat(x):
-        return x.reshape(-1, cells_y)
 
     win0 = sds((chans, EXTRA + part, cells_y), BF16)
     win1 = sds((chans, part, cells_y), BF16)
     tall = pltpu.VMEM((chans, cells_x + 2 * MARGIN, cells_y), F32)
     moved, mine0, mine1, theirs0, theirs1 = call(
         functools.partial(transport_kernel, chans=chans),
-        "transport",
         (sds((chans, cells_x, cells_y), F32), win0, win1, win0, win1),
         [ANY_SPEC, pl.BlockSpec(memory_space=pltpu.SMEM)] + [VMEM_SPEC] * 4,
         [
-            pltpu.VMEM((3, chans * message.shape[1], cells_y), F32),
+            pltpu.VMEM((2, chans * 8, cells_y), F32),
             pltpu.VMEM((2, chans * EXTRA, cells_y), F32),
             tall,
             tall,
@@ -398,7 +410,8 @@
             pltpu.VMEM((4 * cells_y, 2 * cells_y), BF16),
             pltpu.SemaphoreType.DMA((1,)),
         ],
-    )(block, coef, wide_coef, flat(message), flat(up), flat(down))
+        flops=5 * 10**9,
+    )(block, coef, coef.T, columns, up, down)
 
     def swap(x):
         return lax.ppermute(x, "group", [(0, 1), (1, 0)])
@@ -421,7 +434,6 @@
     def physics(chunk, *windows):
         return call(
             functools.partial(physics_kernel, chunk),
-            f"physics{chunk}",
             (win1, win1),
             [ANY_SPEC] + [VMEM_SPEC] * (3 + 2 + 2 * chunk) + [ANY_SPEC] * chunk,
             [
@@ -435,6 +447,7 @@
                 pltpu.VMEM((2, chans * part, cells_y), F32),
                 pltpu.SemaphoreType.DMA((2,)),
             ],
+            flops=7 * 10**9,
         )(neighbours, w1, w2, w3, *windows)
 
     own0, other0 = physics(0, mine0, got0)
@@ -442,7 +455,7 @@
     own1, other1 = physics(1, mine0, got0, mine1, got1, own0)
     back1 = swap(other1)
     updated = call(
-        finish_kernel, "finish", sds((chans, cells_x, cells_y), F32), [VMEM_SPEC] * 5
+        finish_kernel, sds((chans, cells_x, cells_y), F32), [VMEM_SPEC] * 5
     )(moved, own0, own1, back0, back1)
     return updated.reshape(levels, fields, single, cells_x, cells_y)
 

time: 66 us -> 63.7 us (0.965); the launches traced: 65.4 us -> 62.4 us
  waiting for transfers between devices: 19.2 us -> 16.5 us
  local copies, waits for them, and re-layouts: 8.31 us -> 6.77 us
  Pallas kernels: 26.4 us -> 27.8 us
    ppermute x1, waiting for transfers between devices: 8.39 us -> 3.87 us  [across(): lax.ppermute(x, 'tile', [(i, (i + by) % tiles) for i in range(tiles)])]
    ppermute x1, waiting for transfers between devices: 0.26 us -> 1.89 us  [shards(): from_east = lax.ppermute(to_west, 'tile', beside(-1))]
    slice x4 -> x0, local copies, waits for them, and re-layouts: 1.63 us -> none  [the longest x1 0.82 us: shards(): to_west[:, :2]]
    pallas_call x5 -> x6, Pallas kernels: 26.4 us -> 27.8 us  [the longest x2 15.3 us: physics(): call(functools.partial(physics_kernel, chunk), (win1, win1), [ANY_SPEC] +...]
    unnamed x30 -> x34, local copies, waits for them, and re-layouts: 2.9 us -> 4.09 us
    concatenate x1 -> x0, local copies, waits for them, and re-layouts: 1.05 us -> none  [shards(): jnp.concatenate([rows, from_west[:, :3], to_west[:, :2], spare, to_east[:...]
    broadcast_in_dim x2 -> x0, local copies, waits for them, and re-layouts: 0.71 us -> none  [the longest x1 0.7 us: shards(): wide_coef = jnp.broadcast_to(coef[:, :, None], (5, chans, cells_y))]
    another operation x1 -> x2, local copies, waits for them, and re-layouts: 0.02 us -> 0.71 us  [shards(): jnp.stack([1.0 - jnp.abs(ax) - jnp.abs(ay) - 4.0 * nu, jnp.maximum(ax, 0....]
  transfers between devices with their start and end apart: 7 -> 7, of which waited for: 5 -> 5; matrix products, arithmetic and copies ran while one was open for 7% -> 6% of each run, Pallas kernels for 12% -> 12%
where the time goes in v3:
time: 63.7 us; the launch traced here: 62.4 us
  Pallas kernels  27.8 us (44%)
  waiting for transfers between devices  16.5 us (26%)
  starting transfers between devices  11 us (17%)
  local copies, waits for them, and re-layouts  6.77 us (11%)
    pallas_call x2, Pallas kernels, physics(): call(functools.partial(physics_kernel, chunk), (win1, win1), [ANY_SPEC] +...  15.3 us
    ppermute x4, waiting for transfers between devices, swap(): return lax.ppermute(x, 'group', [(0, 1), (1, 0)])  10.7 us
    pallas_call x1, Pallas kernels, shards(): call(functools.partial(transport_kernel, chans=chans), (sds((chans, cells...  5.72 us
    ppermute x1, starting transfers between devices, shards(): from_east = lax.ppermute(to_west, 'tile', beside(-1))  4.54 us
    ppermute x4, starting transfers between devices, swap(): return lax.ppermute(x, 'group', [(0, 1), (1, 0)])  4.18 us
    unnamed x34, local copies, waits for them, and re-layouts  4.09 us
    ppermute x1, waiting for transfers between devices, across(): lax.ppermute(x, 'tile', [(i, (i + by) % tiles) for i in range(tiles)])  3.87 us
    pallas_call x1, Pallas kernels, shards(): call(finish_kernel, sds((chans, cells_x, cells_y), F32), [VMEM_SPEC] * 5)  2.69 us
  transfers between devices with their start and end apart: 7, of which 5 were waited for; matrix products, arithmetic and copies ran while one was open for 6% of the time, Pallas kernels for 12%

profile of v3, /device:TPU:24, one launch (start us, length us, event | category | flops | bytes accessed | tf_op | source)
XLA Modules:
  0.0 62.4 jit_solution(14049423475131126398)
XLA Ops:
  0.0 0.0 copy-start.5
  0.0 0.0 copy-start.6
  0.0 0.0 copy-start.4
  0.0 2.5 %shard_map.82 = (bf16[20,8,128]{2,1,0:T(8,128)(2,1)}, bf16[20,8,128]{2,1,0:T(8,128)(2,1)}, bf16[20,8,128]{2,1,0:T(8,128)(2,1)}) custom-call(f32[20,128,128]{2,1,0:T(8,128)} %bitcast.23), custom_call_target="tpu_custom_call" | custom-call | flops 1000000000 | bytes 1000000 | tf_op jit(solution)/shard_map/pallas_call | solution.py:359
  2.5 1.9 %collective-permute-start = (bf16[20,8,128]{2,1,0:T(8,128)(2,1)}, bf16[20,8,128]{2,1,0:T(8,128)(2,1)S(1)}, u32[]{:S(2)}, u32[]{:S(2)}) collective-permute-start(bf16[20,8,128]{2,1,0:T(8,128)(2,1)} %get-tuple-element.20), channel_id=1, source_target_pairs={{0,2},{2,4},{4,6},{6,8},{8,10},{10,12},{12,14},{16,18},{18,20},{20... | collective-permute-start | bytes 122888 | tf_op jit(solution)/shard_map/ppermute | solution.py:364
  4.4 4.5 %collective-permute-start.1 = (bf16[20,8,128]{2,1,0:T(8,128)(2,1)}, bf16[20,8,128]{2,1,0:T(8,128)(2,1)S(1)}, u32[]{:S(2)}, u32[]{:S(2)}) collective-permute-start(bf16[20,8,128]{2,1,0:T(8,128)(2,1)} %get-tuple-element.21), channel_id=1, source_target_pairs={{2,0},{4,2},{6,4},{8,6},{10,8},{12,10},{14,12},{18,16},{20,18},{22... | collective-permute-start | bytes 122888 | tf_op jit(solution)/shard_map/ppermute | solution.py:365
  8.9 0.0 copy-done.5
  8.9 0.0 copy-done.6
  9.0 0.0 copy-done.4
  9.0 0.0 collective-permute-done
  9.0 0.0 copy-start.14
  9.0 1.9 %collective-permute-done.1 = bf16[20,8,128]{2,1,0:T(8,128)(2,1)S(1)} collective-permute-done((bf16[20,8,128]{2,1,0:T(8,128)(2,1)}, bf16[20,8,128]{2,1,0:T(8,128)(2,1)S(1)}, u32[]{:S(2)}, u32[]{:S(2)}) %collective-permute-start.1) | collective-permute-done | bytes 40992 | tf_op jit(solution)/shard_map/ppermute | solution.py:365
  10.9 0.0 copy-start.15
  10.9 0.0 copy-done.14
  10.9 0.6 copy-done.15
  11.5 0.0 copy-start
  11.5 1.6 %shard_map.83 = (bf16[160,128]{1,0:T(8,128)(2,1)}, f32[10,20,128]{2,1,0:T(8,128)}) custom-call(bf16[160,128]{1,0:T(8,128)(2,1)} %bitcast.29, bf16[160,128]{1,0:T(8,128)(2,1)} %bitcast.27, bf16[160,128]{1,0:T(8,128)(2,1)} %bitcast.28, bf16[160,128]{1,0:T(8,128)(2,1)} %bitcast.26, bf16[160,128]{1,0:T(8,128)(2,1)} %bitcast.25), custom_call_target="tpu_custom_call" | custom-call | flops 1000000000 | bytes 1000000 | tf_op jit(solution)/shard_map/pallas_call | solution.py:370
  13.2 0.3 collective-permute-start.2
  13.5 0.1 broadcast_subtract_fusion
  13.6 0.1 sub.70
  13.6 0.1 sub.68
  13.7 0.1 add.33
  13.8 0.1 add.31
  13.9 0.1 sub.66
  14.0 0.0 copy-start.3
  14.0 0.7 %copy.30 = f32[5,20]{0,1:T(8,128)} copy(f32[5,20]{1,0:T(8,128)S(1)} %stack.2.speed_ref) | data formatting | bytes 800 | tf_op jit(solution)/shard_map/stack | solution.py:386
  14.7 0.0 copy-done
  14.7 0.1 reshape.181
  14.8 3.9 %collective-permute-done.2.up_ref.down_ref = bf16[160,128]{1,0:T(8,128)(2,1)S(1)} collective-permute-done((bf16[160,128]{1,0:T(8,128)(2,1)}, bf16[160,128]{1,0:T(8,128)(2,1)S(1)}, u32[]{:S(2)}, u32[]{:S(2)}) %collective-permute-start.2) | collective-permute-done | bytes 40992 | tf_op jit(solution)/shard_map/ppermute | solution.py:378
  18.7 0.0 copy-start.13
  18.7 0.0 copy-done.3
  18.7 0.6 copy-done.13
  19.3 0.0 copy-start.2
  19.3 0.0 copy-start.1
  19.3 5.7 %shard_map.84 = (f32[20,128,128]{2,1,0:T(8,128)}, bf16[20,48,128]{2,1,0:T(8,128)(2,1)}, bf16[20,32,128]{2,1,0:T(8,128)(2,1)}, bf16[20,48,128]{2,1,0:T(8,128)(2,1)}, bf16[20,32,128]{2,1,0:T(8,128)(2,1)}) custom-call(f32[20,128,128]{2,1,0:T(8,128)} %bitcast.24, f32[5,20]{1,0:T(8,128)} %copy-done.3, f32[20,5]{1,0:T(8,128)} %bitcast.22, ...), custom_call_target="tpu_custom_call" | custom-call | flops 5000000000 | bytes 1000000 | tf_op jit(solution)/shard_map/pallas_call | solution.py:399
  25.0 0.0 copy-start.8
  25.0 1.6 %collective-permute-start.3 = (bf16[20,48,128]{2,1,0:T(8,128)(2,1)}, bf16[20,48,128]{2,1,0:T(8,128)(2,1)S(1)}, u32[]{:S(2)}, u32[]{:S(2)}) collective-permute-start(bf16[20,48,128]{2,1,0:T(8,128)(2,1)} %get-tuple-element.26), channel_id=1, source_target_pairs={{0,1},{1,0},{2,3},{3,2},{4,5},{5,4},{6,7},{7,6},{8,9},{9,8},{10,11... | collective-permute-start | bytes 737288 | tf_op jit(solution)/shard_map/ppermute | solution.py:417
  26.6 0.1 fusion
  26.7 0.0 copy-done.2
  26.7 0.0 copy-done.1
  26.7 0.8 %copy.32 = bf16[256,256]{0,1:T(8,128)(2,1)} copy(bf16[256,256]{1,0:T(8,128)(2,1)S(1)} %copy-done.1) | data formatting | bytes 262144 | tf_op args[6]
  27.5 0.1 copy.36
  27.6 0.6 pad.9
  28.2 0.8 %copy.33.w1_ref = bf16[256,432]{1,0:T(8,128)(2,1)} copy(bf16[256,432]{0,1:T(8,128)(2,1)S(1)} %bitcast.16) | data formatting | bytes 442368 | tf_op jit(solution)/shard_map/reshape | solution.py:429
  29.0 0.0 copy-done.8
  29.0 0.5 collective-permute-start.4
  29.5 4.6 %collective-permute-done.3.rest_1_ = bf16[20,48,128]{2,1,0:T(8,128)(2,1)S(1)} collective-permute-done((bf16[20,48,128]{2,1,0:T(8,128)(2,1)}, bf16[20,48,128]{2,1,0:T(8,128)(2,1)S(1)}, u32[]{:S(2)}, u32[]{:S(2)}) %collective-permute-start.3) | collective-permute-done | bytes 245792 | tf_op jit(solution)/shard_map/ppermute | solution.py:417
  34.1 0.0 copy-start.7
  34.1 0.7 %copy-done.7 = bf16[20,48,128]{2,1,0:T(8,128)(2,1)} copy-done((bf16[20,48,128]{2,1,0:T(8,128)(2,1)}, bf16[20,48,128]{2,1,0:T(8,128)(2,1)S(1)}, u32[]{:S(2)}) %copy-start.7) | copy-done | bytes 245784
  34.8 7.5 %shard_map.85 = (bf16[20,32,128]{2,1,0:T(8,128)(2,1)}, bf16[20,32,128]{2,1,0:T(8,128)(2,1)}) custom-call(s32[9,1,128,128]{3,2,1,0:T(8,128)} %table_ref.3, bf16[256,432]{1,0:T(8,128)(2,1)} %copy.33.w1_ref, bf16[256,256]{1,0:T(8,128)(2,1)} %bitcast.17, bf16[48,256]{1,0:T(8,128)(2,1)} %bitcast.19, bf16[20,48,128]{2,1,0:T(8,128)(2,1)} %get-tuple-element.25.rest_0_, ...), custom_call_target="tpu_custom_call" | custom-call | flops 7000000000 | bytes 1000000 | tf_op jit(solution)/shard_map/pallas_call | solution.py:435
  42.3 0.0 collective-permute-done.4.rest_3_
  42.3 0.0 copy-start.10
  42.4 0.7 %copy-done.10 = bf16[20,32,128]{2,1,0:T(8,128)(2,1)} copy-done((bf16[20,32,128]{2,1,0:T(8,128)(2,1)}, bf16[20,32,128]{2,1,0:T(8,128)(2,1)S(1)}, u32[]{:S(2)}) %copy-start.10) | copy-done | bytes 163864
  43.0 0.0 copy-start.9
  43.0 7.9 %shard_map.86 = (bf16[20,32,128]{2,1,0:T(8,128)(2,1)}, bf16[20,32,128]{2,1,0:T(8,128)(2,1)}) custom-call(s32[9,1,128,128]{3,2,1,0:T(8,128)} %table_ref.3, bf16[256,432]{1,0:T(8,128)(2,1)} %copy.33.w1_ref, bf16[256,256]{1,0:T(8,128)(2,1)} %bitcast.18, bf16[48,256]{1,0:T(8,128)(2,1)} %bitcast.20, bf16[20,48,128]{2,1,0:T(8,128)(2,1)} %get-tuple-element.25.rest_0_, ...), custom_call_target="tpu_custom_call" | custom-call | flops 7000000000 | bytes 1000000 | tf_op jit(solution)/shard_map/pallas_call | solution.py:435
  50.9 1.6 %collective-permute-start.6 = (bf16[20,32,128]{2,1,0:T(8,128)(2,1)}, bf16[20,32,128]{2,1,0:T(8,128)(2,1)S(1)}, u32[]{:S(2)}, u32[]{:S(2)}) collective-permute-start(bf16[20,32,128]{2,1,0:T(8,128)(2,1)} %get-tuple-element.32), channel_id=1, source_target_pairs={{0,1},{1,0},{2,3},{3,2},{4,5},{5,4},{6,7},{7,6},{8,9},{9,8},{10,11... | collective-permute-start | bytes 491528 | tf_op jit(solution)/shard_map/ppermute | solution.py:417
  52.5 0.0 copy-done.9
  52.5 0.5 collective-permute-start.5
  53.0 4.4 %collective-permute-done.6.b1 = bf16[20,32,128]{2,1,0:T(8,128)(2,1)S(1)} collective-permute-done((bf16[20,32,128]{2,1,0:T(8,128)(2,1)}, bf16[20,32,128]{2,1,0:T(8,128)(2,1)S(1)}, u32[]{:S(2)}, u32[]{:S(2)}) %collective-permute-start.6) | collective-permute-done | bytes 163872 | tf_op jit(solution)/shard_map/ppermute | solution.py:417
  57.3 0.0 copy-start.11
  57.3 1.8 %collective-permute-done.5.b0 = bf16[20,32,128]{2,1,0:T(8,128)(2,1)S(1)} collective-permute-done((bf16[20,32,128]{2,1,0:T(8,128)(2,1)S(1)}, bf16[20,32,128]{2,1,0:T(8,128)(2,1)S(1)}, u32[]{:S(2)}, u32[]{:S(2)}) %collective-permute-start.5) | collective-permute-done | bytes 163872 | tf_op jit(solution)/shard_map/ppermute | solution.py:417
  59.1 0.0 copy-done.11
  59.1 0.6 %copy-done.12 = bf16[20,32,128]{2,1,0:T(8,128)(2,1)} copy-done((bf16[20,32,128]{2,1,0:T(8,128)(2,1)}, bf16[20,32,128]{2,1,0:T(8,128)(2,1)S(1)}, u32[]{:S(2)}) %copy-start.12) | copy-done | bytes 163864
  59.7 2.7 %shard_map.87 = f32[20,128,128]{2,1,0:T(8,128)} custom-call(f32[20,128,128]{2,1,0:T(8,128)} %get-tuple-element.24.moved_ref, bf16[20,32,128]{2,1,0:T(8,128)(2,1)} %get-tuple-element.27.rest_4_.a0, bf16[20,32,128]{2,1,0:T(8,128)(2,1)} %get-tuple-element.30.a1, bf16[20,32,128]{2,1,0:T(8,128)(2,1)} %copy-done.12, bf16[20,32,128]{2,1,0:T(8,128)(2,1)} %copy-done.11), custom_call_target="tpu_custom_call" | custom-call | flops 1000000000 | bytes 1000000 | tf_op jit(solution)/shard_map/pallas_call | solution.py:457
  (7 shorter events, 0.1 us)
Async XLA Ops:
  0.0 8.9 %copy-start.5 = (f32[4]{0:T(128)S(1)}, f32[4]{0:T(128)}, u32[]{:S(2)}) copy-start(f32[4]{0:T(128)} %param.10) | copy-start | bytes 52
  0.0 8.9 %copy-start.6 = (f32[4]{0:T(128)S(1)}, f32[4]{0:T(128)}, u32[]{:S(2)}) copy-start(f32[4]{0:T(128)} %param.9) | copy-start | bytes 52
  0.0 9.0 %copy-start.4 = (f32[5]{0:T(128)S(1)}, f32[5]{0:T(128)}, u32[]{:S(2)}) copy-start(f32[5]{0:T(128)} %param.11) | copy-start | bytes 64
  2.5 6.5 %collective-permute-start = (bf16[20,8,128]{2,1,0:T(8,128)(2,1)}, bf16[20,8,128]{2,1,0:T(8,128)(2,1)S(1)}, u32[]{:S(2)}, u32[]{:S(2)}) collective-permute-start(bf16[20,8,128]{2,1,0:T(8,128)(2,1)} %get-tuple-element.20), channel_id=1, source_target_pairs={{0,2},{2,4},{4,6},{6,8},{8,10},{10,12},{12,14},{16,18},{18,20},{20... | collective-permute-start | bytes 122888 | tf_op jit(solution)/shard_map/ppermute | solution.py:364
  4.4 6.5 %collective-permute-start.1 = (bf16[20,8,128]{2,1,0:T(8,128)(2,1)}, bf16[20,8,128]{2,1,0:T(8,128)(2,1)S(1)}, u32[]{:S(2)}, u32[]{:S(2)}) collective-permute-start(bf16[20,8,128]{2,1,0:T(8,128)(2,1)} %get-tuple-element.21), channel_id=1, source_target_pairs={{2,0},{4,2},{6,4},{8,6},{10,8},{12,10},{14,12},{18,16},{20,18},{22... | collective-permute-start | bytes 122888 | tf_op jit(solution)/shard_map/ppermute | solution.py:365
  9.0 1.9 %copy-start.14 = (bf16[20,8,128]{2,1,0:T(8,128)(2,1)}, bf16[20,8,128]{2,1,0:T(8,128)(2,1)S(1)}, u32[]{:S(2)}) copy-start(bf16[20,8,128]{2,1,0:T(8,128)(2,1)S(1)} %collective-permute-done) | copy-start | bytes 122884
  10.9 0.6 copy-start.15
  11.5 3.2 %copy-start = (bf16[360,256]{1,0:T(8,128)(2,1)S(1)}, bf16[360,256]{1,0:T(8,128)(2,1)}, u32[]{:S(2)}) copy-start(bf16[360,256]{1,0:T(8,128)(2,1)} %param.13) | copy-start | bytes 552964
  13.2 5.5 %collective-permute-start.2 = (bf16[160,128]{1,0:T(8,128)(2,1)}, bf16[160,128]{1,0:T(8,128)(2,1)S(1)}, u32[]{:S(2)}, u32[]{:S(2)}) collective-permute-start(bf16[160,128]{1,0:T(8,128)(2,1)} %get-tuple-element.23), channel_id=1, source_target_pairs={{0,16},{2,18},{4,20},{6,22},{8,24},{10,26},{12,28},{14,30},{16,0},... | collective-permute-start | bytes 122888 | tf_op jit(solution)/shard_map/ppermute | solution.py:378
  14.0 4.7 %copy-start.3 = (f32[5,20]{1,0:T(8,128)}, f32[5,20]{1,0:T(8,128)S(1)}, u32[]{:S(2)}) copy-start(f32[5,20]{1,0:T(8,128)S(1)} %stack.2.speed_ref) | copy-start | bytes 1204
  18.7 0.6 copy-start.13
  19.3 7.4 %copy-start.2 = (bf16[256,40]{0,1:T(8,128)(2,1)S(1)}, bf16[256,40]{0,1:T(8,128)(2,1)}, u32[]{:S(2)}) copy-start(bf16[256,40]{0,1:T(8,128)(2,1)} %param.15) | copy-start | bytes 61444
  19.3 7.4 %copy-start.1 = (bf16[256,256]{1,0:T(8,128)(2,1)S(1)}, bf16[256,256]{1,0:T(8,128)(2,1)}, u32[]{:S(2)}) copy-start(bf16[256,256]{1,0:T(8,128)(2,1)} %param.14) | copy-start | bytes 393220
  25.0 4.0 %copy-start.8 = (bf16[20,32,128]{2,1,0:T(8,128)(2,1)S(1)}, bf16[20,32,128]{2,1,0:T(8,128)(2,1)}, u32[]{:S(2)}) copy-start(bf16[20,32,128]{2,1,0:T(8,128)(2,1)} %get-tuple-element.29) | copy-start | bytes 491524
  25.0 9.1 %collective-permute-start.3 = (bf16[20,48,128]{2,1,0:T(8,128)(2,1)}, bf16[20,48,128]{2,1,0:T(8,128)(2,1)S(1)}, u32[]{:S(2)}, u32[]{:S(2)}) collective-permute-start(bf16[20,48,128]{2,1,0:T(8,128)(2,1)} %get-tuple-element.26), channel_id=1, source_target_pairs={{0,1},{1,0},{2,3},{3,2},{4,5},{5,4},{6,7},{7,6},{8,9},{9,8},{10,11... | collective-permute-start | bytes 737288 | tf_op jit(solution)/shard_map/ppermute | solution.py:417
  29.0 13.3 %collective-permute-start.4 = (bf16[20,32,128]{2,1,0:T(8,128)(2,1)S(1)}, bf16[20,32,128]{2,1,0:T(8,128)(2,1)S(1)}, u32[]{:S(2)}, u32[]{:S(2)}) collective-permute-start(bf16[20,32,128]{2,1,0:T(8,128)(2,1)S(1)} %copy-done.8), channel_id=1, source_target_pairs={{0,1},{1,0},{2,3},{3,2},{4,5},{5,4},{6,7},{7,6},{8,9},{9,8},{10,11... | collective-permute-start | bytes 491528 | tf_op jit(solution)/shard_map/ppermute | solution.py:417
  34.1 0.7 %copy-start.7 = (bf16[20,48,128]{2,1,0:T(8,128)(2,1)}, bf16[20,48,128]{2,1,0:T(8,128)(2,1)S(1)}, u32[]{:S(2)}) copy-start(bf16[20,48,128]{2,1,0:T(8,128)(2,1)S(1)} %collective-permute-done.3.rest_1_) | copy-start | bytes 737284
  42.3 0.7 %copy-start.10 = (bf16[20,32,128]{2,1,0:T(8,128)(2,1)}, bf16[20,32,128]{2,1,0:T(8,128)(2,1)S(1)}, u32[]{:S(2)}) copy-start(bf16[20,32,128]{2,1,0:T(8,128)(2,1)S(1)} %collective-permute-done.4.rest_3_) | copy-start | bytes 491524
  43.0 9.5 %copy-start.9 = (bf16[20,32,128]{2,1,0:T(8,128)(2,1)S(1)}, bf16[20,32,128]{2,1,0:T(8,128)(2,1)}, u32[]{:S(2)}) copy-start(bf16[20,32,128]{2,1,0:T(8,128)(2,1)} %get-tuple-element.31) | copy-start | bytes 491524
  50.9 6.5 %collective-permute-start.6 = (bf16[20,32,128]{2,1,0:T(8,128)(2,1)}, bf16[20,32,128]{2,1,0:T(8,128)(2,1)S(1)}, u32[]{:S(2)}, u32[]{:S(2)}) collective-permute-start(bf16[20,32,128]{2,1,0:T(8,128)(2,1)} %get-tuple-element.32), channel_id=1, source_target_pairs={{0,1},{1,0},{2,3},{3,2},{4,5},{5,4},{6,7},{7,6},{8,9},{9,8},{10,11... | collective-permute-start | bytes 491528 | tf_op jit(solution)/shard_map/ppermute | solution.py:417
  52.5 6.6 %collective-permute-start.5 = (bf16[20,32,128]{2,1,0:T(8,128)(2,1)S(1)}, bf16[20,32,128]{2,1,0:T(8,128)(2,1)S(1)}, u32[]{:S(2)}, u32[]{:S(2)}) collective-permute-start(bf16[20,32,128]{2,1,0:T(8,128)(2,1)S(1)} %copy-done.9), channel_id=1, source_target_pairs={{0,1},{1,0},{2,3},{3,2},{4,5},{5,4},{6,7},{7,6},{8,9},{9,8},{10,11... | collective-permute-start | bytes 491528 | tf_op jit(solution)/shard_map/ppermute | solution.py:417
  57.3 1.8 %copy-start.11 = (bf16[20,32,128]{2,1,0:T(8,128)(2,1)}, bf16[20,32,128]{2,1,0:T(8,128)(2,1)S(1)}, u32[]{:S(2)}) copy-start(bf16[20,32,128]{2,1,0:T(8,128)(2,1)S(1)} %collective-permute-done.6.b1) | copy-start | bytes 491524
  59.1 0.7 %copy-start.12 = (bf16[20,32,128]{2,1,0:T(8,128)(2,1)}, bf16[20,32,128]{2,1,0:T(8,128)(2,1)S(1)}, u32[]{:S(2)}) copy-start(bf16[20,32,128]{2,1,0:T(8,128)(2,1)S(1)} %collective-permute-done.5.b0) | copy-start | bytes 491524

commit v4 on v3

--- a/solution.py
+++ b/solution.py
@@ -10,7 +10,8 @@
 
 TILE_ROWS = 8
 DEEP = 3
-EXTRA = 16
+EXTRA = 8
+BLOCK_ROWS = 16
 MARGIN = 16
 GROUP = 4
 
@@ -75,12 +76,13 @@
 
 def transport_kernel(
     state_ref, speed_ref, coef_ref, column_ref, up_ref, down_ref,
-    moved_ref, mine0, mine1, theirs0, theirs1,
-    border, extra, raw_s, once_s, last_s, line_s, matrix, sem, *, chans,
+    moved_ref, *rest, chans, chunks,
 ):
+    count = len(chunks)
+    mine, theirs, rest = rest[:count], rest[count : 2 * count], rest[2 * count :]
+    windows, (border, raw_s, once_s, last_s, line_s, matrix, sem) = rest[:count], rest[count:]
     cells_x, width = state_ref.shape[1:]
     half = cells_x // 2
-    part = half // 2
     message = up_ref.shape[0] // chans
     own = lax.axis_index("group")
     place = lax.axis_index("tile") % TILE_ROWS
@@ -88,6 +90,7 @@
     fetch.start()
     lane = lanes_of((chans, width))
     first, last = lane == 0, lane == width - 1
+    low_lanes = lane < width // 2
     for s, ref in enumerate((up_ref, down_ref)):
         border[s] = ref[...].astype(F32)
     coefs = [jnp.broadcast_to(coef_ref[:, n : n + 1], (chans, width)) for n in range(5)]
@@ -121,6 +124,7 @@
         jnp.where(place == 0, 0.0, 1.0),
         jnp.where(place == TILE_ROWS - 1, 0.0, 1.0),
     )
+    edges = []
     for side in range(2):
         raw = [pair(5 * side + k) for k in range(5)]
         keep = keeps[side]
@@ -133,13 +137,18 @@
         for level, edge in enumerate((raw[2], once[1])):
             for n in range(2):
                 line_s[level, side, n] = edge[n]
-        for q in range(2):
-            if q == 0:
-                lineup = jnp.where(first, roll(aux, 1), roll(main, 1))
-            else:
-                by = width - half + 1
-                lineup = jnp.where(lane <= half, roll(main, by), roll(aux, by))
-            extra[q, pl.ds(2 + side, chans, stride=EXTRA), :] = lineup
+        edges.append((main, aux))
+    for q in range(2):
+        for window, (start, size) in zip(windows, chunks):
+            at = q * half + start - 1
+            sides = []
+            for side, first_lane in enumerate((0, width // 2)):
+                main, aux = edges[side]
+                by = (first_lane - at) % width
+                row_of = lane - first_lane + at
+                off = (row_of < 0) | (row_of >= cells_x)
+                sides.append(jnp.where(off, roll(aux, by), roll(main, by)))
+            window[q, pl.ds(2, chans, stride=EXTRA + size), :] = jnp.where(low_lanes, *sides)
 
     rows = cells_x + 16
     at = lax.broadcasted_iota(jnp.int32, (rows, width), 0) - 8
@@ -187,18 +196,26 @@
                 + cyu * upper
             )
 
+    outs = []
+
     def finish(base):
         for g in range(group):
             c = base + g
-            moved_ref[c] = last_s[c, pl.ds(MARGIN, cells_x), :]
             for q in range(2):
-                for k, i in ((0, -1), (1, half), (4, part)):
-                    extra[q, pl.ds(c * EXTRA + k, 1), :] = last_s[c, pl.ds(MARGIN + q * half + i, 1), :]
-            for dst0, dst1, q in ((mine0, mine1, own), (theirs0, theirs1, 1 - own)):
-                start = pl.multiple_of(MARGIN + q * half, 8)
-                dst0[c, 0:EXTRA] = extra[q, pl.ds(c * EXTRA, EXTRA), :].astype(BF16)
-                dst0[c, EXTRA : EXTRA + part] = last_s[c, pl.ds(start, part), :].astype(BF16)
-                dst1[c] = last_s[c, pl.ds(start + part, part), :].astype(BF16)
+                for window, (start, size) in zip(windows, chunks):
+                    at = MARGIN + q * half + start
+                    to = c * (EXTRA + size)
+                    window[q, pl.ds(to, 1), :] = last_s[c, pl.ds(at - 1, 1), :]
+                    window[q, pl.ds(to + 1, 1), :] = last_s[c, pl.ds(at + size, 1), :]
+                    window[q, pl.ds(to + EXTRA, size), :] = last_s[c, pl.ds(at, size), :]
+        outs.append(
+            pltpu.make_async_copy(
+                last_s.at[pl.ds(base, group), pl.ds(MARGIN, cells_x)],
+                moved_ref.at[pl.ds(base, group)],
+                sem.at[1 + base // group],
+            )
+        )
+        outs[-1].start()
 
     for c in range(chans):
         raw_s[c, pl.ds(MARGIN - DEEP, DEEP), :] = border[0, pl.ds(c * message + DEEP, DEEP), :]
@@ -209,68 +226,76 @@
         if base:
             sweep(1, once_s, last_s, base - group)
             finish(base - group)
-
-
-def physics_kernel(chunk, table_ref, w1_ref, w2_ref, w3_ref, *rest):
-    count = 2 if chunk == 0 else 4
-    ins, rest = rest[:count], rest[count + (chunk > 0) :]
-    own_out, other_out, wide0, wide1, slab, packed, mask, table, stacked, terms, sem = rest
-    chans, part, width = own_out.shape
-    half = 2 * part
-    pad = slab.shape[1] // 2
+    for n in range(count):
+        mine[n][...] = windows[n][own].astype(BF16)
+        theirs[n][...] = windows[n][1 - own].astype(BF16)
+    for copy in outs:
+        copy.wait()
+
+
+def physics_kernel(
+    table_ref, w1_ref, w2_ref, w3_ref, mine_ref, got_ref, image_in,
+    image_ref, other_ref, wide, packed, mask, table, even, odd, terms, patch, sem, *, start, chans,
+):
+    size, width = table.shape[1:]
+    cells_x = image_in.shape[1]
+    half = cells_x // 2
+    height = EXTRA + size
+    pad = -(-chans // 8) * 8
     both = 2 * pad
-    own = lax.axis_index("group")
-    top = own * half + chunk * part
-    copies = []
-    for n, k in enumerate((5, 7)):
-        copies.append(
-            pltpu.make_async_copy(table_ref.at[k, 0, pl.ds(top, part)], table.at[n], sem.at[n])
+    top = lax.axis_index("group") * half + start
+    copies = [
+        pltpu.make_async_copy(table_ref.at[k, 0, pl.ds(top, size)], table.at[n], sem.at[n])
+        for n, k in enumerate((5, 7))
+    ]
+    fetch = pltpu.make_async_copy(image_in.at[:, pl.ds(top, size)], patch, sem.at[2])
+    for copy in copies:
+        copy.start()
+    fetch.start()
+
+    k = lax.broadcasted_iota(jnp.int32, (2 * width, 2 * width), 0)
+    n = lax.broadcasted_iota(jnp.int32, (2 * width, 2 * width), 1)
+    inner = (k < width) & (((n < width) & (n == k + 1)) | ((n >= width) & (n - width == k - 1)))
+    west = (k >= width) & (k < width + width // 2) & (n == 0)
+    east = (k >= width + width // 2) & (n == 2 * width - 1)
+    matrix = jnp.where(inner | west | east, 1.0, 0.0).astype(BF16)
+    slot = lax.broadcasted_iota(jnp.int32, (height, width), 0)
+    line = jnp.where(
+        slot >= EXTRA, slot - EXTRA + 1, jnp.where(slot == 0, 0, jnp.where(slot == 1, size + 1, -1))
+    )
+    diagonal = lanes_of((height, width)) % (width // 2) == line
+    for s, ref in enumerate((mine_ref, got_ref)):
+        cells = ref[...]
+        flat = cells.astype(F32)
+        wide[1, s, pl.ds(0, chans * height)] = flat
+        edges = [
+            jnp.where(diagonal, flat[c * height + 2 : c * height + 3], 0.0) for c in range(chans)
+        ]
+        edges = jnp.concatenate(edges, axis=0).astype(BF16)
+        near = lax.dot_general(
+            jnp.concatenate([cells, edges], axis=1),
+            matrix,
+            (((1,), (0,)), ((), ())),
+            preferred_element_type=F32,
         )
-        copies[-1].start()
-    height0 = EXTRA + part
-    for s in range(2):
-        wide0[s] = ins[s][...].reshape(chans * height0, width).astype(F32)
-        if chunk:
-            wide1[s] = ins[2 + s][...].reshape(chans * part, width).astype(F32)
-
-    slab[...] = jnp.zeros_like(slab)
-
-    def source(s, l):
-        if chunk == 0:
-            if l < 0:
-                return wide0[s, pl.ds(0, chans, stride=height0), :]
-            if l >= part:
-                return wide0[s, pl.ds(4, chans, stride=height0), :]
-            return wide0[s, pl.ds(EXTRA + l, chans, stride=height0), :]
-        if l < 0:
-            return wide0[s, pl.ds(height0 - 1, chans, stride=height0), :]
-        if l >= part:
-            return wide0[s, pl.ds(1, chans, stride=height0), :]
-        return wide1[s, pl.ds(l, chans, stride=part), :]
-
-    for s in range(2):
-        for l in range(-1, part + 1):
-            slab[l + 1, pl.ds(s * pad, chans)] = source(s, l)
-        for k in range(2):
-            slab[part + 2 + k, pl.ds(s * pad, chans)] = wide0[s, pl.ds(2 + k, chans, stride=height0), :]
-
-    lane = lanes_of((both, width))
-
-    def shift(r, _):
-        q = slab[r]
-        idx = r + chunk * part
-        low = jnp.where(lane == 0, pltpu.roll(slab[part + 2], lax.rem(width - idx, width), 1), pltpu.roll(q, 1, 1))
-        high = jnp.where(lane == width - 1, pltpu.roll(slab[part + 3], lax.rem(2 * width - 1 - idx, width), 1), pltpu.roll(q, width - 1, 1))
-        packed[0, r] = low.astype(BF16)
-        packed[1, r] = q.astype(BF16)
-        packed[2, r] = high.astype(BF16)
-        return 0
-
-    lax.fori_loop(0, part + 2, shift, 0, unroll=2)
+        wide[0, s, pl.ds(0, chans * height)] = near[:, :width]
+        wide[2, s, pl.ds(0, chans * height)] = near[:, width:]
+        if pad > chans:
+            for b in range(3):
+                wide[b, s, pl.ds(chans * height, (pad - chans) * height)] = jnp.zeros(
+                    ((pad - chans) * height, width), F32
+                )
+
+    for l in range(-1, size + 1):
+        at = 0 if l < 0 else 1 if l == size else EXTRA + l
+        for b in range(3):
+            pair = [wide[b, s, pl.ds(at, pad, stride=height), :] for s in range(2)]
+            packed[b, l + 1] = jnp.concatenate(pair, axis=0).astype(BF16)
+
     for copy in copies:
         copy.wait()
-    rows_i = lax.broadcasted_iota(jnp.int32, (part, width), 0) + top
-    centre = (rows_i + 1) * (width + 2) + lanes_of((part, width)) + 1
+    rows_i = lax.broadcasted_iota(jnp.int32, (size, width), 0) + top
+    centre = (rows_i + 1) * (width + 2) + lanes_of((size, width)) + 1
     along_y = table[0] - centre
     along_x = table[1] - centre
     turned = jnp.abs(along_x) == 1
@@ -278,17 +303,17 @@
     mask[1] = jnp.where(jnp.where(turned, along_x, along_y) < 0, 1.0, 0.0)
     mask[2] = jnp.where(turned, 1.0, 0.0)
 
-    rows_step = stacked.shape[1] // width
-
     def choose(m, a, b):
         return jnp.where(m, a, b), jnp.where(m, b, a)
 
-    def block(b, _):
+    rows_step = even.shape[1] // width
+
+    def stack(n, dst):
         for u in range(rows_step):
-            l = b * rows_step + u
+            l = n * rows_step + u
             m = []
-            for n in range(3):
-                line = jnp.broadcast_to(mask[n, pl.ds(l, 1), :], (16, width)).astype(BF16)
+            for k in range(3):
+                line = jnp.broadcast_to(mask[k, pl.ds(l, 1), :], (16, width)).astype(BF16)
                 m.append(jnp.concatenate([line] * (both // 16), axis=0) > 0.5)
             x = [[packed[bb, l + aa] for bb in range(3)] for aa in range(3)]
             for bb in range(3):
@@ -298,47 +323,63 @@
             for aa, bb in ((0, 1), (0, 2), (1, 2)):
                 x[aa][bb], x[bb][aa] = choose(m[2], x[bb][aa], x[aa][bb])
             for k in range(9):
-                stacked[pl.ds(k * both, both), pl.ds(u * width, width)] = x[k // 3][k % 3]
-        dot = functools.partial(
-            lax.dot_general,
-            dimension_numbers=(((1,), (0,)), ((), ())),
-            preferred_element_type=F32,
-        )
-
-        def silu(v):
-            h = v * 0.5
-            return (h * jnp.tanh(h) + h).astype(BF16)
-
-        first = silu(dot(w1_ref[...], stacked[...]))
+                dst[pl.ds(k * both, both), pl.ds(u * width, width)] = x[k // 3][k % 3]
+
+    dot = functools.partial(
+        lax.dot_general,
+        dimension_numbers=(((1,), (0,)), ((), ())),
+        preferred_element_type=F32,
+    )
+
+    def silu(v):
+        h = v * 0.5
+        return (h * jnp.tanh(h) + h).astype(BF16)
+
+    def network(n, src):
+        first = silu(dot(w1_ref[...], src[...]))
         second = silu(dot(w2_ref[...], first))
         tend = dot(w3_ref[...], second)
         for u in range(rows_step):
-            l = b * rows_step + u
+            l = n * rows_step + u
             cols = slice(u * width, (u + 1) * width)
-            terms[0, pl.ds(l, chans, stride=part), :] = tend[0:chans, cols]
-            terms[1, pl.ds(l, chans, stride=part), :] = tend[pad : pad + chans, cols]
-        return 0
-
-    lax.fori_loop(0, part // rows_step, block, 0)
-    own_out[...] = terms[0].reshape(chans, part, width).astype(BF16)
-    other_out[...] = terms[1].reshape(chans, part, width).astype(BF16)
-
-
-def finish_kernel(moved_ref, a0, a1, b0, b1, out_ref):
-    _, part, _ = a0.shape
-    own = lax.axis_index("group")
-    for q, pair in ((own, (a0, a1)), (1 - own, (b0, b1))):
-        for n in range(2):
-            rows = pl.ds(pl.multiple_of(q * 2 * part + n * part, 8), part)
-            out_ref[:, rows, :] = moved_ref[:, rows, :] + pair[n][...].astype(F32)
-
-
-def call(kernel, outs, ins, scratch=(), flops=10**9):
+            terms[0, pl.ds(l, chans, stride=size), :] = tend[0:chans, cols]
+            terms[1, pl.ds(l, chans, stride=size), :] = tend[pad : pad + chans, cols]
+
+    steps = size // rows_step
+    slots = (even, odd)
+    stack(0, even)
+    for n in range(steps):
+        if n + 1 < steps:
+            stack(n + 1, slots[(n + 1) % 2])
+        network(n, slots[n % 2])
+    other_ref[...] = terms[1].astype(BF16)
+    fetch.wait()
+    patch[...] = patch[...] + terms[0].reshape(patch.shape)
+    put = pltpu.make_async_copy(patch, image_ref.at[:, pl.ds(top, size)], sem.at[3])
+    put.start()
+    put.wait()
+
+
+def finish_kernel(back_ref, image_in, image_ref, patch, sem, *, start):
+    size = patch.shape[1]
+    half = image_in.shape[1] // 2
+    rows = pl.ds((1 - lax.axis_index("group")) * half + start, size)
+    fetch = pltpu.make_async_copy(image_in.at[:, rows], patch, sem.at[0])
+    fetch.start()
+    fetch.wait()
+    patch[...] = patch[...] + back_ref[...].astype(F32).reshape(patch.shape)
+    put = pltpu.make_async_copy(patch, image_ref.at[:, rows], sem.at[1])
+    put.start()
+    put.wait()
+
+
+def call(kernel, outs, ins, scratch=(), flops=10**9, out_specs=None, aliases=None):
     return pl.pallas_call(
         kernel,
-        out_shape=outs,
+        out_shape=jax.tree.map(lambda x: jax.ShapeDtypeStruct(x.shape, x.dtype), outs),
         in_specs=ins,
-        out_specs=jax.tree.map(lambda _: VMEM_SPEC, outs),
+        out_specs=jax.tree.map(lambda _: VMEM_SPEC, outs) if out_specs is None else out_specs,
+        input_output_aliases=aliases or {},
         scratch_shapes=list(scratch),
         compiler_params=PARAMS,
         cost_estimate=pl.CostEstimate(flops=flops, bytes_accessed=10**6, transcendentals=0),
@@ -350,7 +391,6 @@
     chans = levels * fields
     hidden = w_mid.shape[0]
     tiles = lax.axis_size("tile")
-    part = cells_x // 4
     pad = -(-chans // 8) * 8
     block = state.reshape(chans, cells_x, cells_y)
     sds = jax.ShapeDtypeStruct
@@ -393,31 +433,34 @@
         ]
     )
 
-    win0 = sds((chans, EXTRA + part, cells_y), BF16)
-    win1 = sds((chans, part, cells_y), BF16)
+    quarter = cells_x // 4
+    chunks = [(n * quarter, quarter) for n in range(2)]
+    heights = [chans * (EXTRA + size) for _, size in chunks]
     tall = pltpu.VMEM((chans, cells_x + 2 * MARGIN, cells_y), F32)
-    moved, mine0, mine1, theirs0, theirs1 = call(
-        functools.partial(transport_kernel, chans=chans),
-        (sds((chans, cells_x, cells_y), F32), win0, win1, win0, win1),
+    packets = [sds((height, cells_y), BF16) for height in heights]
+    image, *windows = call(
+        functools.partial(transport_kernel, chans=chans, chunks=chunks),
+        (sds((chans, cells_x, cells_y), F32), *packets, *packets),
         [ANY_SPEC, pl.BlockSpec(memory_space=pltpu.SMEM)] + [VMEM_SPEC] * 4,
-        [
+        [pltpu.VMEM((2, height, cells_y), F32) for height in heights]
+        + [
             pltpu.VMEM((2, chans * 8, cells_y), F32),
-            pltpu.VMEM((2, chans * EXTRA, cells_y), F32),
             tall,
             tall,
             tall,
             pltpu.VMEM((2, 2, 2, chans, cells_y), F32),
             pltpu.VMEM((4 * cells_y, 2 * cells_y), BF16),
-            pltpu.SemaphoreType.DMA((1,)),
+            pltpu.SemaphoreType.DMA((1 + chans,)),
         ],
         flops=5 * 10**9,
+        out_specs=(ANY_SPEC,) + (VMEM_SPEC,) * (2 * len(chunks)),
     )(block, coef, coef.T, columns, up, down)
+    mine, theirs = windows[: len(chunks)], windows[len(chunks) :]
 
     def swap(x):
         return lax.ppermute(x, "group", [(0, 1), (1, 0)])
 
-    got0 = swap(theirs0)
-    got1 = swap(theirs1)
+    got = [swap(packet) for packet in theirs]
 
     own = lax.axis_index("group")
     both = 2 * pad
@@ -431,33 +474,41 @@
     w3 = jnp.pad(w3, ((0, 0), (0, pad - chans), (0, 0))).reshape(both, hidden)
     w2 = w_mid.T
 
-    def physics(chunk, *windows):
-        return call(
-            functools.partial(physics_kernel, chunk),
-            (win1, win1),
-            [ANY_SPEC] + [VMEM_SPEC] * (3 + 2 + 2 * chunk) + [ANY_SPEC] * chunk,
+    back = []
+    for n, (start, size) in enumerate(chunks):
+        depth = 8 * (-(-chans // 8)) * (EXTRA + size)
+        wide = pltpu.VMEM((3, 2, depth, cells_y), F32)
+        blocks = pltpu.VMEM((9 * both, min(BLOCK_ROWS, size) * cells_y), BF16)
+        image, other = call(
+            functools.partial(physics_kernel, start=start, chans=chans),
+            (image, sds((chans * size, cells_y), BF16)),
+            [ANY_SPEC] + [VMEM_SPEC] * 5 + [ANY_SPEC],
             [
-                pltpu.VMEM((2, chans * (EXTRA + part), cells_y), F32),
-                pltpu.VMEM((2, chans * part, cells_y), F32),
-                pltpu.VMEM((part + 4, both, cells_y), F32),
-                pltpu.VMEM((3, part + 2, both, cells_y), BF16),
-                pltpu.VMEM((3, part, cells_y), F32),
-                pltpu.VMEM((2, part, cells_y), jnp.int32),
-                pltpu.VMEM((9 * both, 16 * cells_y), BF16),
-                pltpu.VMEM((2, chans * part, cells_y), F32),
-                pltpu.SemaphoreType.DMA((2,)),
+                wide,
+                pltpu.VMEM((3, size + 2, both, cells_y), BF16),
+                pltpu.VMEM((3, size, cells_y), F32),
+                pltpu.VMEM((2, size, cells_y), jnp.int32),
+                blocks,
+                blocks,
+                pltpu.VMEM((2, chans * size, cells_y), F32),
+                pltpu.VMEM((chans, size, cells_y), F32),
+                pltpu.SemaphoreType.DMA((4,)),
             ],
             flops=7 * 10**9,
-        )(neighbours, w1, w2, w3, *windows)
-
-    own0, other0 = physics(0, mine0, got0)
-    back0 = swap(other0)
-    own1, other1 = physics(1, mine0, got0, mine1, got1, own0)
-    back1 = swap(other1)
-    updated = call(
-        finish_kernel, sds((chans, cells_x, cells_y), F32), [VMEM_SPEC] * 5
-    )(moved, own0, own1, back0, back1)
-    return updated.reshape(levels, fields, single, cells_x, cells_y)
+            out_specs=(ANY_SPEC, VMEM_SPEC),
+            aliases={6: 0},
+        )(neighbours, w1, w2, w3, mine[n], got[n], image)
+        back.append(swap(other))
+    for n, (start, size) in enumerate(chunks):
+        image = call(
+            functools.partial(finish_kernel, start=start),
+            image,
+            [VMEM_SPEC, ANY_SPEC],
+            [pltpu.VMEM((chans, size, cells_y), F32), pltpu.SemaphoreType.DMA((2,))],
+            out_specs=ANY_SPEC,
+            aliases={1: 0},
+        )(back[n], image)
+    return image.reshape(levels, fields, single, cells_x, cells_y)
 
 
 def solution(mesh):

time: 63.7 us -> 60.4 us (0.948); the launches traced: 62.4 us -> 60 us
  waiting for transfers between devices: 16.5 us -> 11.2 us
  Pallas kernels: 27.8 us -> 29.9 us
  local copies, waits for them, and re-layouts: 6.77 us -> 7.46 us
    ppermute x4, waiting for transfers between devices: 10.7 us -> 6.37 us  [swap(): return lax.ppermute(x, 'group', [(0, 1), (1, 0)])]
    pallas_call x4 -> x5, Pallas kernels: 23.8 us -> 25.8 us  [the longest x2 14 us: shards(): call(functools.partial(physics_kernel, start=start, chans=chans), (image,...]
    ppermute x1, waiting for transfers between devices: 3.87 us -> 3.11 us  [across(): lax.ppermute(x, 'tile', [(i, (i + by) % tiles) for i in range(tiles)])]
    unnamed x34 -> x30, local copies, waits for them, and re-layouts: 4.09 us -> 4.78 us
  transfers between devices with their start and end apart: 7 -> 7, of which waited for: 5 -> 4; matrix products, arithmetic and copies ran while one was open for 6% -> 6% of each run, Pallas kernels for 12% -> 28%
where the time goes in v4:
time: 60.4 us; the launch traced here: 60 us
  Pallas kernels  29.9 us (50%)
  waiting for transfers between devices  11.2 us (19%)
  starting transfers between devices  11 us (18%)
  local copies, waits for them, and re-layouts  7.46 us (12%)
    pallas_call x2, Pallas kernels, shards(): call(functools.partial(physics_kernel, start=start, chans=chans), (image,...  14 us
    pallas_call x1, Pallas kernels, shards(): call(functools.partial(transport_kernel, chans=chans, chunks=chunks), (sd...  6.52 us
    ppermute x4, waiting for transfers between devices, swap(): return lax.ppermute(x, 'group', [(0, 1), (1, 0)])  6.37 us
    pallas_call x2, Pallas kernels, shards(): call(functools.partial(finish_kernel, start=start), image, [VMEM_SPEC, AN...  5.31 us
    unnamed x30, local copies, waits for them, and re-layouts  4.78 us
    ppermute x1, starting transfers between devices, shards(): from_east = lax.ppermute(to_west, 'tile', beside(-1))  4.54 us
    ppermute x4, starting transfers between devices, swap(): return lax.ppermute(x, 'group', [(0, 1), (1, 0)])  4.25 us
    ppermute x1, waiting for transfers between devices, across(): lax.ppermute(x, 'tile', [(i, (i + by) % tiles) for i in range(tiles)])  3.11 us
  transfers between devices with their start and end apart: 7, of which 4 were waited for; matrix products, arithmetic and copies ran while one was open for 6% of the time, Pallas kernels for 28%

profile of v4, /device:TPU:24, one launch (start us, length us, event | category | flops | bytes accessed | tf_op | source)
XLA Modules:
  0.0 60.0 jit_solution(2523926384874238926)
XLA Ops:
  0.0 0.0 copy-start
  0.0 0.0 copy-start.5
  0.0 0.0 copy-start.6
  0.0 0.0 copy-start.4
  0.0 2.5 %shard_map.82 = (bf16[20,8,128]{2,1,0:T(8,128)(2,1)}, bf16[20,8,128]{2,1,0:T(8,128)(2,1)}, bf16[20,8,128]{2,1,0:T(8,128)(2,1)}) custom-call(f32[20,128,128]{2,1,0:T(8,128)} %bitcast.23), custom_call_target="tpu_custom_call" | custom-call | flops 1000000000 | bytes 1000000 | tf_op jit(solution)/shard_map/pallas_call | solution.py:399
  2.5 1.9 %collective-permute-start = (bf16[20,8,128]{2,1,0:T(8,128)(2,1)}, bf16[20,8,128]{2,1,0:T(8,128)(2,1)S(1)}, u32[]{:S(2)}, u32[]{:S(2)}) collective-permute-start(bf16[20,8,128]{2,1,0:T(8,128)(2,1)} %get-tuple-element.20), channel_id=1, source_target_pairs={{0,2},{2,4},{4,6},{6,8},{8,10},{10,12},{12,14},{16,18},{18,20},{20... | collective-permute-start | bytes 122888 | tf_op jit(solution)/shard_map/ppermute | solution.py:404
  4.4 4.5 %collective-permute-start.1 = (bf16[20,8,128]{2,1,0:T(8,128)(2,1)}, bf16[20,8,128]{2,1,0:T(8,128)(2,1)S(1)}, u32[]{:S(2)}, u32[]{:S(2)}) collective-permute-start(bf16[20,8,128]{2,1,0:T(8,128)(2,1)} %get-tuple-element.21), channel_id=1, source_target_pairs={{2,0},{4,2},{6,4},{8,6},{10,8},{12,10},{14,12},{18,16},{20,18},{22... | collective-permute-start | bytes 122888 | tf_op jit(solution)/shard_map/ppermute | solution.py:405
  8.9 0.0 copy-done
  9.0 0.1 reshape.175
  9.1 0.0 copy-done.5
  9.1 0.0 copy-done.6
  9.1 0.1 fusion
  9.2 0.0 copy-done.4
  9.2 0.0 collective-permute-done
  9.2 0.0 copy-start.12
  9.2 1.7 %collective-permute-done.1 = bf16[20,8,128]{2,1,0:T(8,128)(2,1)S(1)} collective-permute-done((bf16[20,8,128]{2,1,0:T(8,128)(2,1)}, bf16[20,8,128]{2,1,0:T(8,128)(2,1)S(1)}, u32[]{:S(2)}, u32[]{:S(2)}) %collective-permute-start.1) | collective-permute-done | bytes 40992 | tf_op jit(solution)/shard_map/ppermute | solution.py:405
  10.9 0.0 copy-start.13
  10.9 0.0 copy-done.12
  10.9 0.6 %copy-done.13 = bf16[20,8,128]{2,1,0:T(8,128)(2,1)} copy-done((bf16[20,8,128]{2,1,0:T(8,128)(2,1)}, bf16[20,8,128]{2,1,0:T(8,128)(2,1)S(1)}, u32[]{:S(2)}) %copy-start.13) | copy-done | bytes 40984
  11.5 0.0 copy-start.2
  11.5 0.0 copy-start.1
  11.5 1.6 %shard_map.83 = (bf16[160,128]{1,0:T(8,128)(2,1)}, f32[10,20,128]{2,1,0:T(8,128)}) custom-call(bf16[160,128]{1,0:T(8,128)(2,1)} %bitcast.29, bf16[160,128]{1,0:T(8,128)(2,1)} %bitcast.27, bf16[160,128]{1,0:T(8,128)(2,1)} %bitcast.28, bf16[160,128]{1,0:T(8,128)(2,1)} %bitcast.26, bf16[160,128]{1,0:T(8,128)(2,1)} %bitcast.25), custom_call_target="tpu_custom_call" | custom-call | flops 1000000000 | bytes 1000000 | tf_op jit(solution)/shard_map/pallas_call | solution.py:410
  13.2 0.3 collective-permute-start.2
  13.5 0.1 broadcast_subtract_fusion
  13.6 0.1 sub.70
  13.6 0.1 sub.68
  13.7 0.1 add.33
  13.8 0.1 add.31
  13.9 0.1 sub.66
  14.0 0.0 copy-start.3
  14.0 0.7 %copy.36 = f32[5,20]{0,1:T(8,128)} copy(f32[5,20]{1,0:T(8,128)S(1)} %stack.2.speed_ref) | data formatting | bytes 800 | tf_op jit(solution)/shard_map/stack | solution.py:426
  14.7 0.0 copy-done.2
  14.7 0.0 copy-done.1
  14.7 0.8 %copy.35 = bf16[256,256]{0,1:T(8,128)(2,1)} copy(bf16[256,256]{1,0:T(8,128)(2,1)S(1)} %copy-done.1) | data formatting | bytes 262144 | tf_op args[6]
  15.5 0.1 copy.40
  15.6 3.1 %collective-permute-done.2.up_ref.down_ref = bf16[160,128]{1,0:T(8,128)(2,1)S(1)} collective-permute-done((bf16[160,128]{1,0:T(8,128)(2,1)}, bf16[160,128]{1,0:T(8,128)(2,1)S(1)}, u32[]{:S(2)}, u32[]{:S(2)}) %collective-permute-start.2) | collective-permute-done | bytes 40992 | tf_op jit(solution)/shard_map/ppermute | solution.py:418
  18.7 0.0 copy-start.11
  18.7 0.0 copy-done.3
  18.7 0.6 %copy-done.11 = bf16[160,128]{1,0:T(8,128)(2,1)} copy-done((bf16[160,128]{1,0:T(8,128)(2,1)}, bf16[160,128]{1,0:T(8,128)(2,1)S(1)}, u32[]{:S(2)}) %copy-start.11) | copy-done | bytes 40984
  19.3 6.5 %shard_map.84 = (f32[20,128,128]{2,1,0:T(8,128)}, bf16[800,128]{1,0:T(8,128)(2,1)}, bf16[800,128]{1,0:T(8,128)(2,1)}, bf16[800,128]{1,0:T(8,128)(2,1)}, bf16[800,128]{1,0:T(8,128)(2,1)}) custom-call(f32[20,128,128]{2,1,0:T(8,128)} %bitcast.24, f32[5,20]{1,0:T(8,128)} %copy-done.3, f32[20,5]{1,0:T(8,128)} %bitcast.22, ...), custom_call_target="tpu_custom_call" | custom-call | flops 5000000000 | bytes 1000000 | tf_op jit(solution)/shard_map/pallas_call | solution.py:441
  25.8 1.6 %collective-permute-start.4 = (bf16[800,128]{1,0:T(8,128)(2,1)}, bf16[800,128]{1,0:T(8,128)(2,1)S(1)}, u32[]{:S(2)}, u32[]{:S(2)}) collective-permute-start(bf16[800,128]{1,0:T(8,128)(2,1)} %get-tuple-element.27), channel_id=1, source_target_pairs={{0,1},{1,0},{2,3},{3,2},{4,5},{5,4},{6,7},{7,6},{8,9},{9,8},{10,11... | collective-permute-start | bytes 614408 | tf_op jit(solution)/shard_map/ppermute | solution.py:461
  27.4 0.6 %pad.9 = bf16[2,24,256]{2,1,0:T(8,128)(2,1)} pad(bf16[2,20,256]{2,1,0:T(8,128)(2,1)S(1)} %reverse_select_fusion.1, bf16[]{:T(256)} %constant.4.clone.1), padding=0_0x0_4x0_0 | pad | bytes 45058 | tf_op jit(solution)/shard_map/jit(_pad)/pad | solution.py:474
  28.1 0.8 %copy.38.w1_ref = bf16[256,432]{1,0:T(8,128)(2,1)} copy(bf16[256,432]{0,1:T(8,128)(2,1)S(1)} %bitcast.16) | data formatting | bytes 442368 | tf_op jit(solution)/shard_map/reshape | solution.py:472
  28.9 0.5 collective-permute-start.3
  29.4 4.7 %collective-permute-done.4.got_ref = bf16[800,128]{1,0:T(8,128)(2,1)S(1)} collective-permute-done((bf16[800,128]{1,0:T(8,128)(2,1)}, bf16[800,128]{1,0:T(8,128)(2,1)S(1)}, u32[]{:S(2)}, u32[]{:S(2)}) %collective-permute-start.4) | collective-permute-done | bytes 204832 | tf_op jit(solution)/shard_map/ppermute | solution.py:461
  34.0 0.0 copy-start.8
  34.0 0.7 %copy-done.8 = bf16[800,128]{1,0:T(8,128)(2,1)} copy-done((bf16[800,128]{1,0:T(8,128)(2,1)}, bf16[800,128]{1,0:T(8,128)(2,1)S(1)}, u32[]{:S(2)}) %copy-start.8) | copy-done | bytes 204824
  34.7 7.0 %shard_map.85 = (f32[20,128,128]{2,1,0:T(8,128)}, bf16[640,128]{1,0:T(8,128)(2,1)}) custom-call(s32[9,1,128,128]{3,2,1,0:T(8,128)} %table_ref.3, bf16[256,432]{1,0:T(8,128)(2,1)} %copy.38.w1_ref, bf16[256,256]{1,0:T(8,128)(2,1)} %bitcast.17, bf16[48,256]{1,0:T(8,128)(2,1)} %bitcast.19, ...), custom_call_target="tpu_custom_call", output_to_operand_aliasing={{0}: (6, {})} | custom-call | flops 7000000000 | bytes 1000000 | tf_op jit(solution)/shard_map/pallas_call | solution.py:482
  41.7 1.6 %collective-permute-start.6 = (bf16[640,128]{1,0:T(8,128)(2,1)}, bf16[640,128]{1,0:T(8,128)(2,1)S(1)}, u32[]{:S(2)}, u32[]{:S(2)}) collective-permute-start(bf16[640,128]{1,0:T(8,128)(2,1)} %get-tuple-element.31), channel_id=1, source_target_pairs={{0,1},{1,0},{2,3},{3,2},{4,5},{5,4},{6,7},{7,6},{8,9},{9,8},{10,11... | collective-permute-start | bytes 491528 | tf_op jit(solution)/shard_map/ppermute | solution.py:461
  43.3 0.0 collective-permute-done.3.got_ref
  43.3 0.0 copy-start.7
  43.3 0.7 %copy-done.7 = bf16[800,128]{1,0:T(8,128)(2,1)} copy-done((bf16[800,128]{1,0:T(8,128)(2,1)}, bf16[800,128]{1,0:T(8,128)(2,1)S(1)}, u32[]{:S(2)}) %copy-start.7) | copy-done | bytes 204824
  44.0 7.0 %shard_map.86 = (f32[20,128,128]{2,1,0:T(8,128)}, bf16[640,128]{1,0:T(8,128)(2,1)}) custom-call(s32[9,1,128,128]{3,2,1,0:T(8,128)} %table_ref.3, bf16[256,432]{1,0:T(8,128)(2,1)} %copy.38.w1_ref, bf16[256,256]{1,0:T(8,128)(2,1)} %bitcast.18, bf16[48,256]{1,0:T(8,128)(2,1)} %bitcast.20, ...), custom_call_target="tpu_custom_call", output_to_operand_aliasing={{0}: (6, {})} | custom-call | flops 7000000000 | bytes 1000000 | tf_op jit(solution)/shard_map/pallas_call | solution.py:482
  51.0 0.5 collective-permute-start.5
  51.6 0.0 collective-permute-done.6.back_ref
  51.6 0.0 copy-start.9
  51.6 0.7 %copy-done.9 = bf16[640,128]{1,0:T(8,128)(2,1)} copy-done((bf16[640,128]{1,0:T(8,128)(2,1)}, bf16[640,128]{1,0:T(8,128)(2,1)S(1)}, u32[]{:S(2)}) %copy-start.9) | copy-done | bytes 163864
  52.3 2.7 %shard_map.87.image_in = f32[20,128,128]{2,1,0:T(8,128)} custom-call(bf16[640,128]{1,0:T(8,128)(2,1)} %copy-done.9, f32[20,128,128]{2,1,0:T(8,128)} %get-tuple-element.32.image_in), custom_call_target="tpu_custom_call", output_to_operand_aliasing={{}: (1, {})} | custom-call | flops 1000000000 | bytes 1000000 | tf_op jit(solution)/shard_map/pallas_call | solution.py:503
  54.9 1.7 %collective-permute-done.5.back_ref = bf16[640,128]{1,0:T(8,128)(2,1)S(1)} collective-permute-done((bf16[640,128]{1,0:T(8,128)(2,1)}, bf16[640,128]{1,0:T(8,128)(2,1)S(1)}, u32[]{:S(2)}, u32[]{:S(2)}) %collective-permute-start.5) | collective-permute-done | bytes 163872 | tf_op jit(solution)/shard_map/ppermute | solution.py:461
  56.6 0.0 copy-start.10
  56.6 0.7 %copy-done.10 = bf16[640,128]{1,0:T(8,128)(2,1)} copy-done((bf16[640,128]{1,0:T(8,128)(2,1)}, bf16[640,128]{1,0:T(8,128)(2,1)S(1)}, u32[]{:S(2)}) %copy-start.10) | copy-done | bytes 163864
  57.3 2.7 %shard_map.88 = f32[20,128,128]{2,1,0:T(8,128)} custom-call(bf16[640,128]{1,0:T(8,128)(2,1)} %copy-done.10, f32[20,128,128]{2,1,0:T(8,128)} %shard_map.87.image_in), custom_call_target="tpu_custom_call", output_to_operand_aliasing={{}: (1, {})} | custom-call | flops 1000000000 | bytes 1000000 | tf_op jit(solution)/shard_map/pallas_call | solution.py:503
  (6 shorter events, 0.1 us)
Async XLA Ops:
  0.0 8.9 %copy-start = (bf16[360,256]{1,0:T(8,128)(2,1)S(1)}, bf16[360,256]{1,0:T(8,128)(2,1)}, u32[]{:S(2)}) copy-start(bf16[360,256]{1,0:T(8,128)(2,1)} %param.13) | copy-start | bytes 552964
  0.0 9.1 %copy-start.5 = (f32[4]{0:T(128)S(1)}, f32[4]{0:T(128)}, u32[]{:S(2)}) copy-start(f32[4]{0:T(128)} %param.10) | copy-start | bytes 52
  0.0 9.1 %copy-start.6 = (f32[4]{0:T(128)S(1)}, f32[4]{0:T(128)}, u32[]{:S(2)}) copy-start(f32[4]{0:T(128)} %param.9) | copy-start | bytes 52
  0.0 9.1 %copy-start.4 = (f32[5]{0:T(128)S(1)}, f32[5]{0:T(128)}, u32[]{:S(2)}) copy-start(f32[5]{0:T(128)} %param.11) | copy-start | bytes 64
  2.5 6.7 %collective-permute-start = (bf16[20,8,128]{2,1,0:T(8,128)(2,1)}, bf16[20,8,128]{2,1,0:T(8,128)(2,1)S(1)}, u32[]{:S(2)}, u32[]{:S(2)}) collective-permute-start(bf16[20,8,128]{2,1,0:T(8,128)(2,1)} %get-tuple-element.20), channel_id=1, source_target_pairs={{0,2},{2,4},{4,6},{6,8},{8,10},{10,12},{12,14},{16,18},{18,20},{20... | collective-permute-start | bytes 122888 | tf_op jit(solution)/shard_map/ppermute | solution.py:404
  4.4 6.5 %collective-permute-start.1 = (bf16[20,8,128]{2,1,0:T(8,128)(2,1)}, bf16[20,8,128]{2,1,0:T(8,128)(2,1)S(1)}, u32[]{:S(2)}, u32[]{:S(2)}) collective-permute-start(bf16[20,8,128]{2,1,0:T(8,128)(2,1)} %get-tuple-element.21), channel_id=1, source_target_pairs={{2,0},{4,2},{6,4},{8,6},{10,8},{12,10},{14,12},{18,16},{20,18},{22... | collective-permute-start | bytes 122888 | tf_op jit(solution)/shard_map/ppermute | solution.py:405
  9.2 1.7 %copy-start.12 = (bf16[20,8,128]{2,1,0:T(8,128)(2,1)}, bf16[20,8,128]{2,1,0:T(8,128)(2,1)S(1)}, u32[]{:S(2)}) copy-start(bf16[20,8,128]{2,1,0:T(8,128)(2,1)S(1)} %collective-permute-done) | copy-start | bytes 122884
  10.9 0.6 %copy-start.13 = (bf16[20,8,128]{2,1,0:T(8,128)(2,1)}, bf16[20,8,128]{2,1,0:T(8,128)(2,1)S(1)}, u32[]{:S(2)}) copy-start(bf16[20,8,128]{2,1,0:T(8,128)(2,1)S(1)} %collective-permute-done.1) | copy-start | bytes 122884
  11.5 3.2 %copy-start.2 = (bf16[256,40]{0,1:T(8,128)(2,1)S(1)}, bf16[256,40]{0,1:T(8,128)(2,1)}, u32[]{:S(2)}) copy-start(bf16[256,40]{0,1:T(8,128)(2,1)} %param.15) | copy-start | bytes 61444
  11.5 3.2 %copy-start.1 = (bf16[256,256]{1,0:T(8,128)(2,1)S(1)}, bf16[256,256]{1,0:T(8,128)(2,1)}, u32[]{:S(2)}) copy-start(bf16[256,256]{1,0:T(8,128)(2,1)} %param.14) | copy-start | bytes 393220
  13.2 5.5 %collective-permute-start.2 = (bf16[160,128]{1,0:T(8,128)(2,1)}, bf16[160,128]{1,0:T(8,128)(2,1)S(1)}, u32[]{:S(2)}, u32[]{:S(2)}) collective-permute-start(bf16[160,128]{1,0:T(8,128)(2,1)} %get-tuple-element.23), channel_id=1, source_target_pairs={{0,16},{2,18},{4,20},{6,22},{8,24},{10,26},{12,28},{14,30},{16,0},... | collective-permute-start | bytes 122888 | tf_op jit(solution)/shard_map/ppermute | solution.py:418
  14.0 4.7 %copy-start.3 = (f32[5,20]{1,0:T(8,128)}, f32[5,20]{1,0:T(8,128)S(1)}, u32[]{:S(2)}) copy-start(f32[5,20]{1,0:T(8,128)S(1)} %stack.2.speed_ref) | copy-start | bytes 1204
  18.7 0.6 %copy-start.11 = (bf16[160,128]{1,0:T(8,128)(2,1)}, bf16[160,128]{1,0:T(8,128)(2,1)S(1)}, u32[]{:S(2)}) copy-start(bf16[160,128]{1,0:T(8,128)(2,1)S(1)} %collective-permute-done.2.up_ref.down_ref) | copy-start | bytes 122884
  25.8 8.2 %collective-permute-start.4 = (bf16[800,128]{1,0:T(8,128)(2,1)}, bf16[800,128]{1,0:T(8,128)(2,1)S(1)}, u32[]{:S(2)}, u32[]{:S(2)}) collective-permute-start(bf16[800,128]{1,0:T(8,128)(2,1)} %get-tuple-element.27), channel_id=1, source_target_pairs={{0,1},{1,0},{2,3},{3,2},{4,5},{5,4},{6,7},{7,6},{8,9},{9,8},{10,11... | collective-permute-start | bytes 614408 | tf_op jit(solution)/shard_map/ppermute | solution.py:461
  28.9 14.4 %collective-permute-start.3 = (bf16[800,128]{1,0:T(8,128)(2,1)}, bf16[800,128]{1,0:T(8,128)(2,1)S(1)}, u32[]{:S(2)}, u32[]{:S(2)}) collective-permute-start(bf16[800,128]{1,0:T(8,128)(2,1)} %get-tuple-element.25), channel_id=1, source_target_pairs={{0,1},{1,0},{2,3},{3,2},{4,5},{5,4},{6,7},{7,6},{8,9},{9,8},{10,11... | collective-permute-start | bytes 614408 | tf_op jit(solution)/shard_map/ppermute | solution.py:461
  34.0 0.7 %copy-start.8 = (bf16[800,128]{1,0:T(8,128)(2,1)}, bf16[800,128]{1,0:T(8,128)(2,1)S(1)}, u32[]{:S(2)}) copy-start(bf16[800,128]{1,0:T(8,128)(2,1)S(1)} %collective-permute-done.4.got_ref) | copy-start | bytes 614404
  41.7 9.9 %collective-permute-start.6 = (bf16[640,128]{1,0:T(8,128)(2,1)}, bf16[640,128]{1,0:T(8,128)(2,1)S(1)}, u32[]{:S(2)}, u32[]{:S(2)}) collective-permute-start(bf16[640,128]{1,0:T(8,128)(2,1)} %get-tuple-element.31), channel_id=1, source_target_pairs={{0,1},{1,0},{2,3},{3,2},{4,5},{5,4},{6,7},{7,6},{8,9},{9,8},{10,11... | collective-permute-start | bytes 491528 | tf_op jit(solution)/shard_map/ppermute | solution.py:461
  43.3 0.7 %copy-start.7 = (bf16[800,128]{1,0:T(8,128)(2,1)}, bf16[800,128]{1,0:T(8,128)(2,1)S(1)}, u32[]{:S(2)}) copy-start(bf16[800,128]{1,0:T(8,128)(2,1)S(1)} %collective-permute-done.3.got_ref) | copy-start | bytes 614404
  51.0 5.6 %collective-permute-start.5 = (bf16[640,128]{1,0:T(8,128)(2,1)}, bf16[640,128]{1,0:T(8,128)(2,1)S(1)}, u32[]{:S(2)}, u32[]{:S(2)}) collective-permute-start(bf16[640,128]{1,0:T(8,128)(2,1)} %get-tuple-element.30), channel_id=1, source_target_pairs={{0,1},{1,0},{2,3},{3,2},{4,5},{5,4},{6,7},{7,6},{8,9},{9,8},{10,11... | collective-permute-start | bytes 491528 | tf_op jit(solution)/shard_map/ppermute | solution.py:461
  51.6 0.7 %copy-start.9 = (bf16[640,128]{1,0:T(8,128)(2,1)}, bf16[640,128]{1,0:T(8,128)(2,1)S(1)}, u32[]{:S(2)}) copy-start(bf16[640,128]{1,0:T(8,128)(2,1)S(1)} %collective-permute-done.6.back_ref) | copy-start | bytes 491524
  56.6 0.7 %copy-start.10 = (bf16[640,128]{1,0:T(8,128)(2,1)}, bf16[640,128]{1,0:T(8,128)(2,1)S(1)}, u32[]{:S(2)}) copy-start(bf16[640,128]{1,0:T(8,128)(2,1)S(1)} %collective-permute-done.5.back_ref) | copy-start | bytes 491524

commit v5 on v4

--- a/solution.py
+++ b/solution.py
@@ -19,7 +19,6 @@
 BF16 = jnp.bfloat16
 VMEM_SPEC = pl.BlockSpec(memory_space=pltpu.VMEM)
 ANY_SPEC = pl.BlockSpec(memory_space=pl.ANY)
-PARAMS = pltpu.CompilerParams(vmem_limit_bytes=56 << 20)
 
 
 def lanes_of(shape):
@@ -75,26 +74,35 @@
 
 
 def transport_kernel(
-    state_ref, speed_ref, coef_ref, column_ref, up_ref, down_ref,
-    moved_ref, *rest, chans, chunks,
+    state_ref, speed_ref, coef_ref, column_ref, up_ref, down_ref, *rest, chans, jobs, ahead,
 ):
-    count = len(chunks)
-    mine, theirs, rest = rest[:count], rest[count : 2 * count], rest[2 * count :]
-    windows, (border, raw_s, once_s, last_s, line_s, matrix, sem) = rest[:count], rest[count:]
+    count = len(jobs)
+    moved_ref, rest = (None, rest) if ahead else (rest[0], rest[1:])
+    packets, windows, rest = rest[:count], rest[count : 2 * count], rest[2 * count :]
+    border, raw_s, once_s, last_s, line_s, matrix, up_s, down_s, sem = rest
     cells_x, width = state_ref.shape[1:]
     half = cells_x // 2
     message = up_ref.shape[0] // chans
     own = lax.axis_index("group")
     place = lax.axis_index("tile") % TILE_ROWS
+    base_of = [jnp.where(whose == 0, own, 1 - own) * half + start for whose, start, _ in jobs]
     fetch = pltpu.make_async_copy(state_ref, raw_s.at[:, pl.ds(MARGIN, cells_x)], sem.at[0])
+    halo = [
+        pltpu.make_async_copy(up_ref, up_s, sem.at[1]),
+        pltpu.make_async_copy(down_ref, down_s, sem.at[2]),
+    ]
+    for copy in halo:
+        copy.start()
     fetch.start()
+    matrix[...] = shift_matrix(width)
+    for copy in halo:
+        copy.wait()
     lane = lanes_of((chans, width))
     first, last = lane == 0, lane == width - 1
     low_lanes = lane < width // 2
-    for s, ref in enumerate((up_ref, down_ref)):
+    for s, ref in enumerate((up_s, down_s)):
         border[s] = ref[...].astype(F32)
     coefs = [jnp.broadcast_to(coef_ref[:, n : n + 1], (chans, width)) for n in range(5)]
-    matrix[...] = shift_matrix(width)
 
     above, below = [border[s, pl.ds(2 * DEEP, chans, stride=message), :] for s in range(2)]
     corners = jnp.where(lane % (2 * DEEP) < DEEP, above, below)
@@ -138,44 +146,38 @@
             for n in range(2):
                 line_s[level, side, n] = edge[n]
         edges.append((main, aux))
-    for q in range(2):
-        for window, (start, size) in zip(windows, chunks):
-            at = q * half + start - 1
-            sides = []
-            for side, first_lane in enumerate((0, width // 2)):
-                main, aux = edges[side]
-                by = (first_lane - at) % width
-                row_of = lane - first_lane + at
-                off = (row_of < 0) | (row_of >= cells_x)
-                sides.append(jnp.where(off, roll(aux, by), roll(main, by)))
-            window[q, pl.ds(2, chans, stride=EXTRA + size), :] = jnp.where(low_lanes, *sides)
-
-    rows = cells_x + 16
-    at = lax.broadcasted_iota(jnp.int32, (rows, width), 0) - 8
-    diagonal = (at + width) % width == lanes_of((rows, width))
+    for window, base, (_, _, size) in zip(windows, base_of, jobs):
+        at = base - 1
+        sides = []
+        for side, first_lane in enumerate((0, width // 2)):
+            main, aux = edges[side]
+            by = lax.rem(first_lane - at + width, width)
+            row_of = lane - first_lane + at
+            off = (row_of < 0) | (row_of >= cells_x)
+            sides.append(jnp.where(off, roll(aux, by), roll(main, by)))
+        window[pl.ds(2, chans, stride=EXTRA + size), :] = jnp.where(low_lanes, *sides)
+
+    rows = jobs[0][2] + 16 if ahead else cells_x + 16
+    origin = base_of[0] - 8 if ahead else -8
+    top = pl.multiple_of(origin + MARGIN, 8) if ahead else 8
+    at = lax.broadcasted_iota(jnp.int32, (rows, width), 0) + origin
+    diagonal = lax.rem(at + width, width) == lanes_of((rows, width))
+    within = (at >= 0) & (at < cells_x)
     fetch.wait()
-
-    group = next(n for n in (GROUP, 2, 1) if chans % n == 0)
+    group = next(n for n in (10 if ahead else GROUP, 2, 1) if chans % n == 0)
 
     def sweep(level, src, dst, base):
         parts = []
         for g in range(group):
             c = base + g
-            q = src[c, pl.ds(8, rows), :]
+            q = src[c, pl.ds(top, rows), :]
             hi = q.astype(BF16)
             lo = (q - hi.astype(F32)).astype(BF16)
             sides = []
             for side in range(2):
                 main = line_s[level, side, 0, pl.ds(c, 1), :]
                 aux = line_s[level, side, 1, pl.ds(c, 1), :]
-                values = jnp.concatenate(
-                    [
-                        jnp.broadcast_to(aux, (8, width)),
-                        jnp.broadcast_to(main, (cells_x, width)),
-                        jnp.broadcast_to(aux, (8, width)),
-                    ],
-                    axis=0,
-                )
+                values = jnp.where(within, main, aux)
                 sides.append(jnp.where(diagonal, values, 0.0).astype(BF16))
             parts.append(jnp.concatenate([hi, lo] + sides, axis=1))
         near = lax.dot_general(
@@ -188,10 +190,10 @@
             c = base + g
             lower, upper = near[g * rows : (g + 1) * rows, :width], near[g * rows : (g + 1) * rows, width:]
             c0, cxl, cxu, cyl, cyu = [speed_ref[n, c] for n in range(5)]
-            dst[c, pl.ds(8, rows), :] = (
-                c0 * src[c, pl.ds(8, rows), :]
-                + cxl * src[c, pl.ds(7, rows), :]
-                + cxu * src[c, pl.ds(9, rows), :]
+            dst[c, pl.ds(top, rows), :] = (
+                c0 * src[c, pl.ds(top, rows), :]
+                + cxl * src[c, pl.ds(top - 1, rows), :]
+                + cxu * src[c, pl.ds(top + 1, rows), :]
                 + cyl * lower
                 + cyu * upper
             )
@@ -201,21 +203,21 @@
     def finish(base):
         for g in range(group):
             c = base + g
-            for q in range(2):
-                for window, (start, size) in zip(windows, chunks):
-                    at = MARGIN + q * half + start
-                    to = c * (EXTRA + size)
-                    window[q, pl.ds(to, 1), :] = last_s[c, pl.ds(at - 1, 1), :]
-                    window[q, pl.ds(to + 1, 1), :] = last_s[c, pl.ds(at + size, 1), :]
-                    window[q, pl.ds(to + EXTRA, size), :] = last_s[c, pl.ds(at, size), :]
-        outs.append(
-            pltpu.make_async_copy(
-                last_s.at[pl.ds(base, group), pl.ds(MARGIN, cells_x)],
-                moved_ref.at[pl.ds(base, group)],
-                sem.at[1 + base // group],
+            for window, row, (_, _, size) in zip(windows, base_of, jobs):
+                at = MARGIN + row
+                to = c * (EXTRA + size)
+                window[pl.ds(to, 1), :] = last_s[c, pl.ds(at - 1, 1), :]
+                window[pl.ds(to + 1, 1), :] = last_s[c, pl.ds(at + size, 1), :]
+                window[pl.ds(to + EXTRA, size), :] = last_s[c, pl.ds(pl.multiple_of(at, 8), size), :]
+        if not ahead:
+            outs.append(
+                pltpu.make_async_copy(
+                    last_s.at[pl.ds(base, group), pl.ds(MARGIN, cells_x)],
+                    moved_ref.at[pl.ds(base, group)],
+                    sem.at[3 + base // group],
+                )
             )
-        )
-        outs[-1].start()
+            outs[-1].start()
 
     for c in range(chans):
         raw_s[c, pl.ds(MARGIN - DEEP, DEEP), :] = border[0, pl.ds(c * message + DEEP, DEEP), :]
@@ -226,16 +228,15 @@
         if base:
             sweep(1, once_s, last_s, base - group)
             finish(base - group)
-    for n in range(count):
-        mine[n][...] = windows[n][own].astype(BF16)
-        theirs[n][...] = windows[n][1 - own].astype(BF16)
+    for packet, window in zip(packets, windows):
+        packet[...] = window[...].astype(BF16)
     for copy in outs:
         copy.wait()
 
 
 def physics_kernel(
     table_ref, w1_ref, w2_ref, w3_ref, mine_ref, got_ref, image_in,
-    image_ref, other_ref, wide, packed, mask, table, even, odd, terms, patch, sem, *, start, chans,
+    image_ref, other_ref, wide, packed, mask, table, even, odd, terms, patch, got, sem, *, start, chans,
 ):
     size, width = table.shape[1:]
     cells_x = image_in.shape[1]
@@ -249,8 +250,10 @@
         for n, k in enumerate((5, 7))
     ]
     fetch = pltpu.make_async_copy(image_in.at[:, pl.ds(top, size)], patch, sem.at[2])
+    arrive = pltpu.make_async_copy(got_ref, got, sem.at[4])
     for copy in copies:
         copy.start()
+    arrive.start()
     fetch.start()
 
     k = lax.broadcasted_iota(jnp.int32, (2 * width, 2 * width), 0)
@@ -264,7 +267,9 @@
         slot >= EXTRA, slot - EXTRA + 1, jnp.where(slot == 0, 0, jnp.where(slot == 1, size + 1, -1))
     )
     diagonal = lanes_of((height, width)) % (width // 2) == line
-    for s, ref in enumerate((mine_ref, got_ref)):
+    for s, ref in enumerate((mine_ref, got)):
+        if s == 1:
+            arrive.wait()
         cells = ref[...]
         flat = cells.astype(F32)
         wide[1, s, pl.ds(0, chans * height)] = flat
@@ -332,8 +337,7 @@
     )
 
     def silu(v):
-        h = v * 0.5
-        return (h * jnp.tanh(h) + h).astype(BF16)
+        return (v * jnp.tanh(v) + v).astype(BF16)
 
     def network(n, src):
         first = silu(dot(w1_ref[...], src[...]))
@@ -360,20 +364,36 @@
     put.wait()
 
 
-def finish_kernel(back_ref, image_in, image_ref, patch, sem, *, start):
-    size = patch.shape[1]
+def finish_kernel(back_ref, image_in, image_ref, patch, back, sem, *, start, parts):
+    chans, size, width = patch.shape
     half = image_in.shape[1] // 2
     rows = pl.ds((1 - lax.axis_index("group")) * half + start, size)
-    fetch = pltpu.make_async_copy(image_in.at[:, rows], patch, sem.at[0])
-    fetch.start()
-    fetch.wait()
-    patch[...] = patch[...] + back_ref[...].astype(F32).reshape(patch.shape)
-    put = pltpu.make_async_copy(patch, image_ref.at[:, rows], sem.at[1])
-    put.start()
-    put.wait()
-
-
-def call(kernel, outs, ins, scratch=(), flops=10**9, out_specs=None, aliases=None):
+    some = chans // parts
+    fetch = []
+    for n in range(parts):
+        c, r = pl.ds(n * some, some), pl.ds(n * some * size, some * size)
+        fetch.append(
+            (
+                pltpu.make_async_copy(back_ref.at[r], back.at[r], sem.at[n]),
+                pltpu.make_async_copy(image_in.at[c, rows], patch.at[c], sem.at[parts + n]),
+            )
+        )
+        for copy in fetch[-1]:
+            copy.start()
+    put = []
+    for n in range(parts):
+        for copy in fetch[n]:
+            copy.wait()
+        c = pl.ds(n * some, some)
+        terms = back[pl.ds(n * some * size, some * size)].astype(F32)
+        patch[c] = patch[c] + terms.reshape(some, size, width)
+        put.append(pltpu.make_async_copy(patch.at[c], image_ref.at[c, rows], sem.at[2 * parts + n]))
+        put[-1].start()
+    for copy in put:
+        copy.wait()
+
+
+def call(kernel, outs, ins, scratch=(), flops=10**9, out_specs=None, aliases=None, limit=24):
     return pl.pallas_call(
         kernel,
         out_shape=jax.tree.map(lambda x: jax.ShapeDtypeStruct(x.shape, x.dtype), outs),
@@ -381,7 +401,7 @@
         out_specs=jax.tree.map(lambda _: VMEM_SPEC, outs) if out_specs is None else out_specs,
         input_output_aliases=aliases or {},
         scratch_shapes=list(scratch),
-        compiler_params=PARAMS,
+        compiler_params=pltpu.CompilerParams(vmem_limit_bytes=limit << 20),
         cost_estimate=pl.CostEstimate(flops=flops, bytes_accessed=10**6, transcendentals=0),
     )
 
@@ -435,32 +455,42 @@
 
     quarter = cells_x // 4
     chunks = [(n * quarter, quarter) for n in range(2)]
-    heights = [chans * (EXTRA + size) for _, size in chunks]
     tall = pltpu.VMEM((chans, cells_x + 2 * MARGIN, cells_y), F32)
-    packets = [sds((height, cells_y), BF16) for height in heights]
-    image, *windows = call(
-        functools.partial(transport_kernel, chans=chans, chunks=chunks),
-        (sds((chans, cells_x, cells_y), F32), *packets, *packets),
-        [ANY_SPEC, pl.BlockSpec(memory_space=pltpu.SMEM)] + [VMEM_SPEC] * 4,
-        [pltpu.VMEM((2, height, cells_y), F32) for height in heights]
-        + [
-            pltpu.VMEM((2, chans * 8, cells_y), F32),
-            tall,
-            tall,
-            tall,
-            pltpu.VMEM((2, 2, 2, chans, cells_y), F32),
-            pltpu.VMEM((4 * cells_y, 2 * cells_y), BF16),
-            pltpu.SemaphoreType.DMA((1 + chans,)),
-        ],
-        flops=5 * 10**9,
-        out_specs=(ANY_SPEC,) + (VMEM_SPEC,) * (2 * len(chunks)),
-    )(block, coef, coef.T, columns, up, down)
-    mine, theirs = windows[: len(chunks)], windows[len(chunks) :]
+
+    def transport(jobs, ahead):
+        heights = [chans * (EXTRA + size) for _, _, size in jobs]
+        packets = [sds((height, cells_y), BF16) for height in heights]
+        moved = () if ahead else (sds((chans, cells_x, cells_y), F32),)
+        return call(
+            functools.partial(transport_kernel, chans=chans, jobs=jobs, ahead=ahead),
+            (*moved, *packets),
+            [ANY_SPEC, pl.BlockSpec(memory_space=pltpu.SMEM)] + [VMEM_SPEC] * 2 + [ANY_SPEC] * 2,
+            [pltpu.VMEM((height, cells_y), F32) for height in heights]
+            + [
+                pltpu.VMEM((2, chans * 8, cells_y), F32),
+                tall,
+                tall,
+                tall,
+                pltpu.VMEM((2, 2, 2, chans, cells_y), F32),
+                pltpu.VMEM((4 * cells_y, 2 * cells_y), BF16),
+                pltpu.VMEM(up.shape, BF16),
+                pltpu.VMEM(up.shape, BF16),
+                pltpu.SemaphoreType.DMA((3 + chans,)),
+            ],
+            flops=5 * 10**9,
+            out_specs=(ANY_SPEC,) * len(moved) + (VMEM_SPEC,) * len(jobs),
+        )(block, coef, coef.T, columns, up, down)
 
     def swap(x):
         return lax.ppermute(x, "group", [(0, 1), (1, 0)])
 
-    got = [swap(packet) for packet in theirs]
+    (packet,) = transport([(1, *chunks[0])], True)
+    got = [swap(packet)]
+    image, *packets = transport(
+        [(1, *chunk) for chunk in chunks[1:]] + [(0, *chunk) for chunk in chunks], False
+    )
+    theirs, mine = packets[: len(chunks) - 1], packets[len(chunks) - 1 :]
+    got += [swap(packet) for packet in theirs]
 
     own = lax.axis_index("group")
     both = 2 * pad
@@ -468,12 +498,13 @@
     def ordered(w):
         return jnp.where(own == 0, w, w[::-1])
 
-    w1 = ordered(w_in.reshape(2, chans, 9, hidden)).transpose(3, 2, 0, 1)
+    w1 = ordered((w_in * 0.5).reshape(2, chans, 9, hidden)).transpose(3, 2, 0, 1)
     w1 = jnp.pad(w1, ((0, 0), (0, 0), (0, 0), (0, pad - chans))).reshape(hidden, 9 * both)
     w3 = ordered(w_out.T.reshape(2, chans, hidden))
     w3 = jnp.pad(w3, ((0, 0), (0, pad - chans), (0, 0))).reshape(both, hidden)
-    w2 = w_mid.T
-
+    w2 = (w_mid * 0.5).T
+
+    parts = 4 if chans % 4 == 0 else 1
     back = []
     for n, (start, size) in enumerate(chunks):
         depth = 8 * (-(-chans // 8)) * (EXTRA + size)
@@ -482,7 +513,7 @@
         image, other = call(
             functools.partial(physics_kernel, start=start, chans=chans),
             (image, sds((chans * size, cells_y), BF16)),
-            [ANY_SPEC] + [VMEM_SPEC] * 5 + [ANY_SPEC],
+            [ANY_SPEC] + [VMEM_SPEC] * 4 + [ANY_SPEC] * 2,
             [
                 wide,
                 pltpu.VMEM((3, size + 2, both, cells_y), BF16),
@@ -492,7 +523,8 @@
                 blocks,
                 pltpu.VMEM((2, chans * size, cells_y), F32),
                 pltpu.VMEM((chans, size, cells_y), F32),
-                pltpu.SemaphoreType.DMA((4,)),
+                pltpu.VMEM((chans * (EXTRA + size), cells_y), BF16),
+                pltpu.SemaphoreType.DMA((5,)),
             ],
             flops=7 * 10**9,
             out_specs=(ANY_SPEC, VMEM_SPEC),
@@ -501,12 +533,17 @@
         back.append(swap(other))
     for n, (start, size) in enumerate(chunks):
         image = call(
-            functools.partial(finish_kernel, start=start),
+            functools.partial(finish_kernel, start=start, parts=parts),
             image,
-            [VMEM_SPEC, ANY_SPEC],
-            [pltpu.VMEM((chans, size, cells_y), F32), pltpu.SemaphoreType.DMA((2,))],
+            [ANY_SPEC, ANY_SPEC],
+            [
+                pltpu.VMEM((chans, size, cells_y), F32),
+                pltpu.VMEM((chans * size, cells_y), BF16),
+                pltpu.SemaphoreType.DMA((3 * parts,)),
+            ],
             out_specs=ANY_SPEC,
             aliases={1: 0},
+            limit=4,
         )(back[n], image)
     return image.reshape(levels, fields, single, cells_x, cells_y)
 

time: 60.4 us -> 44.4 us (0.74)
  Pallas kernels: 29.9 us -> 21.1 us
  local copies, waits for them, and re-layouts: 7.46 us -> 2.32 us
  waiting for transfers between devices: 11.2 us -> 8.8 us
    pallas_call x2, Pallas kernels: 14 us -> 9.98 us  [shards(): call(functools.partial(physics_kernel, start=start, chans=chans), (image,...]
    unnamed x30 -> x20, local copies, waits for them, and re-layouts: 4.78 us -> 1.53 us
    ppermute x4, waiting for transfers between devices: 6.37 us -> 3.4 us  [swap(): return lax.ppermute(x, 'group', [(0, 1), (1, 0)])]
    pallas_call x1, Pallas kernels: 2.46 us -> 0.43 us  [shards(): call(edge_kernel, (strip, strip, strip), [VMEM_SPEC])(block)]
    pallas_call x1, Pallas kernels: 1.63 us -> 0.13 us  [shards(): call(functools.partial(pack_kernel, chans=chans), (sds((chans * 8, cells_...]
    pallas_call x3 -> x4, Pallas kernels: 11.8 us -> 10.6 us  [the longest x2 6.86 us: transport(): call(functools.partial(transport_kernel, chans=chans, jobs=jobs, ahead=ah...]
    ppermute x1, waiting for transfers between devices: 3.11 us -> 4.2 us  [across(): lax.ppermute(x, 'tile', [(i, (i + by) % tiles) for i in range(tiles)])]
    reshape x1, local copies, waits for them, and re-layouts: 0.84 us -> 0.14 us  [shards(): jnp.pad(w1, ((0, 0), (0, 0), (0, 0), (0, pad - chans)))]
  transfers between devices with their start and end apart: 7 -> 7, of which waited for: 4 -> 4; matrix products, arithmetic and copies ran while one was open for 6% -> 3% of each run, Pallas kernels for 28% -> 37%
where the time goes in v5:
time: 44.4 us; the launch traced here: 44 us
  Pallas kernels  21.1 us (48%)
  starting transfers between devices  11.3 us (25%)
  waiting for transfers between devices  8.8 us (20%)
  local copies, waits for them, and re-layouts  2.32 us (5%)
    pallas_call x2, Pallas kernels, shards(): call(functools.partial(physics_kernel, start=start, chans=chans), (image,...  9.98 us
    pallas_call x2, Pallas kernels, transport(): call(functools.partial(transport_kernel, chans=chans, jobs=jobs, ahead=ah...  6.86 us
    ppermute x1, starting transfers between devices, shards(): from_east = lax.ppermute(to_west, 'tile', beside(-1))  4.54 us
    ppermute x4, starting transfers between devices, swap(): return lax.ppermute(x, 'group', [(0, 1), (1, 0)])  4.32 us
    ppermute x1, waiting for transfers between devices, across(): lax.ppermute(x, 'tile', [(i, (i + by) % tiles) for i in range(tiles)])  4.2 us
    pallas_call x2, Pallas kernels, shards(): call(functools.partial(finish_kernel, start=start, parts=parts), image, [...  3.7 us
    ppermute x4, waiting for transfers between devices, swap(): return lax.ppermute(x, 'group', [(0, 1), (1, 0)])  3.4 us
    ppermute x1, starting transfers between devices, shards(): from_west = lax.ppermute(to_east, 'tile', beside(1))  2.05 us
  transfers between devices with their start and end apart: 7, of which 4 were waited for; matrix products, arithmetic and copies ran while one was open for 3% of the time, Pallas kernels for 37%

profile of v5, /device:TPU:24, one launch (start us, length us, event | category | flops | bytes accessed | tf_op | source)
XLA Modules:
  0.0 44.0 jit_solution(2648011385375869608)
XLA Ops:
  0.0 0.0 copy-start
  0.0 1.3 %copy-done = f32[4,5,1,128,128]{4,3,2,1,0:T(8,128)S(1)} copy-done((f32[4,5,1,128,128]{4,3,2,1,0:T(8,128)S(1)}, f32[4,5,1,128,128]{4,3,2,1,0:T(8,128)}, u32[]{:S(2)}) %copy-start) | copy-done | bytes 1310744
  1.3 0.0 copy-start.5
  1.3 0.0 copy-start.4
  1.3 0.0 copy-start.3
  1.3 0.4 shard_map.82
  1.8 0.0 copy-start.7
  1.8 0.0 copy-start.8
  1.8 0.0 copy-start.6
  1.8 2.1 %collective-permute-start = (bf16[20,8,128]{2,1,0:T(8,128)(2,1)S(1)}, bf16[20,8,128]{2,1,0:T(8,128)(2,1)S(1)}, u32[]{:S(2)}, u32[]{:S(2)}) collective-permute-start(bf16[20,8,128]{2,1,0:T(8,128)(2,1)S(1)} %get-tuple-element.19), channel_id=1, source_target_pairs={{0,2},{2,4},{4,6},{6,8},{8,10},{10,12},{12,14},{16,18},{18,20},{20... | collective-permute-start | bytes 122888 | tf_op jit(solution)/shard_map/ppermute | solution.py:424
  3.9 4.5 %collective-permute-start.1 = (bf16[20,8,128]{2,1,0:T(8,128)(2,1)S(1)}, bf16[20,8,128]{2,1,0:T(8,128)(2,1)S(1)}, u32[]{:S(2)}, u32[]{:S(2)}) collective-permute-start(bf16[20,8,128]{2,1,0:T(8,128)(2,1)S(1)} %get-tuple-element.20), channel_id=1, source_target_pairs={{2,0},{4,2},{6,4},{8,6},{10,8},{12,10},{14,12},{18,16},{20,18},{22... | collective-permute-start | bytes 122888 | tf_op jit(solution)/shard_map/ppermute | solution.py:425
  8.4 0.0 copy-done.5
  8.4 0.0 copy-done.4
  8.4 0.1 copy.37
  8.6 0.0 copy-done.3
  8.6 0.1 reshape.175
  8.7 0.1 fusion
  8.8 0.0 copy-done.7
  8.8 0.0 copy-done.8
  8.8 0.0 copy-done.6
  8.8 0.0 collective-permute-done
  8.9 1.2 %collective-permute-done.1 = bf16[20,8,128]{2,1,0:T(8,128)(2,1)S(1)} collective-permute-done((bf16[20,8,128]{2,1,0:T(8,128)(2,1)S(1)}, bf16[20,8,128]{2,1,0:T(8,128)(2,1)S(1)}, u32[]{:S(2)}, u32[]{:S(2)}) %collective-permute-start.1) | collective-permute-done | bytes 40992 | tf_op jit(solution)/shard_map/ppermute | solution.py:425
  10.1 0.1 shard_map.83
  10.2 0.0 copy-start.1
  10.2 0.4 collective-permute-start.2
  10.6 0.1 broadcast_subtract_fusion
  10.7 0.1 sub.70
  10.8 0.1 sub.68
  10.8 0.1 add.33
  10.9 0.1 add.31
  11.0 0.1 sub.66
  11.1 0.1 copy.38
  11.2 0.1 copy.42
  11.3 0.1 copy.40.w1_ref
  11.5 4.2 %collective-permute-done.2.up_ref.down_ref = bf16[160,128]{1,0:T(8,128)(2,1)S(1)} collective-permute-done((bf16[160,128]{1,0:T(8,128)(2,1)S(1)}, bf16[160,128]{1,0:T(8,128)(2,1)S(1)}, u32[]{:S(2)}, u32[]{:S(2)}) %collective-permute-start.2) | collective-permute-done | bytes 40992 | tf_op jit(solution)/shard_map/ppermute | solution.py:438
  15.7 0.0 copy-done.1
  15.7 2.3 %shard_map.85 = bf16[800,128]{1,0:T(8,128)(2,1)S(1)} custom-call(f32[20,128,128]{2,1,0:T(8,128)S(1)} %bitcast.22, f32[5,20]{1,0:T(8,128)S(1)} %stack.2.speed_ref, f32[20,5]{1,0:T(8,128)S(1)} %bitcast.19, f32[10,20,128]{2,1,0:T(8,128)S(1)} %get-tuple-element.21.column_ref, bf16[160,128]{1,0:T(8,128)(2,1)S(1)} %collective-permute-done.2.up_ref.down_ref, ...), custom_call_target="tpu_custom_call" | custom-call | flops 5000000000 | bytes 1000000 | tf_op jit(solution)/shard_map/pallas_call | solution.py:464
  18.0 0.0 copy-start.2
  18.0 1.6 %collective-permute-start.4 = (bf16[800,128]{1,0:T(8,128)(2,1)S(1)}, bf16[800,128]{1,0:T(8,128)(2,1)S(1)}, u32[]{:S(2)}, u32[]{:S(2)}) collective-permute-start(bf16[800,128]{1,0:T(8,128)(2,1)S(1)} %shard_map.85), channel_id=1, source_target_pairs={{0,1},{1,0},{2,3},{3,2},{4,5},{5,4},{6,7},{7,6},{8,9},{9,8},{10,11... | collective-permute-start | bytes 614408 | tf_op jit(solution)/shard_map/ppermute | solution.py:485
  19.6 4.5 %shard_map.84 = (f32[20,128,128]{2,1,0:T(8,128)}, bf16[800,128]{1,0:T(8,128)(2,1)S(1)}, bf16[800,128]{1,0:T(8,128)(2,1)S(1)}, bf16[800,128]{1,0:T(8,128)(2,1)S(1)}) custom-call(f32[20,128,128]{2,1,0:T(8,128)S(1)} %bitcast.23, f32[5,20]{1,0:T(8,128)S(1)} %stack.2.speed_ref, f32[20,5]{1,0:T(8,128)S(1)} %bitcast.20, ...), custom_call_target="tpu_custom_call" | custom-call | flops 5000000000 | bytes 1000000 | tf_op jit(solution)/shard_map/pallas_call | solution.py:464
  24.1 0.6 %collective-permute-start.3 = (bf16[800,128]{1,0:T(8,128)(2,1)S(1)}, bf16[800,128]{1,0:T(8,128)(2,1)S(1)}, u32[]{:S(2)}, u32[]{:S(2)}) collective-permute-start(bf16[800,128]{1,0:T(8,128)(2,1)S(1)} %get-tuple-element.24), channel_id=1, source_target_pairs={{0,1},{1,0},{2,3},{3,2},{4,5},{5,4},{6,7},{7,6},{8,9},{9,8},{10,11... | collective-permute-start | bytes 614408 | tf_op jit(solution)/shard_map/ppermute | solution.py:485
  24.7 0.4 %collective-permute-done.4.got_ref = bf16[800,128]{1,0:T(8,128)(2,1)S(1)} collective-permute-done((bf16[800,128]{1,0:T(8,128)(2,1)S(1)}, bf16[800,128]{1,0:T(8,128)(2,1)S(1)}, u32[]{:S(2)}, u32[]{:S(2)}) %collective-permute-start.4) | collective-permute-done | bytes 204832 | tf_op jit(solution)/shard_map/ppermute | solution.py:485
  25.2 0.0 copy-done.2
  25.2 5.0 %shard_map.86 = (f32[20,128,128]{2,1,0:T(8,128)}, bf16[640,128]{1,0:T(8,128)(2,1)S(1)}) custom-call(s32[9,1,128,128]{3,2,1,0:T(8,128)S(1)} %copy-done.2, bf16[256,432]{1,0:T(8,128)(2,1)S(1)} %copy.40.w1_ref, bf16[256,256]{1,0:T(8,128)(2,1)S(1)} %multiply_bitcast_fusion.w2_ref, bf16[48,256]{1,0:T(8,128)(2,1)S(1)} %bitcast.17, ...), custom_call_target="tpu_custom_call", output_to_operand_aliasing={{0}: (6, {})} | custom-call | flops 7000000000 | bytes 1000000 | tf_op jit(solution)/shard_map/pallas_call | solution.py:513
  30.2 1.6 %collective-permute-start.6 = (bf16[640,128]{1,0:T(8,128)(2,1)S(1)}, bf16[640,128]{1,0:T(8,128)(2,1)S(1)}, u32[]{:S(2)}, u32[]{:S(2)}) collective-permute-start(bf16[640,128]{1,0:T(8,128)(2,1)S(1)} %get-tuple-element.29), channel_id=1, source_target_pairs={{0,1},{1,0},{2,3},{3,2},{4,5},{5,4},{6,7},{7,6},{8,9},{9,8},{10,11... | collective-permute-start | bytes 491528 | tf_op jit(solution)/shard_map/ppermute | solution.py:485
  31.8 0.0 collective-permute-done.3.got_ref
  31.8 5.0 %shard_map.87 = (f32[20,128,128]{2,1,0:T(8,128)}, bf16[640,128]{1,0:T(8,128)(2,1)S(1)}) custom-call(s32[9,1,128,128]{3,2,1,0:T(8,128)S(1)} %copy-done.2, bf16[256,432]{1,0:T(8,128)(2,1)S(1)} %copy.40.w1_ref, bf16[256,256]{1,0:T(8,128)(2,1)S(1)} %multiply_bitcast_fusion.w2_ref, bf16[48,256]{1,0:T(8,128)(2,1)S(1)} %bitcast.18, ...), custom_call_target="tpu_custom_call", output_to_operand_aliasing={{0}: (6, {})} | custom-call | flops 7000000000 | bytes 1000000 | tf_op jit(solution)/shard_map/pallas_call | solution.py:513
  36.8 0.6 %collective-permute-start.5 = (bf16[640,128]{1,0:T(8,128)(2,1)S(1)}, bf16[640,128]{1,0:T(8,128)(2,1)S(1)}, u32[]{:S(2)}, u32[]{:S(2)}) collective-permute-start(bf16[640,128]{1,0:T(8,128)(2,1)S(1)} %get-tuple-element.28), channel_id=1, source_target_pairs={{0,1},{1,0},{2,3},{3,2},{4,5},{5,4},{6,7},{7,6},{8,9},{9,8},{10,11... | collective-permute-start | bytes 491528 | tf_op jit(solution)/shard_map/ppermute | solution.py:485
  37.3 0.0 collective-permute-done.6.back_ref
  37.3 1.9 %shard_map.88.image_in = f32[20,128,128]{2,1,0:T(8,128)} custom-call(bf16[640,128]{1,0:T(8,128)(2,1)S(1)} %collective-permute-done.6.back_ref, f32[20,128,128]{2,1,0:T(8,128)} %get-tuple-element.30.image_in), custom_call_target="tpu_custom_call", output_to_operand_aliasing={{}: (1, {})} | custom-call | flops 1000000000 | bytes 1000000 | tf_op jit(solution)/shard_map/pallas_call | solution.py:535
  39.2 2.9 %collective-permute-done.5.back_ref = bf16[640,128]{1,0:T(8,128)(2,1)S(1)} collective-permute-done((bf16[640,128]{1,0:T(8,128)(2,1)S(1)}, bf16[640,128]{1,0:T(8,128)(2,1)S(1)}, u32[]{:S(2)}, u32[]{:S(2)}) %collective-permute-start.5) | collective-permute-done | bytes 163872 | tf_op jit(solution)/shard_map/ppermute | solution.py:485
  42.1 1.8 %shard_map.89 = f32[20,128,128]{2,1,0:T(8,128)} custom-call(bf16[640,128]{1,0:T(8,128)(2,1)S(1)} %collective-permute-done.5.back_ref, f32[20,128,128]{2,1,0:T(8,128)} %shard_map.88.image_in), custom_call_target="tpu_custom_call", output_to_operand_aliasing={{}: (1, {})} | custom-call | flops 1000000000 | bytes 1000000 | tf_op jit(solution)/shard_map/pallas_call | solution.py:535
  (9 shorter events, 0.1 us)
Async XLA Ops:
  0.0 1.3 %copy-start = (f32[4,5,1,128,128]{4,3,2,1,0:T(8,128)S(1)}, f32[4,5,1,128,128]{4,3,2,1,0:T(8,128)}, u32[]{:S(2)}) copy-start(f32[4,5,1,128,128]{4,3,2,1,0:T(8,128)} %param.8) | copy-start | bytes 3932164
  1.3 7.1 %copy-start.5 = (bf16[256,40]{0,1:T(8,128)(2,1)S(1)}, bf16[256,40]{0,1:T(8,128)(2,1)}, u32[]{:S(2)}) copy-start(bf16[256,40]{0,1:T(8,128)(2,1)} %param.15) | copy-start | bytes 61444
  1.3 7.1 %copy-start.4 = (bf16[256,256]{1,0:T(8,128)(2,1)S(1)}, bf16[256,256]{1,0:T(8,128)(2,1)}, u32[]{:S(2)}) copy-start(bf16[256,256]{1,0:T(8,128)(2,1)} %param.14) | copy-start | bytes 393220
  1.3 7.3 %copy-start.3 = (bf16[360,256]{1,0:T(8,128)(2,1)S(1)}, bf16[360,256]{1,0:T(8,128)(2,1)}, u32[]{:S(2)}) copy-start(bf16[360,256]{1,0:T(8,128)(2,1)} %param.13) | copy-start | bytes 552964
  1.8 7.0 %copy-start.7 = (f32[4]{0:T(128)S(1)}, f32[4]{0:T(128)}, u32[]{:S(2)}) copy-start(f32[4]{0:T(128)} %param.10) | copy-start | bytes 52
  1.8 7.0 %copy-start.8 = (f32[4]{0:T(128)S(1)}, f32[4]{0:T(128)}, u32[]{:S(2)}) copy-start(f32[4]{0:T(128)} %param.9) | copy-start | bytes 52
  1.8 7.1 %copy-start.6 = (f32[5]{0:T(128)S(1)}, f32[5]{0:T(128)}, u32[]{:S(2)}) copy-start(f32[5]{0:T(128)} %param.11) | copy-start | bytes 64
  1.8 7.1 %collective-permute-start = (bf16[20,8,128]{2,1,0:T(8,128)(2,1)S(1)}, bf16[20,8,128]{2,1,0:T(8,128)(2,1)S(1)}, u32[]{:S(2)}, u32[]{:S(2)}) collective-permute-start(bf16[20,8,128]{2,1,0:T(8,128)(2,1)S(1)} %get-tuple-element.19), channel_id=1, source_target_pairs={{0,2},{2,4},{4,6},{6,8},{8,10},{10,12},{12,14},{16,18},{18,20},{20... | collective-permute-start | bytes 122888 | tf_op jit(solution)/shard_map/ppermute | solution.py:424
  3.9 6.2 %collective-permute-start.1 = (bf16[20,8,128]{2,1,0:T(8,128)(2,1)S(1)}, bf16[20,8,128]{2,1,0:T(8,128)(2,1)S(1)}, u32[]{:S(2)}, u32[]{:S(2)}) collective-permute-start(bf16[20,8,128]{2,1,0:T(8,128)(2,1)S(1)} %get-tuple-element.20), channel_id=1, source_target_pairs={{2,0},{4,2},{6,4},{8,6},{10,8},{12,10},{14,12},{18,16},{20,18},{22... | collective-permute-start | bytes 122888 | tf_op jit(solution)/shard_map/ppermute | solution.py:425
  10.2 5.5 %copy-start.1 = (f32[4,5,1,128,128]{4,3,2,1,0:T(8,128)S(1)}, f32[4,5,1,128,128]{4,3,2,1,0:T(8,128)}, u32[]{:S(2)}) copy-start(f32[4,5,1,128,128]{4,3,2,1,0:T(8,128)} %param.8) | copy-start | bytes 3932164
  10.2 5.5 %collective-permute-start.2 = (bf16[160,128]{1,0:T(8,128)(2,1)S(1)}, bf16[160,128]{1,0:T(8,128)(2,1)S(1)}, u32[]{:S(2)}, u32[]{:S(2)}) collective-permute-start(bf16[160,128]{1,0:T(8,128)(2,1)S(1)} %get-tuple-element.22), channel_id=1, source_target_pairs={{0,16},{2,18},{4,20},{6,22},{8,24},{10,26},{12,28},{14,30},{16,0},... | collective-permute-start | bytes 122888 | tf_op jit(solution)/shard_map/ppermute | solution.py:438
  18.0 7.2 %copy-start.2 = (s32[9,1,128,128]{3,2,1,0:T(8,128)S(1)}, s32[9,1,128,128]{3,2,1,0:T(8,128)}, u32[]{:S(2)}) copy-start(s32[9,1,128,128]{3,2,1,0:T(8,128)} %table_ref.3) | copy-start | bytes 1769476
  18.0 7.1 %collective-permute-start.4 = (bf16[800,128]{1,0:T(8,128)(2,1)S(1)}, bf16[800,128]{1,0:T(8,128)(2,1)S(1)}, u32[]{:S(2)}, u32[]{:S(2)}) collective-permute-start(bf16[800,128]{1,0:T(8,128)(2,1)S(1)} %shard_map.85), channel_id=1, source_target_pairs={{0,1},{1,0},{2,3},{3,2},{4,5},{5,4},{6,7},{7,6},{8,9},{9,8},{10,11... | collective-permute-start | bytes 614408 | tf_op jit(solution)/shard_map/ppermute | solution.py:485
  24.1 7.6 %collective-permute-start.3 = (bf16[800,128]{1,0:T(8,128)(2,1)S(1)}, bf16[800,128]{1,0:T(8,128)(2,1)S(1)}, u32[]{:S(2)}, u32[]{:S(2)}) collective-permute-start(bf16[800,128]{1,0:T(8,128)(2,1)S(1)} %get-tuple-element.24), channel_id=1, source_target_pairs={{0,1},{1,0},{2,3},{3,2},{4,5},{5,4},{6,7},{7,6},{8,9},{9,8},{10,11... | collective-permute-start | bytes 614408 | tf_op jit(solution)/shard_map/ppermute | solution.py:485
  30.2 7.2 %collective-permute-start.6 = (bf16[640,128]{1,0:T(8,128)(2,1)S(1)}, bf16[640,128]{1,0:T(8,128)(2,1)S(1)}, u32[]{:S(2)}, u32[]{:S(2)}) collective-permute-start(bf16[640,128]{1,0:T(8,128)(2,1)S(1)} %get-tuple-element.29), channel_id=1, source_target_pairs={{0,1},{1,0},{2,3},{3,2},{4,5},{5,4},{6,7},{7,6},{8,9},{9,8},{10,11... | collective-permute-start | bytes 491528 | tf_op jit(solution)/shard_map/ppermute | solution.py:485
  36.8 5.4 %collective-permute-start.5 = (bf16[640,128]{1,0:T(8,128)(2,1)S(1)}, bf16[640,128]{1,0:T(8,128)(2,1)S(1)}, u32[]{:S(2)}, u32[]{:S(2)}) collective-permute-start(bf16[640,128]{1,0:T(8,128)(2,1)S(1)} %get-tuple-element.28), channel_id=1, source_target_pairs={{0,1},{1,0},{2,3},{3,2},{4,5},{5,4},{6,7},{7,6},{8,9},{9,8},{10,11... | collective-permute-start | bytes 491528 | tf_op jit(solution)/shard_map/ppermute | solution.py:485

commit v6 on v5

--- a/solution.py
+++ b/solution.py
@@ -25,14 +25,30 @@
     return lax.broadcasted_iota(jnp.int32, shape, len(shape) - 1)
 
 
-def edge_kernel(state_ref, east_ref, west_ref, rows_ref):
+def first_row(q, n, quarter):
+    return quarter * (1 + q) if n == 0 else 3 * quarter * q
+
+
+def edge_kernel(source_ref, east_ref, west_ref, rows_ref, state_ref, sem):
     chans, cells_x, cells_y = state_ref.shape
+    parts = sem.shape[0]
+    some = chans // parts
+    fetch = [
+        pltpu.make_async_copy(
+            source_ref.at[pl.ds(n * some, some)], state_ref.at[pl.ds(n * some, some)], sem.at[n]
+        )
+        for n in range(parts)
+    ]
+    for copy in fetch:
+        copy.start()
     slot = lax.broadcasted_iota(jnp.int32, (16, cells_y), 0)
     lane = lanes_of((16, cells_y))
     wanted = jnp.where(slot < 8, slot + cells_y - DEEP, slot - 8)
     valid = (slot % 8) < DEEP
     pick = jnp.where(valid & (lane == wanted), 1.0, 0.0).astype(BF16)
     for c in range(chans):
+        if c % some == 0:
+            fetch[c // some].wait()
         block = state_ref[c].astype(BF16)
         strips = lax.dot_general(
             pick, block, (((1,), (1,)), ((), ())), preferred_element_type=F32
@@ -73,39 +89,34 @@
     return jnp.where(((k < 2 * width) & (lower | upper)) | west | east, 1.0, 0.0).astype(BF16)
 
 
-def transport_kernel(
-    state_ref, speed_ref, coef_ref, column_ref, up_ref, down_ref, *rest, chans, jobs, ahead,
-):
+def transport_kernel(state_ref, speed_ref, coef_ref, column_ref, *rest, chans, jobs, size, ahead):
     count = len(jobs)
-    moved_ref, rest = (None, rest) if ahead else (rest[0], rest[1:])
-    packets, windows, rest = rest[:count], rest[count : 2 * count], rest[2 * count :]
-    border, raw_s, once_s, last_s, line_s, matrix, up_s, down_s, sem = rest
+    halos, rest = ((), rest) if ahead else (rest[:2], rest[2:])
+    packets, rest = rest[:count], rest[count:]
+    quarters, rest = ((), rest) if ahead else (rest[:4], rest[4:])
+    windows, rest = rest[:count], rest[count:]
+    border, raw_s, once_s, last_s, line_s, matrix, sem = rest
     cells_x, width = state_ref.shape[1:]
-    half = cells_x // 2
-    message = up_ref.shape[0] // chans
     own = lax.axis_index("group")
     place = lax.axis_index("tile") % TILE_ROWS
-    base_of = [jnp.where(whose == 0, own, 1 - own) * half + start for whose, start, _ in jobs]
+    half_of = (own, 1 - own)
+    base_of = [first_row(half_of[whose], n, size) for whose, n in jobs]
     fetch = pltpu.make_async_copy(state_ref, raw_s.at[:, pl.ds(MARGIN, cells_x)], sem.at[0])
-    halo = [
-        pltpu.make_async_copy(up_ref, up_s, sem.at[1]),
-        pltpu.make_async_copy(down_ref, down_s, sem.at[2]),
-    ]
-    for copy in halo:
-        copy.start()
     fetch.start()
     matrix[...] = shift_matrix(width)
-    for copy in halo:
-        copy.wait()
     lane = lanes_of((chans, width))
     first, last = lane == 0, lane == width - 1
     low_lanes = lane < width // 2
-    for s, ref in enumerate((up_s, down_s)):
+    for s, ref in enumerate(halos):
         border[s] = ref[...].astype(F32)
     coefs = [jnp.broadcast_to(coef_ref[:, n : n + 1], (chans, width)) for n in range(5)]
-
-    above, below = [border[s, pl.ds(2 * DEEP, chans, stride=message), :] for s in range(2)]
-    corners = jnp.where(lane % (2 * DEEP) < DEEP, above, below)
+    message = border.shape[1] // chans
+
+    if ahead:
+        corners = jnp.zeros((chans, width), F32)
+    else:
+        above, below = [border[s, pl.ds(2 * DEEP, chans, stride=message), :] for s in range(2)]
+        corners = jnp.where(lane % (2 * DEEP) < DEEP, above, below)
 
     def pair(k):
         return column_ref[k], roll(corners, width - (2 * DEEP * k + DEEP))
@@ -146,7 +157,7 @@
             for n in range(2):
                 line_s[level, side, n] = edge[n]
         edges.append((main, aux))
-    for window, base, (_, _, size) in zip(windows, base_of, jobs):
+    for window, base in zip(windows, base_of):
         at = base - 1
         sides = []
         for side, first_lane in enumerate((0, width // 2)):
@@ -157,7 +168,7 @@
             sides.append(jnp.where(off, roll(aux, by), roll(main, by)))
         window[pl.ds(2, chans, stride=EXTRA + size), :] = jnp.where(low_lanes, *sides)
 
-    rows = jobs[0][2] + 16 if ahead else cells_x + 16
+    rows = size + 16 if ahead else cells_x + 16
     origin = base_of[0] - 8 if ahead else -8
     top = pl.multiple_of(origin + MARGIN, 8) if ahead else 8
     at = lax.broadcasted_iota(jnp.int32, (rows, width), 0) + origin
@@ -198,28 +209,20 @@
                 + cyu * upper
             )
 
-    outs = []
-
     def finish(base):
         for g in range(group):
             c = base + g
-            for window, row, (_, _, size) in zip(windows, base_of, jobs):
+            for window, row in zip(windows, base_of):
                 at = MARGIN + row
                 to = c * (EXTRA + size)
                 window[pl.ds(to, 1), :] = last_s[c, pl.ds(at - 1, 1), :]
                 window[pl.ds(to + 1, 1), :] = last_s[c, pl.ds(at + size, 1), :]
                 window[pl.ds(to + EXTRA, size), :] = last_s[c, pl.ds(pl.multiple_of(at, 8), size), :]
-        if not ahead:
-            outs.append(
-                pltpu.make_async_copy(
-                    last_s.at[pl.ds(base, group), pl.ds(MARGIN, cells_x)],
-                    moved_ref.at[pl.ds(base, group)],
-                    sem.at[3 + base // group],
-                )
-            )
-            outs[-1].start()
-
-    for c in range(chans):
+            for k, quarter in enumerate(quarters):
+                at = pl.multiple_of(MARGIN + first_row(half_of[k // 2], k % 2, size), 8)
+                quarter[pl.ds(c * size, size), :] = last_s[c, pl.ds(at, size), :]
+
+    for c in range(0 if ahead else chans):
         raw_s[c, pl.ds(MARGIN - DEEP, DEEP), :] = border[0, pl.ds(c * message + DEEP, DEEP), :]
         raw_s[c, pl.ds(MARGIN + cells_x, DEEP), :] = border[1, pl.ds(c * message, DEEP), :]
     for base in range(0, chans + group, group):
@@ -230,31 +233,25 @@
             finish(base - group)
     for packet, window in zip(packets, windows):
         packet[...] = window[...].astype(BF16)
-    for copy in outs:
-        copy.wait()
-
-
-def physics_kernel(
-    table_ref, w1_ref, w2_ref, w3_ref, mine_ref, got_ref, image_in,
-    image_ref, other_ref, wide, packed, mask, table, even, odd, terms, patch, got, sem, *, start, chans,
-):
+
+
+def physics_kernel(chunk, table_ref, w1_ref, w2_ref, w3_ref, mine_ref, got_ref, kept_ref, *rest, chans):
+    (
+        image_ref, other_ref, wide, packed, mask, table, even, odd, terms, patch, got, sem
+    ) = rest[-12:]
     size, width = table.shape[1:]
-    cells_x = image_in.shape[1]
-    half = cells_x // 2
     height = EXTRA + size
     pad = -(-chans // 8) * 8
     both = 2 * pad
-    top = lax.axis_index("group") * half + start
+    top = first_row(lax.axis_index("group"), chunk, size)
     copies = [
         pltpu.make_async_copy(table_ref.at[k, 0, pl.ds(top, size)], table.at[n], sem.at[n])
         for n, k in enumerate((5, 7))
     ]
-    fetch = pltpu.make_async_copy(image_in.at[:, pl.ds(top, size)], patch, sem.at[2])
-    arrive = pltpu.make_async_copy(got_ref, got, sem.at[4])
+    arrive = pltpu.make_async_copy(got_ref, got, sem.at[2])
     for copy in copies:
         copy.start()
     arrive.start()
-    fetch.start()
 
     k = lax.broadcasted_iota(jnp.int32, (2 * width, 2 * width), 0)
     n = lax.broadcasted_iota(jnp.int32, (2 * width, 2 * width), 1)
@@ -357,37 +354,21 @@
             stack(n + 1, slots[(n + 1) % 2])
         network(n, slots[n % 2])
     other_ref[...] = terms[1].astype(BF16)
-    fetch.wait()
-    patch[...] = patch[...] + terms[0].reshape(patch.shape)
+    patch[...] = (kept_ref[...] + terms[0]).reshape(patch.shape)
     put = pltpu.make_async_copy(patch, image_ref.at[:, pl.ds(top, size)], sem.at[3])
     put.start()
     put.wait()
 
 
-def finish_kernel(back_ref, image_in, image_ref, patch, back, sem, *, start, parts):
+def finish_kernel(chunk, back_ref, moved_ref, image_in, image_ref, patch, sem, *, parts):
     chans, size, width = patch.shape
-    half = image_in.shape[1] // 2
-    rows = pl.ds((1 - lax.axis_index("group")) * half + start, size)
+    rows = pl.ds(first_row(1 - lax.axis_index("group"), chunk, size), size)
     some = chans // parts
-    fetch = []
+    put = []
     for n in range(parts):
         c, r = pl.ds(n * some, some), pl.ds(n * some * size, some * size)
-        fetch.append(
-            (
-                pltpu.make_async_copy(back_ref.at[r], back.at[r], sem.at[n]),
-                pltpu.make_async_copy(image_in.at[c, rows], patch.at[c], sem.at[parts + n]),
-            )
-        )
-        for copy in fetch[-1]:
-            copy.start()
-    put = []
-    for n in range(parts):
-        for copy in fetch[n]:
-            copy.wait()
-        c = pl.ds(n * some, some)
-        terms = back[pl.ds(n * some * size, some * size)].astype(F32)
-        patch[c] = patch[c] + terms.reshape(some, size, width)
-        put.append(pltpu.make_async_copy(patch.at[c], image_ref.at[c, rows], sem.at[2 * parts + n]))
+        patch[c] = (moved_ref[r] + back_ref[r].astype(F32)).reshape(some, size, width)
+        put.append(pltpu.make_async_copy(patch.at[c], image_ref.at[c, rows], sem.at[n]))
         put[-1].start()
     for copy in put:
         copy.wait()
@@ -416,7 +397,12 @@
     sds = jax.ShapeDtypeStruct
 
     strip = sds((chans, 8, cells_y), BF16)
-    to_east, to_west, rows = call(edge_kernel, (strip, strip, strip), [VMEM_SPEC])(block)
+    to_east, to_west, rows = call(
+        edge_kernel,
+        (strip, strip, strip),
+        [pl.BlockSpec(memory_space=pltpu.HBM)],
+        [pltpu.VMEM(block.shape, F32), pltpu.SemaphoreType.DMA((chans // 2,))],
+    )(block)
 
     def beside(by):
         return [(i, i + by) for i in range(tiles) if 0 <= i % TILE_ROWS + by < TILE_ROWS]
@@ -453,19 +439,18 @@
         ]
     )
 
-    quarter = cells_x // 4
-    chunks = [(n * quarter, quarter) for n in range(2)]
+    size = cells_x // 4
     tall = pltpu.VMEM((chans, cells_x + 2 * MARGIN, cells_y), F32)
-
-    def transport(jobs, ahead):
-        heights = [chans * (EXTRA + size) for _, _, size in jobs]
-        packets = [sds((height, cells_y), BF16) for height in heights]
-        moved = () if ahead else (sds((chans, cells_x, cells_y), F32),)
+    height = chans * (EXTRA + size)
+    moved = sds((chans * size, cells_y), F32)
+
+    def transport(jobs, *halos):
+        ahead = len(halos) == 0
         return call(
-            functools.partial(transport_kernel, chans=chans, jobs=jobs, ahead=ahead),
-            (*moved, *packets),
-            [ANY_SPEC, pl.BlockSpec(memory_space=pltpu.SMEM)] + [VMEM_SPEC] * 2 + [ANY_SPEC] * 2,
-            [pltpu.VMEM((height, cells_y), F32) for height in heights]
+            functools.partial(transport_kernel, chans=chans, jobs=jobs, size=size, ahead=ahead),
+            (sds((height, cells_y), BF16),) * len(jobs) + (() if ahead else (moved,) * 4),
+            [ANY_SPEC, pl.BlockSpec(memory_space=pltpu.SMEM)] + [VMEM_SPEC] * (2 + len(halos)),
+            [pltpu.VMEM((height, cells_y), F32) for _ in jobs]
             + [
                 pltpu.VMEM((2, chans * 8, cells_y), F32),
                 tall,
@@ -473,24 +458,18 @@
                 tall,
                 pltpu.VMEM((2, 2, 2, chans, cells_y), F32),
                 pltpu.VMEM((4 * cells_y, 2 * cells_y), BF16),
-                pltpu.VMEM(up.shape, BF16),
-                pltpu.VMEM(up.shape, BF16),
-                pltpu.SemaphoreType.DMA((3 + chans,)),
+                pltpu.SemaphoreType.DMA((1,)),
             ],
             flops=5 * 10**9,
-            out_specs=(ANY_SPEC,) * len(moved) + (VMEM_SPEC,) * len(jobs),
-        )(block, coef, coef.T, columns, up, down)
+        )(block, coef, coef.T, columns, *halos)
 
     def swap(x):
         return lax.ppermute(x, "group", [(0, 1), (1, 0)])
 
-    (packet,) = transport([(1, *chunks[0])], True)
-    got = [swap(packet)]
-    image, *packets = transport(
-        [(1, *chunk) for chunk in chunks[1:]] + [(0, *chunk) for chunk in chunks], False
-    )
-    theirs, mine = packets[: len(chunks) - 1], packets[len(chunks) - 1 :]
-    got += [swap(packet) for packet in theirs]
+    (theirs0,) = transport([(1, 0)])
+    theirs1, *rest = transport([(1, 1), (0, 0), (0, 1)], up, down)
+    mine, kept, others = rest[:2], rest[2:4], rest[4:]
+    got = [swap(theirs0), swap(theirs1)]
 
     own = lax.axis_index("group")
     both = 2 * pad
@@ -504,18 +483,18 @@
     w3 = jnp.pad(w3, ((0, 0), (0, pad - chans), (0, 0))).reshape(both, hidden)
     w2 = (w_mid * 0.5).T
 
-    parts = 4 if chans % 4 == 0 else 1
     back = []
-    for n, (start, size) in enumerate(chunks):
-        depth = 8 * (-(-chans // 8)) * (EXTRA + size)
-        wide = pltpu.VMEM((3, 2, depth, cells_y), F32)
-        blocks = pltpu.VMEM((9 * both, min(BLOCK_ROWS, size) * cells_y), BF16)
+    image = None
+    blocks = pltpu.VMEM((9 * both, BLOCK_ROWS * cells_y), BF16)
+    whole = sds((chans, cells_x, cells_y), F32)
+    for n in range(2):
+        images = () if image is None else (image,)
         image, other = call(
-            functools.partial(physics_kernel, start=start, chans=chans),
-            (image, sds((chans * size, cells_y), BF16)),
-            [ANY_SPEC] + [VMEM_SPEC] * 4 + [ANY_SPEC] * 2,
+            functools.partial(physics_kernel, n, chans=chans),
+            (whole, sds((chans * size, cells_y), BF16)),
+            [ANY_SPEC] + [VMEM_SPEC] * 4 + [ANY_SPEC, VMEM_SPEC] + [ANY_SPEC] * len(images),
             [
-                wide,
+                pltpu.VMEM((3, 2, pad * (EXTRA + size), cells_y), F32),
                 pltpu.VMEM((3, size + 2, both, cells_y), BF16),
                 pltpu.VMEM((3, size, cells_y), F32),
                 pltpu.VMEM((2, size, cells_y), jnp.int32),
@@ -523,28 +502,25 @@
                 blocks,
                 pltpu.VMEM((2, chans * size, cells_y), F32),
                 pltpu.VMEM((chans, size, cells_y), F32),
-                pltpu.VMEM((chans * (EXTRA + size), cells_y), BF16),
-                pltpu.SemaphoreType.DMA((5,)),
+                pltpu.VMEM((height, cells_y), BF16),
+                pltpu.SemaphoreType.DMA((4,)),
             ],
             flops=7 * 10**9,
             out_specs=(ANY_SPEC, VMEM_SPEC),
-            aliases={6: 0},
-        )(neighbours, w1, w2, w3, mine[n], got[n], image)
+            aliases={7: 0} if images else {},
+        )(neighbours, w1, w2, w3, mine[n], got[n], kept[n], *images)
         back.append(swap(other))
-    for n, (start, size) in enumerate(chunks):
+    parts = 4 if chans % 4 == 0 else 1
+    for n in range(2):
         image = call(
-            functools.partial(finish_kernel, start=start, parts=parts),
-            image,
-            [ANY_SPEC, ANY_SPEC],
-            [
-                pltpu.VMEM((chans, size, cells_y), F32),
-                pltpu.VMEM((chans * size, cells_y), BF16),
-                pltpu.SemaphoreType.DMA((3 * parts,)),
-            ],
+            functools.partial(finish_kernel, n, parts=parts),
+            whole,
+            [VMEM_SPEC, VMEM_SPEC, ANY_SPEC],
+            [pltpu.VMEM((chans, size, cells_y), F32), pltpu.SemaphoreType.DMA((parts,))],
             out_specs=ANY_SPEC,
-            aliases={1: 0},
+            aliases={2: 0},
             limit=4,
-        )(back[n], image)
+        )(back[n], others[n], image)
     return image.reshape(levels, fields, single, cells_x, cells_y)
 
 

time: 44.4 us -> 43.4 us (0.977)
  the two profiles are of different devices: /device:TPU:24 before, /device:TPU:8 now
where the time goes in v6:
time: 43.4 us; the launch traced here: 43.3 us
  Pallas kernels  20.4 us (47%)
  starting transfers between devices  13.6 us (31%)
  waiting for transfers between devices  6.54 us (15%)
  local copies, waits for them, and re-layouts  2.31 us (5%)
    pallas_call x2, Pallas kernels, shards(): call(functools.partial(physics_kernel, n, chans=chans), (whole, sds((chan...  10 us
    ppermute x4, waiting for transfers between devices, swap(): return lax.ppermute(x, 'group', [(0, 1), (1, 0)])  6.22 us
    pallas_call x2, Pallas kernels, transport(): call(functools.partial(transport_kernel, chans=chans, jobs=jobs, size=siz...  5.39 us
    ppermute x1, starting transfers between devices, shards(): from_east = lax.ppermute(to_west, 'tile', beside(-1))  4.54 us
    ppermute x4, starting transfers between devices, swap(): return lax.ppermute(x, 'group', [(0, 1), (1, 0)])  4.44 us
    pallas_call x1, Pallas kernels, shards(): call(edge_kernel, (strip, strip, strip), [pl.BlockSpec(memory_space=pltpu...  3.33 us
    ppermute x1, starting transfers between devices, across(): lax.ppermute(x, 'tile', [(i, (i + by) % tiles) for i in range(tiles)])  2.65 us
    ppermute x1, starting transfers between devices, shards(): from_west = lax.ppermute(to_east, 'tile', beside(1))  1.92 us
  transfers between devices with their start and end apart: 7, of which 3 were waited for; matrix products, arithmetic and copies ran while one was open for 3% of the time, Pallas kernels for 37%

profile of v6, /device:TPU:8, one launch (start us, length us, event | category | flops | bytes accessed | tf_op | source)
XLA Modules:
  0.0 43.3 jit_solution(1493639832217942912)
XLA Ops:
  0.0 0.0 copy-start
  0.0 1.3 %copy-done = f32[4,5,1,128,128]{4,3,2,1,0:T(8,128)S(1)} copy-done((f32[4,5,1,128,128]{4,3,2,1,0:T(8,128)S(1)}, f32[4,5,1,128,128]{4,3,2,1,0:T(8,128)}, u32[]{:S(2)}) %copy-start) | copy-done | bytes 1310744
  1.3 0.0 copy-start.6
  1.3 0.0 copy-start.5
  1.3 0.0 copy-start.4
  1.3 0.0 copy-start.3
  1.3 3.3 %shard_map.82 = (bf16[20,8,128]{2,1,0:T(8,128)(2,1)S(1)}, bf16[20,8,128]{2,1,0:T(8,128)(2,1)S(1)}, bf16[20,8,128]{2,1,0:T(8,128)(2,1)S(1)}) custom-call(f32[20,128,128]{2,1,0:T(8,128)S(1)} %bitcast.21), custom_call_target="tpu_custom_call" | custom-call | flops 1000000000 | bytes 1000000 | tf_op jit(solution)/shard_map/pallas_call | solution.py:400
  4.7 0.0 copy-start.7
  4.7 0.0 copy-start.8
  4.7 1.9 %collective-permute-start = (bf16[20,8,128]{2,1,0:T(8,128)(2,1)S(1)}, bf16[20,8,128]{2,1,0:T(8,128)(2,1)S(1)}, u32[]{:S(2)}, u32[]{:S(2)}) collective-permute-start(bf16[20,8,128]{2,1,0:T(8,128)(2,1)S(1)} %get-tuple-element.22), channel_id=1, source_target_pairs={{0,2},{2,4},{4,6},{6,8},{8,10},{10,12},{12,14},{16,18},{18,20},{20... | collective-permute-start | bytes 122888 | tf_op jit(solution)/shard_map/ppermute | solution.py:410
  6.6 4.5 %collective-permute-start.1 = (bf16[20,8,128]{2,1,0:T(8,128)(2,1)S(1)}, bf16[20,8,128]{2,1,0:T(8,128)(2,1)S(1)}, u32[]{:S(2)}, u32[]{:S(2)}) collective-permute-start(bf16[20,8,128]{2,1,0:T(8,128)(2,1)S(1)} %get-tuple-element.23), channel_id=1, source_target_pairs={{2,0},{4,2},{6,4},{8,6},{10,8},{12,10},{14,12},{18,16},{20,18},{22... | collective-permute-start | bytes 122888 | tf_op jit(solution)/shard_map/ppermute | solution.py:411
  11.2 0.0 copy-done.6
  11.2 0.0 copy-done.5
  11.2 0.0 copy-done.4
  11.2 0.1 copy.36
  11.4 0.0 copy-done.3
  11.4 0.1 reshape.175
  11.5 0.1 fusion
  11.6 0.0 copy-done.7
  11.6 0.0 copy-done.8
  11.6 0.1 broadcast_subtract_fusion
  11.7 0.1 sub.70
  11.8 0.1 sub.68
  11.8 0.1 add.33
  11.9 0.1 add.31
  12.0 0.1 sub.66
  12.1 0.1 copy.37
  12.2 0.1 copy.41
  12.3 0.1 copy.39.w1_ref
  12.5 0.0 collective-permute-done
  12.5 0.3 collective-permute-done.1
  12.8 0.0 copy-start.1
  12.8 0.1 shard_map.83
  12.9 2.7 %collective-permute-start.2 = (bf16[160,128]{1,0:T(8,128)(2,1)S(1)}, bf16[160,128]{1,0:T(8,128)(2,1)S(1)}, u32[]{:S(2)}, u32[]{:S(2)}) collective-permute-start(bf16[160,128]{1,0:T(8,128)(2,1)S(1)} %get-tuple-element.25), channel_id=1, source_target_pairs={{0,16},{2,18},{4,20},{6,22},{8,24},{10,26},{12,28},{14,30},{16,0},... | collective-permute-start | bytes 122888 | tf_op jit(solution)/shard_map/ppermute | solution.py:424
  15.6 0.0 copy-done.1
  15.6 1.8 %shard_map.85 = bf16[800,128]{1,0:T(8,128)(2,1)S(1)} custom-call(f32[20,128,128]{2,1,0:T(8,128)S(1)} %bitcast.22, f32[5,20]{1,0:T(8,128)S(1)} %stack.2.speed_ref, f32[20,5]{1,0:T(8,128)S(1)} %bitcast.19, f32[10,20,128]{2,1,0:T(8,128)S(1)} %get-tuple-element.24.column_ref), custom_call_target="tpu_custom_call" | custom-call | flops 5000000000 | bytes 1000000 | tf_op jit(solution)/shard_map/pallas_call | solution.py:449
  17.5 0.0 copy-start.2
  17.5 1.6 %collective-permute-start.4 = (bf16[800,128]{1,0:T(8,128)(2,1)S(1)}, bf16[800,128]{1,0:T(8,128)(2,1)S(1)}, u32[]{:S(2)}, u32[]{:S(2)}) collective-permute-start(bf16[800,128]{1,0:T(8,128)(2,1)S(1)} %shard_map.85), channel_id=1, source_target_pairs={{0,1},{1,0},{2,3},{3,2},{4,5},{5,4},{6,7},{7,6},{8,9},{9,8},{10,11... | collective-permute-start | bytes 614408 | tf_op jit(solution)/shard_map/ppermute | solution.py:467
  19.1 0.0 collective-permute-done.2.rest_0_.rest_1_
  19.1 3.5 %shard_map.84 = (bf16[800,128]{1,0:T(8,128)(2,1)S(1)}, bf16[800,128]{1,0:T(8,128)(2,1)S(1)}, bf16[800,128]{1,0:T(8,128)(2,1)S(1)}, f32[640,128]{1,0:T(8,128)S(1)...) custom-call(f32[20,128,128]{2,1,0:T(8,128)S(1)} %bitcast.23, ...), custom_call_target="tpu_custom_call" | custom-call | flops 5000000000 | bytes 1000000 | tf_op jit(solution)/shard_map/pallas_call | solution.py:449
  22.6 0.6 %collective-permute-start.3 = (bf16[800,128]{1,0:T(8,128)(2,1)S(1)}, bf16[800,128]{1,0:T(8,128)(2,1)S(1)}, u32[]{:S(2)}, u32[]{:S(2)}) collective-permute-start(bf16[800,128]{1,0:T(8,128)(2,1)S(1)} %get-tuple-element.27), channel_id=1, source_target_pairs={{0,1},{1,0},{2,3},{3,2},{4,5},{5,4},{6,7},{7,6},{8,9},{9,8},{10,11... | collective-permute-start | bytes 614408 | tf_op jit(solution)/shard_map/ppermute | solution.py:467
  23.2 1.7 %collective-permute-done.4.got_ref = bf16[800,128]{1,0:T(8,128)(2,1)S(1)} collective-permute-done((bf16[800,128]{1,0:T(8,128)(2,1)S(1)}, bf16[800,128]{1,0:T(8,128)(2,1)S(1)}, u32[]{:S(2)}, u32[]{:S(2)}) %collective-permute-start.4) | collective-permute-done | bytes 204832 | tf_op jit(solution)/shard_map/ppermute | solution.py:467
  25.0 0.0 copy-done.2
  25.0 5.0 %shard_map.86 = (f32[20,128,128]{2,1,0:T(8,128)}, bf16[640,128]{1,0:T(8,128)(2,1)S(1)}) custom-call(s32[9,1,128,128]{3,2,1,0:T(8,128)S(1)} %copy-done.2, bf16[256,432]{1,0:T(8,128)(2,1)S(1)} %copy.39.w1_ref, bf16[256,256]{1,0:T(8,128)(2,1)S(1)} %multiply_bitcast_fusion.w2_ref, bf16[48,256]{1,0:T(8,128)(2,1)S(1)} %bitcast.17, ...), custom_call_target="tpu_custom_call" | custom-call | flops 7000000000 | bytes 1000000 | tf_op jit(solution)/shard_map/pallas_call | solution.py:492
  30.0 2.1 %collective-permute-start.6 = (bf16[640,128]{1,0:T(8,128)(2,1)S(1)}, bf16[640,128]{1,0:T(8,128)(2,1)S(1)}, u32[]{:S(2)}, u32[]{:S(2)}) collective-permute-start(bf16[640,128]{1,0:T(8,128)(2,1)S(1)} %get-tuple-element.34), channel_id=1, source_target_pairs={{0,1},{1,0},{2,3},{3,2},{4,5},{5,4},{6,7},{7,6},{8,9},{9,8},{10,11... | collective-permute-start | bytes 491528 | tf_op jit(solution)/shard_map/ppermute | solution.py:467
  32.1 0.0 collective-permute-done.3.got_ref
  32.1 5.0 %shard_map.87 = (f32[20,128,128]{2,1,0:T(8,128)}, bf16[640,128]{1,0:T(8,128)(2,1)S(1)}) custom-call(s32[9,1,128,128]{3,2,1,0:T(8,128)S(1)} %copy-done.2, bf16[256,432]{1,0:T(8,128)(2,1)S(1)} %copy.39.w1_ref, bf16[256,256]{1,0:T(8,128)(2,1)S(1)} %multiply_bitcast_fusion.w2_ref, bf16[48,256]{1,0:T(8,128)(2,1)S(1)} %bitcast.18, ...), custom_call_target="tpu_custom_call", output_to_operand_aliasing={{0}: (7, {})} | custom-call | flops 7000000000 | bytes 1000000 | tf_op jit(solution)/shard_map/pallas_call | solution.py:492
  37.1 0.1 collective-permute-start.5
  37.2 0.0 collective-permute-done.6.back_ref
  37.2 0.8 %shard_map.88.image_in = f32[20,128,128]{2,1,0:T(8,128)} custom-call(bf16[640,128]{1,0:T(8,128)(2,1)S(1)} %collective-permute-done.6.back_ref, f32[640,128]{1,0:T(8,128)S(1)} %get-tuple-element.35.moved_ref, f32[20,128,128]{2,1,0:T(8,128)} %get-tuple-element.36.image_in), custom_call_target="tpu_custom_call", output_to_operand_aliasing={{}: (2, {})} | custom-call | flops 1000000000 | bytes 1000000 | tf_op jit(solution)/shard_map/pallas_call | solution.py:515
  38.0 4.5 %collective-permute-done.5.back_ref = bf16[640,128]{1,0:T(8,128)(2,1)S(1)} collective-permute-done((bf16[640,128]{1,0:T(8,128)(2,1)S(1)}, bf16[640,128]{1,0:T(8,128)(2,1)S(1)}, u32[]{:S(2)}, u32[]{:S(2)}) %collective-permute-start.5) | collective-permute-done | bytes 163872 | tf_op jit(solution)/shard_map/ppermute | solution.py:467
  42.5 0.8 %shard_map.89 = f32[20,128,128]{2,1,0:T(8,128)} custom-call(bf16[640,128]{1,0:T(8,128)(2,1)S(1)} %collective-permute-done.5.back_ref, f32[640,128]{1,0:T(8,128)S(1)} %get-tuple-element.33.moved_ref, f32[20,128,128]{2,1,0:T(8,128)} %shard_map.88.image_in), custom_call_target="tpu_custom_call", output_to_operand_aliasing={{}: (2, {})} | custom-call | flops 1000000000 | bytes 1000000 | tf_op jit(solution)/shard_map/pallas_call | solution.py:515
  (9 shorter events, 0.1 us)
Async XLA Ops:
  0.0 1.3 %copy-start = (f32[4,5,1,128,128]{4,3,2,1,0:T(8,128)S(1)}, f32[4,5,1,128,128]{4,3,2,1,0:T(8,128)}, u32[]{:S(2)}) copy-start(f32[4,5,1,128,128]{4,3,2,1,0:T(8,128)} %param.8) | copy-start | bytes 3932164
  1.3 9.9 %copy-start.6 = (f32[5]{0:T(128)S(1)}, f32[5]{0:T(128)}, u32[]{:S(2)}) copy-start(f32[5]{0:T(128)} %param.11) | copy-start | bytes 64
  1.3 9.9 %copy-start.5 = (bf16[256,40]{0,1:T(8,128)(2,1)S(1)}, bf16[256,40]{0,1:T(8,128)(2,1)}, u32[]{:S(2)}) copy-start(bf16[256,40]{0,1:T(8,128)(2,1)} %param.15) | copy-start | bytes 61444
  1.3 9.9 %copy-start.4 = (bf16[256,256]{1,0:T(8,128)(2,1)S(1)}, bf16[256,256]{1,0:T(8,128)(2,1)}, u32[]{:S(2)}) copy-start(bf16[256,256]{1,0:T(8,128)(2,1)} %param.14) | copy-start | bytes 393220
  1.3 10.0 %copy-start.3 = (bf16[360,256]{1,0:T(8,128)(2,1)S(1)}, bf16[360,256]{1,0:T(8,128)(2,1)}, u32[]{:S(2)}) copy-start(bf16[360,256]{1,0:T(8,128)(2,1)} %param.13) | copy-start | bytes 552964
  4.7 6.9 %copy-start.7 = (f32[4]{0:T(128)S(1)}, f32[4]{0:T(128)}, u32[]{:S(2)}) copy-start(f32[4]{0:T(128)} %param.10) | copy-start | bytes 52
  4.7 6.9 %copy-start.8 = (f32[4]{0:T(128)S(1)}, f32[4]{0:T(128)}, u32[]{:S(2)}) copy-start(f32[4]{0:T(128)} %param.9) | copy-start | bytes 52
  4.7 7.8 %collective-permute-start = (bf16[20,8,128]{2,1,0:T(8,128)(2,1)S(1)}, bf16[20,8,128]{2,1,0:T(8,128)(2,1)S(1)}, u32[]{:S(2)}, u32[]{:S(2)}) collective-permute-start(bf16[20,8,128]{2,1,0:T(8,128)(2,1)S(1)} %get-tuple-element.22), channel_id=1, source_target_pairs={{0,2},{2,4},{4,6},{6,8},{8,10},{10,12},{12,14},{16,18},{18,20},{20... | collective-permute-start | bytes 122888 | tf_op jit(solution)/shard_map/ppermute | solution.py:410
  6.6 6.2 %collective-permute-start.1 = (bf16[20,8,128]{2,1,0:T(8,128)(2,1)S(1)}, bf16[20,8,128]{2,1,0:T(8,128)(2,1)S(1)}, u32[]{:S(2)}, u32[]{:S(2)}) collective-permute-start(bf16[20,8,128]{2,1,0:T(8,128)(2,1)S(1)} %get-tuple-element.23), channel_id=1, source_target_pairs={{2,0},{4,2},{6,4},{8,6},{10,8},{12,10},{14,12},{18,16},{20,18},{22... | collective-permute-start | bytes 122888 | tf_op jit(solution)/shard_map/ppermute | solution.py:411
  12.8 2.8 %copy-start.1 = (f32[4,5,1,128,128]{4,3,2,1,0:T(8,128)S(1)}, f32[4,5,1,128,128]{4,3,2,1,0:T(8,128)}, u32[]{:S(2)}) copy-start(f32[4,5,1,128,128]{4,3,2,1,0:T(8,128)} %param.8) | copy-start | bytes 3932164
  12.9 6.1 %collective-permute-start.2 = (bf16[160,128]{1,0:T(8,128)(2,1)S(1)}, bf16[160,128]{1,0:T(8,128)(2,1)S(1)}, u32[]{:S(2)}, u32[]{:S(2)}) collective-permute-start(bf16[160,128]{1,0:T(8,128)(2,1)S(1)} %get-tuple-element.25), channel_id=1, source_target_pairs={{0,16},{2,18},{4,20},{6,22},{8,24},{10,26},{12,28},{14,30},{16,0},... | collective-permute-start | bytes 122888 | tf_op jit(solution)/shard_map/ppermute | solution.py:424
  17.5 7.5 %copy-start.2 = (s32[9,1,128,128]{3,2,1,0:T(8,128)S(1)}, s32[9,1,128,128]{3,2,1,0:T(8,128)}, u32[]{:S(2)}) copy-start(s32[9,1,128,128]{3,2,1,0:T(8,128)} %table_ref.3) | copy-start | bytes 1769476
  17.5 7.5 %collective-permute-start.4 = (bf16[800,128]{1,0:T(8,128)(2,1)S(1)}, bf16[800,128]{1,0:T(8,128)(2,1)S(1)}, u32[]{:S(2)}, u32[]{:S(2)}) collective-permute-start(bf16[800,128]{1,0:T(8,128)(2,1)S(1)} %shard_map.85), channel_id=1, source_target_pairs={{0,1},{1,0},{2,3},{3,2},{4,5},{5,4},{6,7},{7,6},{8,9},{9,8},{10,11... | collective-permute-start | bytes 614408 | tf_op jit(solution)/shard_map/ppermute | solution.py:467
  22.6 9.5 %collective-permute-start.3 = (bf16[800,128]{1,0:T(8,128)(2,1)S(1)}, bf16[800,128]{1,0:T(8,128)(2,1)S(1)}, u32[]{:S(2)}, u32[]{:S(2)}) collective-permute-start(bf16[800,128]{1,0:T(8,128)(2,1)S(1)} %get-tuple-element.27), channel_id=1, source_target_pairs={{0,1},{1,0},{2,3},{3,2},{4,5},{5,4},{6,7},{7,6},{8,9},{9,8},{10,11... | collective-permute-start | bytes 614408 | tf_op jit(solution)/shard_map/ppermute | solution.py:467
  30.0 7.3 %collective-permute-start.6 = (bf16[640,128]{1,0:T(8,128)(2,1)S(1)}, bf16[640,128]{1,0:T(8,128)(2,1)S(1)}, u32[]{:S(2)}, u32[]{:S(2)}) collective-permute-start(bf16[640,128]{1,0:T(8,128)(2,1)S(1)} %get-tuple-element.34), channel_id=1, source_target_pairs={{0,1},{1,0},{2,3},{3,2},{4,5},{5,4},{6,7},{7,6},{8,9},{9,8},{10,11... | collective-permute-start | bytes 491528 | tf_op jit(solution)/shard_map/ppermute | solution.py:467
  37.1 5.4 %collective-permute-start.5 = (bf16[640,128]{1,0:T(8,128)(2,1)S(1)}, bf16[640,128]{1,0:T(8,128)(2,1)S(1)}, u32[]{:S(2)}, u32[]{:S(2)}) collective-permute-start(bf16[640,128]{1,0:T(8,128)(2,1)S(1)} %get-tuple-element.32), channel_id=1, source_target_pairs={{0,1},{1,0},{2,3},{3,2},{4,5},{5,4},{6,7},{7,6},{8,9},{9,8},{10,11... | collective-permute-start | bytes 491528 | tf_op jit(solution)/shard_map/ppermute | solution.py:467

commit v7 on v6

--- a/solution.py
+++ b/solution.py
@@ -29,26 +29,14 @@
     return quarter * (1 + q) if n == 0 else 3 * quarter * q
 
 
-def edge_kernel(source_ref, east_ref, west_ref, rows_ref, state_ref, sem):
+def edge_kernel(state_ref, east_ref, west_ref, rows_ref):
     chans, cells_x, cells_y = state_ref.shape
-    parts = sem.shape[0]
-    some = chans // parts
-    fetch = [
-        pltpu.make_async_copy(
-            source_ref.at[pl.ds(n * some, some)], state_ref.at[pl.ds(n * some, some)], sem.at[n]
-        )
-        for n in range(parts)
-    ]
-    for copy in fetch:
-        copy.start()
     slot = lax.broadcasted_iota(jnp.int32, (16, cells_y), 0)
     lane = lanes_of((16, cells_y))
     wanted = jnp.where(slot < 8, slot + cells_y - DEEP, slot - 8)
     valid = (slot % 8) < DEEP
     pick = jnp.where(valid & (lane == wanted), 1.0, 0.0).astype(BF16)
     for c in range(chans):
-        if c % some == 0:
-            fetch[c // some].wait()
         block = state_ref[c].astype(BF16)
         strips = lax.dot_general(
             pick, block, (((1,), (1,)), ((), ())), preferred_element_type=F32
@@ -102,7 +90,8 @@
     half_of = (own, 1 - own)
     base_of = [first_row(half_of[whose], n, size) for whose, n in jobs]
     fetch = pltpu.make_async_copy(state_ref, raw_s.at[:, pl.ds(MARGIN, cells_x)], sem.at[0])
-    fetch.start()
+    if not ahead:
+        fetch.start()
     matrix[...] = shift_matrix(width)
     lane = lanes_of((chans, width))
     first, last = lane == 0, lane == width - 1
@@ -174,14 +163,16 @@
     at = lax.broadcasted_iota(jnp.int32, (rows, width), 0) + origin
     diagonal = lax.rem(at + width, width) == lanes_of((rows, width))
     within = (at >= 0) & (at < cells_x)
-    fetch.wait()
+    if not ahead:
+        fetch.wait()
     group = next(n for n in (10 if ahead else GROUP, 2, 1) if chans % n == 0)
 
     def sweep(level, src, dst, base):
+        near_top = pl.multiple_of(origin, 8) if ahead and level == 0 else top
         parts = []
         for g in range(group):
             c = base + g
-            q = src[c, pl.ds(top, rows), :]
+            q = src[c, pl.ds(near_top, rows), :]
             hi = q.astype(BF16)
             lo = (q - hi.astype(F32)).astype(BF16)
             sides = []
@@ -202,9 +193,9 @@
             lower, upper = near[g * rows : (g + 1) * rows, :width], near[g * rows : (g + 1) * rows, width:]
             c0, cxl, cxu, cyl, cyu = [speed_ref[n, c] for n in range(5)]
             dst[c, pl.ds(top, rows), :] = (
-                c0 * src[c, pl.ds(top, rows), :]
-                + cxl * src[c, pl.ds(top - 1, rows), :]
-                + cxu * src[c, pl.ds(top + 1, rows), :]
+                c0 * src[c, pl.ds(near_top, rows), :]
+                + cxl * src[c, pl.ds(near_top - 1, rows), :]
+                + cxu * src[c, pl.ds(near_top + 1, rows), :]
                 + cyl * lower
                 + cyu * upper
             )
@@ -227,7 +218,7 @@
         raw_s[c, pl.ds(MARGIN + cells_x, DEEP), :] = border[1, pl.ds(c * message, DEEP), :]
     for base in range(0, chans + group, group):
         if base < chans:
-            sweep(0, raw_s, once_s, base)
+            sweep(0, state_ref if ahead else raw_s, once_s, base)
         if base:
             sweep(1, once_s, last_s, base - group)
             finish(base - group)
@@ -397,12 +388,7 @@
     sds = jax.ShapeDtypeStruct
 
     strip = sds((chans, 8, cells_y), BF16)
-    to_east, to_west, rows = call(
-        edge_kernel,
-        (strip, strip, strip),
-        [pl.BlockSpec(memory_space=pltpu.HBM)],
-        [pltpu.VMEM(block.shape, F32), pltpu.SemaphoreType.DMA((chans // 2,))],
-    )(block)
+    to_east, to_west, rows = call(edge_kernel, (strip, strip, strip), [VMEM_SPEC])(block)
 
     def beside(by):
         return [(i, i + by) for i in range(tiles) if 0 <= i % TILE_ROWS + by < TILE_ROWS]
@@ -449,7 +435,8 @@
         return call(
             functools.partial(transport_kernel, chans=chans, jobs=jobs, size=size, ahead=ahead),
             (sds((height, cells_y), BF16),) * len(jobs) + (() if ahead else (moved,) * 4),
-            [ANY_SPEC, pl.BlockSpec(memory_space=pltpu.SMEM)] + [VMEM_SPEC] * (2 + len(halos)),
+            [VMEM_SPEC if ahead else ANY_SPEC, pl.BlockSpec(memory_space=pltpu.SMEM)]
+            + [VMEM_SPEC] * (2 + len(halos)),
             [pltpu.VMEM((height, cells_y), F32) for _ in jobs]
             + [
                 pltpu.VMEM((2, chans * 8, cells_y), F32),

time: 43.4 us -> 40.3 us (0.929)
  Pallas kernels: 20.4 us -> 17.2 us
    pallas_call x1, Pallas kernels: 3.33 us -> 0.44 us  [shards(): call(edge_kernel, (strip, strip, strip), [VMEM_SPEC])(block)]
  transfers between devices with their start and end apart: 7 -> 7, of which waited for: 3 -> 3; matrix products, arithmetic and copies ran while one was open for 3% -> 3% of each run, Pallas kernels for 37% -> 40%
where the time goes in v7:
time: 40.3 us; the launch traced here: 40.1 us
  Pallas kernels  17.2 us (43%)
  starting transfers between devices  13.9 us (34%)
  waiting for transfers between devices  6.22 us (15%)
  local copies, waits for them, and re-layouts  2.31 us (6%)
    pallas_call x2, Pallas kernels, shards(): call(functools.partial(physics_kernel, n, chans=chans), (whole, sds((chan...  10 us
    ppermute x4, waiting for transfers between devices, swap(): return lax.ppermute(x, 'group', [(0, 1), (1, 0)])  5.89 us
    pallas_call x2, Pallas kernels, transport(): call(functools.partial(transport_kernel, chans=chans, jobs=jobs, size=siz...  5.07 us
    ppermute x4, starting transfers between devices, swap(): return lax.ppermute(x, 'group', [(0, 1), (1, 0)])  4.69 us
    ppermute x1, starting transfers between devices, shards(): from_east = lax.ppermute(to_west, 'tile', beside(-1))  4.54 us
    ppermute x1, starting transfers between devices, across(): lax.ppermute(x, 'tile', [(i, (i + by) % tiles) for i in range(tiles)])  2.65 us
    ppermute x1, starting transfers between devices, shards(): from_west = lax.ppermute(to_east, 'tile', beside(1))  2.06 us
    pallas_call x2, Pallas kernels, shards(): call(functools.partial(finish_kernel, n, parts=parts), whole, [VMEM_SPEC,...  1.52 us
  transfers between devices with their start and end apart: 7, of which 3 were waited for; matrix products, arithmetic and copies ran while one was open for 3% of the time, Pallas kernels for 40%

profile of v7, /device:TPU:8, one launch (start us, length us, event | category | flops | bytes accessed | tf_op | source)
XLA Modules:
  0.0 40.1 jit_solution(4949606148292444073)
XLA Ops:
  0.0 0.0 copy-start
  0.0 1.3 %copy-done = f32[4,5,1,128,128]{4,3,2,1,0:T(8,128)S(1)} copy-done((f32[4,5,1,128,128]{4,3,2,1,0:T(8,128)S(1)}, f32[4,5,1,128,128]{4,3,2,1,0:T(8,128)}, u32[]{:S(2)}) %copy-start) | copy-done | bytes 1310744
  1.3 0.0 copy-start.6
  1.3 0.0 copy-start.5
  1.3 0.0 copy-start.4
  1.3 0.0 copy-start.3
  1.3 0.4 %shard_map.82 = (bf16[20,8,128]{2,1,0:T(8,128)(2,1)S(1)}, bf16[20,8,128]{2,1,0:T(8,128)(2,1)S(1)}, bf16[20,8,128]{2,1,0:T(8,128)(2,1)S(1)}) custom-call(f32[20,128,128]{2,1,0:T(8,128)S(1)} %bitcast.21), custom_call_target="tpu_custom_call" | custom-call | flops 1000000000 | bytes 1000000 | tf_op jit(solution)/shard_map/pallas_call | solution.py:391
  1.8 0.0 copy-start.7
  1.8 0.0 copy-start.8
  1.8 2.1 %collective-permute-start = (bf16[20,8,128]{2,1,0:T(8,128)(2,1)S(1)}, bf16[20,8,128]{2,1,0:T(8,128)(2,1)S(1)}, u32[]{:S(2)}, u32[]{:S(2)}) collective-permute-start(bf16[20,8,128]{2,1,0:T(8,128)(2,1)S(1)} %get-tuple-element.22), channel_id=1, source_target_pairs={{0,2},{2,4},{4,6},{6,8},{8,10},{10,12},{12,14},{16,18},{18,20},{20... | collective-permute-start | bytes 122888 | tf_op jit(solution)/shard_map/ppermute | solution.py:396
  3.8 4.5 %collective-permute-start.1 = (bf16[20,8,128]{2,1,0:T(8,128)(2,1)S(1)}, bf16[20,8,128]{2,1,0:T(8,128)(2,1)S(1)}, u32[]{:S(2)}, u32[]{:S(2)}) collective-permute-start(bf16[20,8,128]{2,1,0:T(8,128)(2,1)S(1)} %get-tuple-element.23), channel_id=1, source_target_pairs={{2,0},{4,2},{6,4},{8,6},{10,8},{12,10},{14,12},{18,16},{20,18},{22... | collective-permute-start | bytes 122888 | tf_op jit(solution)/shard_map/ppermute | solution.py:397
  8.4 0.0 copy-done.6
  8.4 0.0 copy-done.5
  8.4 0.0 copy-done.4
  8.5 0.1 copy.36
  8.6 0.0 copy-done.3
  8.6 0.1 reshape.175
  8.7 0.1 fusion
  8.8 0.0 copy-done.7
  8.8 0.0 copy-done.8
  8.8 0.1 broadcast_subtract_fusion
  8.9 0.1 sub.70
  9.0 0.1 sub.68
  9.1 0.1 add.33
  9.2 0.1 add.31
  9.2 0.1 sub.66
  9.4 0.1 copy.37
  9.5 0.1 copy.41
  9.6 0.1 copy.39.w1_ref
  9.7 0.0 collective-permute-done
  9.7 0.3 collective-permute-done.1
  10.0 0.0 copy-start.1
  10.0 0.1 shard_map.83
  10.2 2.7 %collective-permute-start.2 = (bf16[160,128]{1,0:T(8,128)(2,1)S(1)}, bf16[160,128]{1,0:T(8,128)(2,1)S(1)}, u32[]{:S(2)}, u32[]{:S(2)}) collective-permute-start(bf16[160,128]{1,0:T(8,128)(2,1)S(1)} %get-tuple-element.25), channel_id=1, source_target_pairs={{0,16},{2,18},{4,20},{6,22},{8,24},{10,26},{12,28},{14,30},{16,0},... | collective-permute-start | bytes 122888 | tf_op jit(solution)/shard_map/ppermute | solution.py:410
  12.8 0.0 copy-done.1
  12.8 1.5 %shard_map.85 = bf16[800,128]{1,0:T(8,128)(2,1)S(1)} custom-call(f32[20,128,128]{2,1,0:T(8,128)S(1)} %bitcast.22, f32[5,20]{1,0:T(8,128)S(1)} %stack.2.speed_ref, f32[20,5]{1,0:T(8,128)S(1)} %bitcast.19, f32[10,20,128]{2,1,0:T(8,128)S(1)} %get-tuple-element.24.column_ref), custom_call_target="tpu_custom_call" | custom-call | flops 5000000000 | bytes 1000000 | tf_op jit(solution)/shard_map/pallas_call | solution.py:435
  14.4 0.0 copy-start.2
  14.4 1.6 %collective-permute-start.4 = (bf16[800,128]{1,0:T(8,128)(2,1)S(1)}, bf16[800,128]{1,0:T(8,128)(2,1)S(1)}, u32[]{:S(2)}, u32[]{:S(2)}) collective-permute-start(bf16[800,128]{1,0:T(8,128)(2,1)S(1)} %shard_map.85), channel_id=1, source_target_pairs={{0,1},{1,0},{2,3},{3,2},{4,5},{5,4},{6,7},{7,6},{8,9},{9,8},{10,11... | collective-permute-start | bytes 614408 | tf_op jit(solution)/shard_map/ppermute | solution.py:454
  16.0 0.0 collective-permute-done.2.rest_0_.rest_1_
  16.0 3.6 %shard_map.84 = (bf16[800,128]{1,0:T(8,128)(2,1)S(1)}, bf16[800,128]{1,0:T(8,128)(2,1)S(1)}, bf16[800,128]{1,0:T(8,128)(2,1)S(1)}, f32[640,128]{1,0:T(8,128)S(1)...) custom-call(f32[20,128,128]{2,1,0:T(8,128)S(1)} %bitcast.23, ...), custom_call_target="tpu_custom_call" | custom-call | flops 5000000000 | bytes 1000000 | tf_op jit(solution)/shard_map/pallas_call | solution.py:435
  19.5 0.9 %collective-permute-start.3 = (bf16[800,128]{1,0:T(8,128)(2,1)S(1)}, bf16[800,128]{1,0:T(8,128)(2,1)S(1)}, u32[]{:S(2)}, u32[]{:S(2)}) collective-permute-start(bf16[800,128]{1,0:T(8,128)(2,1)S(1)} %get-tuple-element.27), channel_id=1, source_target_pairs={{0,1},{1,0},{2,3},{3,2},{4,5},{5,4},{6,7},{7,6},{8,9},{9,8},{10,11... | collective-permute-start | bytes 614408 | tf_op jit(solution)/shard_map/ppermute | solution.py:454
  20.5 1.4 %collective-permute-done.4.got_ref = bf16[800,128]{1,0:T(8,128)(2,1)S(1)} collective-permute-done((bf16[800,128]{1,0:T(8,128)(2,1)S(1)}, bf16[800,128]{1,0:T(8,128)(2,1)S(1)}, u32[]{:S(2)}, u32[]{:S(2)}) %collective-permute-start.4) | collective-permute-done | bytes 204832 | tf_op jit(solution)/shard_map/ppermute | solution.py:454
  21.9 0.0 copy-done.2
  21.9 5.0 %shard_map.86 = (f32[20,128,128]{2,1,0:T(8,128)}, bf16[640,128]{1,0:T(8,128)(2,1)S(1)}) custom-call(s32[9,1,128,128]{3,2,1,0:T(8,128)S(1)} %copy-done.2, bf16[256,432]{1,0:T(8,128)(2,1)S(1)} %copy.39.w1_ref, bf16[256,256]{1,0:T(8,128)(2,1)S(1)} %multiply_bitcast_fusion.w2_ref, bf16[48,256]{1,0:T(8,128)(2,1)S(1)} %bitcast.17, ...), custom_call_target="tpu_custom_call" | custom-call | flops 7000000000 | bytes 1000000 | tf_op jit(solution)/shard_map/pallas_call | solution.py:479
  26.9 2.0 %collective-permute-start.6 = (bf16[640,128]{1,0:T(8,128)(2,1)S(1)}, bf16[640,128]{1,0:T(8,128)(2,1)S(1)}, u32[]{:S(2)}, u32[]{:S(2)}) collective-permute-start(bf16[640,128]{1,0:T(8,128)(2,1)S(1)} %get-tuple-element.34), channel_id=1, source_target_pairs={{0,1},{1,0},{2,3},{3,2},{4,5},{5,4},{6,7},{7,6},{8,9},{9,8},{10,11... | collective-permute-start | bytes 491528 | tf_op jit(solution)/shard_map/ppermute | solution.py:454
  28.9 0.0 collective-permute-done.3.got_ref
  28.9 5.0 %shard_map.87 = (f32[20,128,128]{2,1,0:T(8,128)}, bf16[640,128]{1,0:T(8,128)(2,1)S(1)}) custom-call(s32[9,1,128,128]{3,2,1,0:T(8,128)S(1)} %copy-done.2, bf16[256,432]{1,0:T(8,128)(2,1)S(1)} %copy.39.w1_ref, bf16[256,256]{1,0:T(8,128)(2,1)S(1)} %multiply_bitcast_fusion.w2_ref, bf16[48,256]{1,0:T(8,128)(2,1)S(1)} %bitcast.18, ...), custom_call_target="tpu_custom_call", output_to_operand_aliasing={{0}: (7, {})} | custom-call | flops 7000000000 | bytes 1000000 | tf_op jit(solution)/shard_map/pallas_call | solution.py:479
  34.0 0.1 collective-permute-start.5
  34.1 0.0 collective-permute-done.6.back_ref
  34.1 0.8 %shard_map.88.image_in = f32[20,128,128]{2,1,0:T(8,128)} custom-call(bf16[640,128]{1,0:T(8,128)(2,1)S(1)} %collective-permute-done.6.back_ref, f32[640,128]{1,0:T(8,128)S(1)} %get-tuple-element.35.moved_ref, f32[20,128,128]{2,1,0:T(8,128)} %get-tuple-element.36.image_in), custom_call_target="tpu_custom_call", output_to_operand_aliasing={{}: (2, {})} | custom-call | flops 1000000000 | bytes 1000000 | tf_op jit(solution)/shard_map/pallas_call | solution.py:502
  34.8 4.5 %collective-permute-done.5.back_ref = bf16[640,128]{1,0:T(8,128)(2,1)S(1)} collective-permute-done((bf16[640,128]{1,0:T(8,128)(2,1)S(1)}, bf16[640,128]{1,0:T(8,128)(2,1)S(1)}, u32[]{:S(2)}, u32[]{:S(2)}) %collective-permute-start.5) | collective-permute-done | bytes 163872 | tf_op jit(solution)/shard_map/ppermute | solution.py:454
  39.3 0.8 %shard_map.89 = f32[20,128,128]{2,1,0:T(8,128)} custom-call(bf16[640,128]{1,0:T(8,128)(2,1)S(1)} %collective-permute-done.5.back_ref, f32[640,128]{1,0:T(8,128)S(1)} %get-tuple-element.33.moved_ref, f32[20,128,128]{2,1,0:T(8,128)} %shard_map.88.image_in), custom_call_target="tpu_custom_call", output_to_operand_aliasing={{}: (2, {})} | custom-call | flops 1000000000 | bytes 1000000 | tf_op jit(solution)/shard_map/pallas_call | solution.py:502
  (9 shorter events, 0.1 us)
Async XLA Ops:
  0.0 1.3 %copy-start = (f32[4,5,1,128,128]{4,3,2,1,0:T(8,128)S(1)}, f32[4,5,1,128,128]{4,3,2,1,0:T(8,128)}, u32[]{:S(2)}) copy-start(f32[4,5,1,128,128]{4,3,2,1,0:T(8,128)} %param.8) | copy-start | bytes 3932164
  1.3 7.1 %copy-start.6 = (f32[5]{0:T(128)S(1)}, f32[5]{0:T(128)}, u32[]{:S(2)}) copy-start(f32[5]{0:T(128)} %param.11) | copy-start | bytes 64
  1.3 7.1 %copy-start.5 = (bf16[256,40]{0,1:T(8,128)(2,1)S(1)}, bf16[256,40]{0,1:T(8,128)(2,1)}, u32[]{:S(2)}) copy-start(bf16[256,40]{0,1:T(8,128)(2,1)} %param.15) | copy-start | bytes 61444
  1.3 7.1 %copy-start.4 = (bf16[256,256]{1,0:T(8,128)(2,1)S(1)}, bf16[256,256]{1,0:T(8,128)(2,1)}, u32[]{:S(2)}) copy-start(bf16[256,256]{1,0:T(8,128)(2,1)} %param.14) | copy-start | bytes 393220
  1.3 7.3 %copy-start.3 = (bf16[360,256]{1,0:T(8,128)(2,1)S(1)}, bf16[360,256]{1,0:T(8,128)(2,1)}, u32[]{:S(2)}) copy-start(bf16[360,256]{1,0:T(8,128)(2,1)} %param.13) | copy-start | bytes 552964
  1.8 7.0 %copy-start.7 = (f32[4]{0:T(128)S(1)}, f32[4]{0:T(128)}, u32[]{:S(2)}) copy-start(f32[4]{0:T(128)} %param.10) | copy-start | bytes 52
  1.8 7.0 %copy-start.8 = (f32[4]{0:T(128)S(1)}, f32[4]{0:T(128)}, u32[]{:S(2)}) copy-start(f32[4]{0:T(128)} %param.9) | copy-start | bytes 52
  1.8 7.9 %collective-permute-start = (bf16[20,8,128]{2,1,0:T(8,128)(2,1)S(1)}, bf16[20,8,128]{2,1,0:T(8,128)(2,1)S(1)}, u32[]{:S(2)}, u32[]{:S(2)}) collective-permute-start(bf16[20,8,128]{2,1,0:T(8,128)(2,1)S(1)} %get-tuple-element.22), channel_id=1, source_target_pairs={{0,2},{2,4},{4,6},{6,8},{8,10},{10,12},{12,14},{16,18},{18,20},{20... | collective-permute-start | bytes 122888 | tf_op jit(solution)/shard_map/ppermute | solution.py:396
  3.8 6.2 %collective-permute-start.1 = (bf16[20,8,128]{2,1,0:T(8,128)(2,1)S(1)}, bf16[20,8,128]{2,1,0:T(8,128)(2,1)S(1)}, u32[]{:S(2)}, u32[]{:S(2)}) collective-permute-start(bf16[20,8,128]{2,1,0:T(8,128)(2,1)S(1)} %get-tuple-element.23), channel_id=1, source_target_pairs={{2,0},{4,2},{6,4},{8,6},{10,8},{12,10},{14,12},{18,16},{20,18},{22... | collective-permute-start | bytes 122888 | tf_op jit(solution)/shard_map/ppermute | solution.py:397
  10.0 2.8 %copy-start.1 = (f32[4,5,1,128,128]{4,3,2,1,0:T(8,128)S(1)}, f32[4,5,1,128,128]{4,3,2,1,0:T(8,128)}, u32[]{:S(2)}) copy-start(f32[4,5,1,128,128]{4,3,2,1,0:T(8,128)} %param.8) | copy-start | bytes 3932164
  10.2 5.8 %collective-permute-start.2 = (bf16[160,128]{1,0:T(8,128)(2,1)S(1)}, bf16[160,128]{1,0:T(8,128)(2,1)S(1)}, u32[]{:S(2)}, u32[]{:S(2)}) collective-permute-start(bf16[160,128]{1,0:T(8,128)(2,1)S(1)} %get-tuple-element.25), channel_id=1, source_target_pairs={{0,16},{2,18},{4,20},{6,22},{8,24},{10,26},{12,28},{14,30},{16,0},... | collective-permute-start | bytes 122888 | tf_op jit(solution)/shard_map/ppermute | solution.py:410
  14.4 7.5 %copy-start.2 = (s32[9,1,128,128]{3,2,1,0:T(8,128)S(1)}, s32[9,1,128,128]{3,2,1,0:T(8,128)}, u32[]{:S(2)}) copy-start(s32[9,1,128,128]{3,2,1,0:T(8,128)} %table_ref.3) | copy-start | bytes 1769476
  14.4 7.5 %collective-permute-start.4 = (bf16[800,128]{1,0:T(8,128)(2,1)S(1)}, bf16[800,128]{1,0:T(8,128)(2,1)S(1)}, u32[]{:S(2)}, u32[]{:S(2)}) collective-permute-start(bf16[800,128]{1,0:T(8,128)(2,1)S(1)} %shard_map.85), channel_id=1, source_target_pairs={{0,1},{1,0},{2,3},{3,2},{4,5},{5,4},{6,7},{7,6},{8,9},{9,8},{10,11... | collective-permute-start | bytes 614408 | tf_op jit(solution)/shard_map/ppermute | solution.py:454
  19.5 9.4 %collective-permute-start.3 = (bf16[800,128]{1,0:T(8,128)(2,1)S(1)}, bf16[800,128]{1,0:T(8,128)(2,1)S(1)}, u32[]{:S(2)}, u32[]{:S(2)}) collective-permute-start(bf16[800,128]{1,0:T(8,128)(2,1)S(1)} %get-tuple-element.27), channel_id=1, source_target_pairs={{0,1},{1,0},{2,3},{3,2},{4,5},{5,4},{6,7},{7,6},{8,9},{9,8},{10,11... | collective-permute-start | bytes 614408 | tf_op jit(solution)/shard_map/ppermute | solution.py:454
  26.9 7.2 %collective-permute-start.6 = (bf16[640,128]{1,0:T(8,128)(2,1)S(1)}, bf16[640,128]{1,0:T(8,128)(2,1)S(1)}, u32[]{:S(2)}, u32[]{:S(2)}) collective-permute-start(bf16[640,128]{1,0:T(8,128)(2,1)S(1)} %get-tuple-element.34), channel_id=1, source_target_pairs={{0,1},{1,0},{2,3},{3,2},{4,5},{5,4},{6,7},{7,6},{8,9},{9,8},{10,11... | collective-permute-start | bytes 491528 | tf_op jit(solution)/shard_map/ppermute | solution.py:454
  34.0 5.4 %collective-permute-start.5 = (bf16[640,128]{1,0:T(8,128)(2,1)S(1)}, bf16[640,128]{1,0:T(8,128)(2,1)S(1)}, u32[]{:S(2)}, u32[]{:S(2)}) collective-permute-start(bf16[640,128]{1,0:T(8,128)(2,1)S(1)} %get-tuple-element.32), channel_id=1, source_target_pairs={{0,1},{1,0},{2,3},{3,2},{4,5},{5,4},{6,7},{7,6},{8,9},{9,8},{10,11... | collective-permute-start | bytes 491528 | tf_op jit(solution)/shard_map/ppermute | solution.py:454

commit v8 on v7

--- a/solution.py
+++ b/solution.py
@@ -48,7 +48,9 @@
         ).astype(BF16)
 
 
-def pack_kernel(rows_ref, west_in, east_in, west_own, east_own, out_ref, column_ref, wide, *, chans):
+def pack_kernel(
+    rows_ref, west_in, east_in, west_own, east_own, coef_ref, out_ref, column_ref, wide_ref, wide, *, chans
+):
     width = rows_ref.shape[1]
     lane = lanes_of((chans, width))
     for n, ref in enumerate((rows_ref, west_in, east_in, west_own, east_own)):
@@ -62,6 +64,8 @@
         corner = jnp.where(
             (lane >= at) & (lane < at + 2 * DEEP), pltpu.roll(line, at + DEEP, 1), corner
         )
+    for n in range(wide_ref.shape[0]):
+        wide_ref[n] = jnp.broadcast_to(coef_ref[:, n : n + 1], (chans, width))
     wide[0, pl.ds(2 * DEEP, chans, stride=8), :] = corner
     out_ref[...] = wide[0].astype(BF16)
 
@@ -77,7 +81,7 @@
     return jnp.where(((k < 2 * width) & (lower | upper)) | west | east, 1.0, 0.0).astype(BF16)
 
 
-def transport_kernel(state_ref, speed_ref, coef_ref, column_ref, *rest, chans, jobs, size, ahead):
+def transport_kernel(state_ref, coef_ref, column_ref, *rest, chans, jobs, size, ahead):
     count = len(jobs)
     halos, rest = ((), rest) if ahead else (rest[:2], rest[2:])
     packets, rest = rest[:count], rest[count:]
@@ -98,7 +102,7 @@
     low_lanes = lane < width // 2
     for s, ref in enumerate(halos):
         border[s] = ref[...].astype(F32)
-    coefs = [jnp.broadcast_to(coef_ref[:, n : n + 1], (chans, width)) for n in range(5)]
+    coefs = [coef_ref[n] for n in range(5)]
     message = border.shape[1] // chans
 
     if ahead:
@@ -191,7 +195,7 @@
         for g in range(group):
             c = base + g
             lower, upper = near[g * rows : (g + 1) * rows, :width], near[g * rows : (g + 1) * rows, width:]
-            c0, cxl, cxu, cyl, cyu = [speed_ref[n, c] for n in range(5)]
+            c0, cxl, cxu, cyl, cyu = [coef_ref[n, pl.ds(c, 1), :] for n in range(5)]
             dst[c, pl.ds(top, rows), :] = (
                 c0 * src[c, pl.ds(near_top, rows), :]
                 + cxl * src[c, pl.ds(near_top - 1, rows), :]
@@ -226,10 +230,10 @@
         packet[...] = window[...].astype(BF16)
 
 
-def physics_kernel(chunk, table_ref, w1_ref, w2_ref, w3_ref, mine_ref, got_ref, kept_ref, *rest, chans):
-    (
-        image_ref, other_ref, wide, packed, mask, table, even, odd, terms, patch, got, sem
-    ) = rest[-12:]
+def physics_kernel(
+    chunk, table_ref, w1_ref, w2_ref, w3_ref, mine_ref, got_ref, kept_ref, *rest, chans
+):
+    own_ref, other_ref, wide, packed, mask, table, even, odd, terms, sem = rest[-10:]
     size, width = table.shape[1:]
     height = EXTRA + size
     pad = -(-chans // 8) * 8
@@ -239,10 +243,8 @@
         pltpu.make_async_copy(table_ref.at[k, 0, pl.ds(top, size)], table.at[n], sem.at[n])
         for n, k in enumerate((5, 7))
     ]
-    arrive = pltpu.make_async_copy(got_ref, got, sem.at[2])
     for copy in copies:
         copy.start()
-    arrive.start()
 
     k = lax.broadcasted_iota(jnp.int32, (2 * width, 2 * width), 0)
     n = lax.broadcasted_iota(jnp.int32, (2 * width, 2 * width), 1)
@@ -255,9 +257,7 @@
         slot >= EXTRA, slot - EXTRA + 1, jnp.where(slot == 0, 0, jnp.where(slot == 1, size + 1, -1))
     )
     diagonal = lanes_of((height, width)) % (width // 2) == line
-    for s, ref in enumerate((mine_ref, got)):
-        if s == 1:
-            arrive.wait()
+    for s, ref in enumerate((mine_ref, got_ref)):
         cells = ref[...]
         flat = cells.astype(F32)
         wide[1, s, pl.ds(0, chans * height)] = flat
@@ -345,17 +345,21 @@
             stack(n + 1, slots[(n + 1) % 2])
         network(n, slots[n % 2])
     other_ref[...] = terms[1].astype(BF16)
-    patch[...] = (kept_ref[...] + terms[0]).reshape(patch.shape)
-    put = pltpu.make_async_copy(patch, image_ref.at[:, pl.ds(top, size)], sem.at[3])
-    put.start()
-    put.wait()
-
-
-def finish_kernel(chunk, back_ref, moved_ref, image_in, image_ref, patch, sem, *, parts):
+    own_ref[...] = kept_ref[...] + terms[0]
+
+
+def finish_kernel(chunk, back_ref, moved_ref, *rest, parts):
+    image_ref, patch, sem = rest[-3:]
     chans, size, width = patch.shape
-    rows = pl.ds(first_row(1 - lax.axis_index("group"), chunk, size), size)
+    own = lax.axis_index("group")
+    put = []
+    if chunk == 0:
+        for n in range(2):
+            rows = pl.ds(first_row(own, n, size), size)
+            put.append(pltpu.make_async_copy(rest[n], image_ref.at[:, rows], sem.at[parts + n]))
+            put[-1].start()
+    rows = pl.ds(first_row(1 - own, chunk, size), size)
     some = chans // parts
-    put = []
     for n in range(parts):
         c, r = pl.ds(n * some, some), pl.ds(n * some * size, some * size)
         patch[c] = (moved_ref[r] + back_ref[r].astype(F32)).reshape(some, size, width)
@@ -398,19 +402,6 @@
 
     def flat(x):
         return x.reshape(-1, cells_y)
-
-    message, columns = call(
-        functools.partial(pack_kernel, chans=chans),
-        (sds((chans * 8, cells_y), BF16), sds((10, chans, cells_y), F32)),
-        [VMEM_SPEC] * 5,
-        [pltpu.VMEM((5, chans * 8, cells_y), F32)],
-    )(flat(rows), flat(from_west), flat(from_east), flat(to_west), flat(to_east))
-
-    def across(x, by):
-        return lax.ppermute(x, "tile", [(i, (i + by) % tiles) for i in range(tiles)])
-
-    up = across(message, TILE_ROWS)
-    down = up if tiles == 2 * TILE_ROWS else across(message, -TILE_ROWS)
 
     ax = jnp.repeat(courant_x, fields)
     ay = jnp.repeat(courant_y, fields)
@@ -425,6 +416,23 @@
         ]
     )
 
+    message, columns, wide_coef = call(
+        functools.partial(pack_kernel, chans=chans),
+        (
+            sds((chans * 8, cells_y), BF16),
+            sds((10, chans, cells_y), F32),
+            sds((5, chans, cells_y), F32),
+        ),
+        [VMEM_SPEC] * 6,
+        [pltpu.VMEM((5, chans * 8, cells_y), F32)],
+    )(flat(rows), flat(from_west), flat(from_east), flat(to_west), flat(to_east), coef.T)
+
+    def across(x, by):
+        return lax.ppermute(x, "tile", [(i, (i + by) % tiles) for i in range(tiles)])
+
+    up = across(message, TILE_ROWS)
+    down = up if tiles == 2 * TILE_ROWS else across(message, -TILE_ROWS)
+
     size = cells_x // 4
     tall = pltpu.VMEM((chans, cells_x + 2 * MARGIN, cells_y), F32)
     height = chans * (EXTRA + size)
@@ -435,8 +443,7 @@
         return call(
             functools.partial(transport_kernel, chans=chans, jobs=jobs, size=size, ahead=ahead),
             (sds((height, cells_y), BF16),) * len(jobs) + (() if ahead else (moved,) * 4),
-            [VMEM_SPEC if ahead else ANY_SPEC, pl.BlockSpec(memory_space=pltpu.SMEM)]
-            + [VMEM_SPEC] * (2 + len(halos)),
+            [VMEM_SPEC if ahead else ANY_SPEC] + [VMEM_SPEC] * (2 + len(halos)),
             [pltpu.VMEM((height, cells_y), F32) for _ in jobs]
             + [
                 pltpu.VMEM((2, chans * 8, cells_y), F32),
@@ -448,7 +455,7 @@
                 pltpu.SemaphoreType.DMA((1,)),
             ],
             flops=5 * 10**9,
-        )(block, coef, coef.T, columns, *halos)
+        )(block, wide_coef, columns, *halos)
 
     def swap(x):
         return lax.ppermute(x, "group", [(0, 1), (1, 0)])
@@ -470,16 +477,13 @@
     w3 = jnp.pad(w3, ((0, 0), (0, pad - chans), (0, 0))).reshape(both, hidden)
     w2 = (w_mid * 0.5).T
 
-    back = []
-    image = None
+    back, owned = [], []
     blocks = pltpu.VMEM((9 * both, BLOCK_ROWS * cells_y), BF16)
-    whole = sds((chans, cells_x, cells_y), F32)
     for n in range(2):
-        images = () if image is None else (image,)
-        image, other = call(
+        mixed, other = call(
             functools.partial(physics_kernel, n, chans=chans),
-            (whole, sds((chans * size, cells_y), BF16)),
-            [ANY_SPEC] + [VMEM_SPEC] * 4 + [ANY_SPEC, VMEM_SPEC] + [ANY_SPEC] * len(images),
+            (moved, sds((chans * size, cells_y), BF16)),
+            [ANY_SPEC] + [VMEM_SPEC] * 6 + [ANY_SPEC] * n,
             [
                 pltpu.VMEM((3, 2, pad * (EXTRA + size), cells_y), F32),
                 pltpu.VMEM((3, size + 2, both, cells_y), BF16),
@@ -488,26 +492,32 @@
                 blocks,
                 blocks,
                 pltpu.VMEM((2, chans * size, cells_y), F32),
-                pltpu.VMEM((chans, size, cells_y), F32),
-                pltpu.VMEM((height, cells_y), BF16),
-                pltpu.SemaphoreType.DMA((4,)),
+                pltpu.SemaphoreType.DMA((2,)),
             ],
             flops=7 * 10**9,
-            out_specs=(ANY_SPEC, VMEM_SPEC),
-            aliases={7: 0} if images else {},
-        )(neighbours, w1, w2, w3, mine[n], got[n], kept[n], *images)
+        )(neighbours, w1, w2, w3, mine[n], got[n], kept[n], *owned)
+        owned.append(mixed)
         back.append(swap(other))
+    owned = [x.reshape(chans, size, cells_y) for x in owned]
     parts = 4 if chans % 4 == 0 else 1
-    for n in range(2):
-        image = call(
-            functools.partial(finish_kernel, n, parts=parts),
-            whole,
-            [VMEM_SPEC, VMEM_SPEC, ANY_SPEC],
-            [pltpu.VMEM((chans, size, cells_y), F32), pltpu.SemaphoreType.DMA((parts,))],
-            out_specs=ANY_SPEC,
-            aliases={2: 0},
-            limit=4,
-        )(back[n], others[n], image)
+    whole = sds((chans, cells_x, cells_y), F32)
+    image = call(
+        functools.partial(finish_kernel, 0, parts=parts),
+        whole,
+        [VMEM_SPEC] * 4,
+        [pltpu.VMEM((chans, size, cells_y), F32), pltpu.SemaphoreType.DMA((parts + 2,))],
+        out_specs=ANY_SPEC,
+        limit=4,
+    )(back[0], others[0], *owned)
+    image = call(
+        functools.partial(finish_kernel, 1, parts=parts),
+        whole,
+        [VMEM_SPEC, VMEM_SPEC, ANY_SPEC],
+        [pltpu.VMEM((chans, size, cells_y), F32), pltpu.SemaphoreType.DMA((parts,))],
+        out_specs=ANY_SPEC,
+        aliases={2: 0},
+        limit=4,
+    )(back[1], others[1], image)
     return image.reshape(levels, fields, single, cells_x, cells_y)
 
 

time: 40.3 us -> 37.1 us (0.921)
  Pallas kernels: 17.2 us -> 13.6 us
  starting transfers between devices: 13.9 us -> 14.6 us
    pallas_call x4, Pallas kernels: 11.5 us -> 9.22 us  [the longest x2 7.46 us: shards(): call(functools.partial(physics_kernel, n, chans=chans), (moved, sds((chan...]
    pallas_call x2, Pallas kernels: 5.07 us -> 3.8 us  [transport(): call(functools.partial(transport_kernel, chans=chans, jobs=jobs, size=siz...]
    ppermute x4, starting transfers between devices: 4.69 us -> 5.34 us  [swap(): return lax.ppermute(x, 'group', [(0, 1), (1, 0)])]
  transfers between devices with their start and end apart: 7 -> 7, of which waited for: 3 -> 3; matrix products, arithmetic and copies ran while one was open for 3% -> 3% of each run, Pallas kernels for 40% -> 33%
where the time goes in v8:
time: 37.1 us; the launch traced here: 36.9 us
  starting transfers between devices  14.6 us (39%)
  Pallas kernels  13.6 us (37%)
  waiting for transfers between devices  5.97 us (16%)
  local copies, waits for them, and re-layouts  2.31 us (6%)
    pallas_call x2, Pallas kernels, shards(): call(functools.partial(physics_kernel, n, chans=chans), (moved, sds((chan...  7.46 us
    ppermute x4, waiting for transfers between devices, swap(): return lax.ppermute(x, 'group', [(0, 1), (1, 0)])  5.64 us
    ppermute x4, starting transfers between devices, swap(): return lax.ppermute(x, 'group', [(0, 1), (1, 0)])  5.34 us
    ppermute x1, starting transfers between devices, shards(): from_east = lax.ppermute(to_west, 'tile', beside(-1))  4.54 us
    pallas_call x2, Pallas kernels, transport(): call(functools.partial(transport_kernel, chans=chans, jobs=jobs, size=siz...  3.8 us
    ppermute x1, starting transfers between devices, across(): lax.ppermute(x, 'tile', [(i, (i + by) % tiles) for i in range(tiles)])  2.65 us
    ppermute x1, starting transfers between devices, shards(): from_west = lax.ppermute(to_east, 'tile', beside(1))  2.06 us
    unnamed x20, local copies, waits for them, and re-layouts  1.51 us
  transfers between devices with their start and end apart: 7, of which 3 were waited for; matrix products, arithmetic and copies ran while one was open for 3% of the time, Pallas kernels for 33%

profile of v8, /device:TPU:8, one launch (start us, length us, event | category | flops | bytes accessed | tf_op | source)
XLA Modules:
  0.0 36.9 jit_solution(1382179740003640965)
XLA Ops:
  0.0 0.0 copy-start
  0.0 1.3 %copy-done = f32[4,5,1,128,128]{4,3,2,1,0:T(8,128)S(1)} copy-done((f32[4,5,1,128,128]{4,3,2,1,0:T(8,128)S(1)}, f32[4,5,1,128,128]{4,3,2,1,0:T(8,128)}, u32[]{:S(2)}) %copy-start) | copy-done | bytes 1310744
  1.3 0.0 copy-start.6
  1.3 0.0 copy-start.5
  1.3 0.0 copy-start.4
  1.3 0.0 copy-start.3
  1.3 0.4 %shard_map.82 = (bf16[20,8,128]{2,1,0:T(8,128)(2,1)S(1)}, bf16[20,8,128]{2,1,0:T(8,128)(2,1)S(1)}, bf16[20,8,128]{2,1,0:T(8,128)(2,1)S(1)}) custom-call(f32[20,128,128]{2,1,0:T(8,128)S(1)} %bitcast.22), custom_call_target="tpu_custom_call" | custom-call | flops 1000000000 | bytes 1000000 | tf_op jit(solution)/shard_map/pallas_call | solution.py:395
  1.8 0.0 copy-start.7
  1.8 0.0 copy-start.8
  1.8 2.1 %collective-permute-start = (bf16[20,8,128]{2,1,0:T(8,128)(2,1)S(1)}, bf16[20,8,128]{2,1,0:T(8,128)(2,1)S(1)}, u32[]{:S(2)}, u32[]{:S(2)}) collective-permute-start(bf16[20,8,128]{2,1,0:T(8,128)(2,1)S(1)} %get-tuple-element.23), channel_id=1, source_target_pairs={{0,2},{2,4},{4,6},{6,8},{8,10},{10,12},{12,14},{16,18},{18,20},{20... | collective-permute-start | bytes 122888 | tf_op jit(solution)/shard_map/ppermute | solution.py:400
  3.8 4.5 %collective-permute-start.1 = (bf16[20,8,128]{2,1,0:T(8,128)(2,1)S(1)}, bf16[20,8,128]{2,1,0:T(8,128)(2,1)S(1)}, u32[]{:S(2)}, u32[]{:S(2)}) collective-permute-start(bf16[20,8,128]{2,1,0:T(8,128)(2,1)S(1)} %get-tuple-element.24), channel_id=1, source_target_pairs={{2,0},{4,2},{6,4},{8,6},{10,8},{12,10},{14,12},{18,16},{20,18},{22... | collective-permute-start | bytes 122888 | tf_op jit(solution)/shard_map/ppermute | solution.py:401
  8.4 0.0 copy-done.6
  8.4 0.0 copy-done.5
  8.4 0.0 copy-done.4
  8.5 0.1 copy.30
  8.6 0.0 copy-done.3
  8.6 0.1 reshape.181
  8.7 0.1 fusion
  8.8 0.0 copy-done.7
  8.8 0.0 copy-done.8
  8.8 0.1 broadcast_subtract_fusion
  8.9 0.1 sub.70
  9.0 0.1 sub.68
  9.1 0.1 add.33
  9.2 0.1 add.31
  9.2 0.1 sub.66
  9.4 0.1 copy.31
  9.5 0.1 copy.35
  9.6 0.1 copy.33.w1_ref
  9.7 0.0 collective-permute-done
  9.7 0.3 collective-permute-done.1
  10.0 0.0 copy-start.1
  10.0 0.1 shard_map.83
  10.2 2.7 %collective-permute-start.2 = (bf16[160,128]{1,0:T(8,128)(2,1)S(1)}, bf16[160,128]{1,0:T(8,128)(2,1)S(1)}, u32[]{:S(2)}, u32[]{:S(2)}) collective-permute-start(bf16[160,128]{1,0:T(8,128)(2,1)S(1)} %get-tuple-element.27), channel_id=1, source_target_pairs={{0,16},{2,18},{4,20},{6,22},{8,24},{10,26},{12,28},{14,30},{16,0},... | collective-permute-start | bytes 122888 | tf_op jit(solution)/shard_map/ppermute | solution.py:431
  12.8 0.0 copy-done.1
  12.8 0.9 %shard_map.85 = bf16[800,128]{1,0:T(8,128)(2,1)S(1)} custom-call(f32[20,128,128]{2,1,0:T(8,128)S(1)} %bitcast.23, f32[5,20,128]{2,1,0:T(8,128)S(1)} %get-tuple-element.25.coef_ref, f32[10,20,128]{2,1,0:T(8,128)S(1)} %get-tuple-element.26.column_ref), custom_call_target="tpu_custom_call" | custom-call | flops 5000000000 | bytes 1000000 | tf_op jit(solution)/shard_map/pallas_call | solution.py:443
  13.7 0.0 copy-start.2
  13.8 1.6 %collective-permute-start.4 = (bf16[800,128]{1,0:T(8,128)(2,1)S(1)}, bf16[800,128]{1,0:T(8,128)(2,1)S(1)}, u32[]{:S(2)}, u32[]{:S(2)}) collective-permute-start(bf16[800,128]{1,0:T(8,128)(2,1)S(1)} %shard_map.85), channel_id=1, source_target_pairs={{0,1},{1,0},{2,3},{3,2},{4,5},{5,4},{6,7},{7,6},{8,9},{9,8},{10,11... | collective-permute-start | bytes 614408 | tf_op jit(solution)/shard_map/ppermute | solution.py:461
  15.3 0.0 collective-permute-done.2.rest_0_.rest_1_
  15.3 2.9 %shard_map.84 = (bf16[800,128]{1,0:T(8,128)(2,1)S(1)}, bf16[800,128]{1,0:T(8,128)(2,1)S(1)}, bf16[800,128]{1,0:T(8,128)(2,1)S(1)}, f32[640,128]{1,0:T(8,128)S(1)...) custom-call(f32[20,128,128]{2,1,0:T(8,128)S(1)} %bitcast.24, ...), custom_call_target="tpu_custom_call" | custom-call | flops 5000000000 | bytes 1000000 | tf_op jit(solution)/shard_map/pallas_call | solution.py:443
  18.3 1.6 %collective-permute-start.3 = (bf16[800,128]{1,0:T(8,128)(2,1)S(1)}, bf16[800,128]{1,0:T(8,128)(2,1)S(1)}, u32[]{:S(2)}, u32[]{:S(2)}) collective-permute-start(bf16[800,128]{1,0:T(8,128)(2,1)S(1)} %get-tuple-element.29), channel_id=1, source_target_pairs={{0,1},{1,0},{2,3},{3,2},{4,5},{5,4},{6,7},{7,6},{8,9},{9,8},{10,11... | collective-permute-start | bytes 614408 | tf_op jit(solution)/shard_map/ppermute | solution.py:461
  19.9 1.5 %collective-permute-done.4.got_ref = bf16[800,128]{1,0:T(8,128)(2,1)S(1)} collective-permute-done((bf16[800,128]{1,0:T(8,128)(2,1)S(1)}, bf16[800,128]{1,0:T(8,128)(2,1)S(1)}, u32[]{:S(2)}, u32[]{:S(2)}) %collective-permute-start.4) | collective-permute-done | bytes 204832 | tf_op jit(solution)/shard_map/ppermute | solution.py:461
  21.4 0.0 copy-done.2
  21.4 3.8 %shard_map.86 = (f32[640,128]{1,0:T(8,128)S(1)}, bf16[640,128]{1,0:T(8,128)(2,1)S(1)}) custom-call(s32[9,1,128,128]{3,2,1,0:T(8,128)S(1)} %copy-done.2, bf16[256,432]{1,0:T(8,128)(2,1)S(1)} %copy.33.w1_ref, bf16[256,256]{1,0:T(8,128)(2,1)S(1)} %multiply_bitcast_fusion.w2_ref, bf16[48,256]{1,0:T(8,128)(2,1)S(1)} %bitcast.19, ...), custom_call_target="tpu_custom_call" | custom-call | flops 7000000000 | bytes 1000000 | tf_op jit(solution)/shard_map/pallas_call | solution.py:483
  25.1 1.9 %collective-permute-start.6 = (bf16[640,128]{1,0:T(8,128)(2,1)S(1)}, bf16[640,128]{1,0:T(8,128)(2,1)S(1)}, u32[]{:S(2)}, u32[]{:S(2)}) collective-permute-start(bf16[640,128]{1,0:T(8,128)(2,1)S(1)} %get-tuple-element.36), channel_id=1, source_target_pairs={{0,1},{1,0},{2,3},{3,2},{4,5},{5,4},{6,7},{7,6},{8,9},{9,8},{10,11... | collective-permute-start | bytes 491528 | tf_op jit(solution)/shard_map/ppermute | solution.py:461
  27.1 0.0 collective-permute-done.3.got_ref
  27.1 3.7 %shard_map.87 = (f32[640,128]{1,0:T(8,128)S(1)}, bf16[640,128]{1,0:T(8,128)(2,1)S(1)}) custom-call(s32[9,1,128,128]{3,2,1,0:T(8,128)S(1)} %copy-done.2, bf16[256,432]{1,0:T(8,128)(2,1)S(1)} %copy.33.w1_ref, bf16[256,256]{1,0:T(8,128)(2,1)S(1)} %multiply_bitcast_fusion.w2_ref, bf16[48,256]{1,0:T(8,128)(2,1)S(1)} %bitcast.20, ...), custom_call_target="tpu_custom_call" | custom-call | flops 7000000000 | bytes 1000000 | tf_op jit(solution)/shard_map/pallas_call | solution.py:483
  30.8 0.3 collective-permute-start.5
  31.0 0.0 collective-permute-done.6.back_ref
  31.0 1.0 %shard_map.88.rest_0_ = f32[20,128,128]{2,1,0:T(8,128)} custom-call(bf16[640,128]{1,0:T(8,128)(2,1)S(1)} %collective-permute-done.6.back_ref, f32[640,128]{1,0:T(8,128)S(1)} %get-tuple-element.37.moved_ref, f32[20,32,128]{2,1,0:T(8,128)S(1)} %bitcast.29, f32[20,32,128]{2,1,0:T(8,128)S(1)} %bitcast.30), custom_call_target="tpu_custom_call" | custom-call | flops 1000000000 | bytes 1000000 | tf_op jit(solution)/shard_map/pallas_call | solution.py:504
  32.0 4.1 %collective-permute-done.5.back_ref = bf16[640,128]{1,0:T(8,128)(2,1)S(1)} collective-permute-done((bf16[640,128]{1,0:T(8,128)(2,1)S(1)}, bf16[640,128]{1,0:T(8,128)(2,1)S(1)}, u32[]{:S(2)}, u32[]{:S(2)}) %collective-permute-start.5) | collective-permute-done | bytes 163872 | tf_op jit(solution)/shard_map/ppermute | solution.py:461
  36.1 0.8 %shard_map.89 = f32[20,128,128]{2,1,0:T(8,128)} custom-call(bf16[640,128]{1,0:T(8,128)(2,1)S(1)} %collective-permute-done.5.back_ref, f32[640,128]{1,0:T(8,128)S(1)} %get-tuple-element.35.moved_ref, f32[20,128,128]{2,1,0:T(8,128)} %shard_map.88.rest_0_), custom_call_target="tpu_custom_call", output_to_operand_aliasing={{}: (2, {})} | custom-call | flops 1000000000 | bytes 1000000 | tf_op jit(solution)/shard_map/pallas_call | solution.py:512
  (9 shorter events, 0.1 us)
Async XLA Ops:
  0.0 1.3 %copy-start = (f32[4,5,1,128,128]{4,3,2,1,0:T(8,128)S(1)}, f32[4,5,1,128,128]{4,3,2,1,0:T(8,128)}, u32[]{:S(2)}) copy-start(f32[4,5,1,128,128]{4,3,2,1,0:T(8,128)} %param.8) | copy-start | bytes 3932164
  1.3 7.1 %copy-start.6 = (f32[5]{0:T(128)S(1)}, f32[5]{0:T(128)}, u32[]{:S(2)}) copy-start(f32[5]{0:T(128)} %param.11) | copy-start | bytes 64
  1.3 7.1 %copy-start.5 = (bf16[256,40]{0,1:T(8,128)(2,1)S(1)}, bf16[256,40]{0,1:T(8,128)(2,1)}, u32[]{:S(2)}) copy-start(bf16[256,40]{0,1:T(8,128)(2,1)} %param.15) | copy-start | bytes 61444
  1.3 7.1 %copy-start.4 = (bf16[256,256]{1,0:T(8,128)(2,1)S(1)}, bf16[256,256]{1,0:T(8,128)(2,1)}, u32[]{:S(2)}) copy-start(bf16[256,256]{1,0:T(8,128)(2,1)} %param.14) | copy-start | bytes 393220
  1.3 7.3 %copy-start.3 = (bf16[360,256]{1,0:T(8,128)(2,1)S(1)}, bf16[360,256]{1,0:T(8,128)(2,1)}, u32[]{:S(2)}) copy-start(bf16[360,256]{1,0:T(8,128)(2,1)} %param.13) | copy-start | bytes 552964
  1.8 7.0 %copy-start.7 = (f32[4]{0:T(128)S(1)}, f32[4]{0:T(128)}, u32[]{:S(2)}) copy-start(f32[4]{0:T(128)} %param.10) | copy-start | bytes 52
  1.8 7.0 %copy-start.8 = (f32[4]{0:T(128)S(1)}, f32[4]{0:T(128)}, u32[]{:S(2)}) copy-start(f32[4]{0:T(128)} %param.9) | copy-start | bytes 52
  1.8 7.9 %collective-permute-start = (bf16[20,8,128]{2,1,0:T(8,128)(2,1)S(1)}, bf16[20,8,128]{2,1,0:T(8,128)(2,1)S(1)}, u32[]{:S(2)}, u32[]{:S(2)}) collective-permute-start(bf16[20,8,128]{2,1,0:T(8,128)(2,1)S(1)} %get-tuple-element.23), channel_id=1, source_target_pairs={{0,2},{2,4},{4,6},{6,8},{8,10},{10,12},{12,14},{16,18},{18,20},{20... | collective-permute-start | bytes 122888 | tf_op jit(solution)/shard_map/ppermute | solution.py:400
  3.8 6.2 %collective-permute-start.1 = (bf16[20,8,128]{2,1,0:T(8,128)(2,1)S(1)}, bf16[20,8,128]{2,1,0:T(8,128)(2,1)S(1)}, u32[]{:S(2)}, u32[]{:S(2)}) collective-permute-start(bf16[20,8,128]{2,1,0:T(8,128)(2,1)S(1)} %get-tuple-element.24), channel_id=1, source_target_pairs={{2,0},{4,2},{6,4},{8,6},{10,8},{12,10},{14,12},{18,16},{20,18},{22... | collective-permute-start | bytes 122888 | tf_op jit(solution)/shard_map/ppermute | solution.py:401
  10.0 2.8 %copy-start.1 = (f32[4,5,1,128,128]{4,3,2,1,0:T(8,128)S(1)}, f32[4,5,1,128,128]{4,3,2,1,0:T(8,128)}, u32[]{:S(2)}) copy-start(f32[4,5,1,128,128]{4,3,2,1,0:T(8,128)} %param.8) | copy-start | bytes 3932164
  10.2 5.2 %collective-permute-start.2 = (bf16[160,128]{1,0:T(8,128)(2,1)S(1)}, bf16[160,128]{1,0:T(8,128)(2,1)S(1)}, u32[]{:S(2)}, u32[]{:S(2)}) collective-permute-start(bf16[160,128]{1,0:T(8,128)(2,1)S(1)} %get-tuple-element.27), channel_id=1, source_target_pairs={{0,16},{2,18},{4,20},{6,22},{8,24},{10,26},{12,28},{14,30},{16,0},... | collective-permute-start | bytes 122888 | tf_op jit(solution)/shard_map/ppermute | solution.py:431
  13.7 7.6 %copy-start.2 = (s32[9,1,128,128]{3,2,1,0:T(8,128)S(1)}, s32[9,1,128,128]{3,2,1,0:T(8,128)}, u32[]{:S(2)}) copy-start(s32[9,1,128,128]{3,2,1,0:T(8,128)} %table_ref.3) | copy-start | bytes 1769476
  13.8 7.6 %collective-permute-start.4 = (bf16[800,128]{1,0:T(8,128)(2,1)S(1)}, bf16[800,128]{1,0:T(8,128)(2,1)S(1)}, u32[]{:S(2)}, u32[]{:S(2)}) collective-permute-start(bf16[800,128]{1,0:T(8,128)(2,1)S(1)} %shard_map.85), channel_id=1, source_target_pairs={{0,1},{1,0},{2,3},{3,2},{4,5},{5,4},{6,7},{7,6},{8,9},{9,8},{10,11... | collective-permute-start | bytes 614408 | tf_op jit(solution)/shard_map/ppermute | solution.py:461
  18.3 8.8 %collective-permute-start.3 = (bf16[800,128]{1,0:T(8,128)(2,1)S(1)}, bf16[800,128]{1,0:T(8,128)(2,1)S(1)}, u32[]{:S(2)}, u32[]{:S(2)}) collective-permute-start(bf16[800,128]{1,0:T(8,128)(2,1)S(1)} %get-tuple-element.29), channel_id=1, source_target_pairs={{0,1},{1,0},{2,3},{3,2},{4,5},{5,4},{6,7},{7,6},{8,9},{9,8},{10,11... | collective-permute-start | bytes 614408 | tf_op jit(solution)/shard_map/ppermute | solution.py:461
  25.1 5.9 %collective-permute-start.6 = (bf16[640,128]{1,0:T(8,128)(2,1)S(1)}, bf16[640,128]{1,0:T(8,128)(2,1)S(1)}, u32[]{:S(2)}, u32[]{:S(2)}) collective-permute-start(bf16[640,128]{1,0:T(8,128)(2,1)S(1)} %get-tuple-element.36), channel_id=1, source_target_pairs={{0,1},{1,0},{2,3},{3,2},{4,5},{5,4},{6,7},{7,6},{8,9},{9,8},{10,11... | collective-permute-start | bytes 491528 | tf_op jit(solution)/shard_map/ppermute | solution.py:461
  30.8 5.4 %collective-permute-start.5 = (bf16[640,128]{1,0:T(8,128)(2,1)S(1)}, bf16[640,128]{1,0:T(8,128)(2,1)S(1)}, u32[]{:S(2)}, u32[]{:S(2)}) collective-permute-start(bf16[640,128]{1,0:T(8,128)(2,1)S(1)} %get-tuple-element.34), channel_id=1, source_target_pairs={{0,1},{1,0},{2,3},{3,2},{4,5},{5,4},{6,7},{7,6},{8,9},{9,8},{10,11... | collective-permute-start | bytes 491528 | tf_op jit(solution)/shard_map/ppermute | solution.py:461

commit v9 on v8

--- a/solution.py
+++ b/solution.py
@@ -29,8 +29,9 @@
     return quarter * (1 + q) if n == 0 else 3 * quarter * q
 
 
-def edge_kernel(state_ref, east_ref, west_ref, rows_ref):
+def edge_kernel(state_ref, first_ref, second_ref, rows_ref):
     chans, cells_x, cells_y = state_ref.shape
+    even = lax.axis_index("tile") % 2 == 0
     slot = lax.broadcasted_iota(jnp.int32, (16, cells_y), 0)
     lane = lanes_of((16, cells_y))
     wanted = jnp.where(slot < 8, slot + cells_y - DEEP, slot - 8)
@@ -40,21 +41,28 @@
         block = state_ref[c].astype(BF16)
         strips = lax.dot_general(
             pick, block, (((1,), (1,)), ((), ())), preferred_element_type=F32
-        ).astype(BF16)
-        east_ref[c] = strips[0:8]
-        west_ref[c] = strips[8:16]
+        )
+        east, west = strips[0:8], strips[8:16]
+        first_ref[c] = jnp.where(even, east, west).astype(BF16)
+        second_ref[c] = jnp.where(even, west, east).astype(BF16)
         rows_ref[c] = jnp.concatenate(
             [state_ref[c, 0:DEEP], state_ref[c, cells_x - DEEP : cells_x], state_ref[c, 0:2]], axis=0
         ).astype(BF16)
 
 
 def pack_kernel(
-    rows_ref, west_in, east_in, west_own, east_own, coef_ref, out_ref, column_ref, wide_ref, wide, *, chans
+    rows_ref, first_in, second_in, first_own, second_own, coef_ref, out_ref, column_ref, wide_ref, wide, *, chans
 ):
     width = rows_ref.shape[1]
     lane = lanes_of((chans, width))
-    for n, ref in enumerate((rows_ref, west_in, east_in, west_own, east_own)):
-        wide[n] = ref[...].astype(F32)
+    even = lax.axis_index("tile") % 2 == 0
+    wide[0] = rows_ref[...].astype(F32)
+    got = first_in[...].astype(F32), second_in[...].astype(F32)
+    sent = first_own[...].astype(F32), second_own[...].astype(F32)
+    wide[1] = jnp.where(even, got[1], got[0])
+    wide[2] = jnp.where(even, got[0], got[1])
+    wide[3] = jnp.where(even, sent[1], sent[0])
+    wide[4] = jnp.where(even, sent[0], sent[1])
     sources = [(1, 0), (1, 1), (1, 2), (3, 0), (3, 1), (4, 1), (4, 2), (2, 0), (2, 1), (2, 2)]
     corner = jnp.zeros((chans, width), F32)
     for k, (n, slot) in enumerate(sources):
@@ -392,13 +400,14 @@
     sds = jax.ShapeDtypeStruct
 
     strip = sds((chans, 8, cells_y), BF16)
-    to_east, to_west, rows = call(edge_kernel, (strip, strip, strip), [VMEM_SPEC])(block)
-
-    def beside(by):
-        return [(i, i + by) for i in range(tiles) if 0 <= i % TILE_ROWS + by < TILE_ROWS]
-
-    from_west = lax.ppermute(to_east, "tile", beside(1))
-    from_east = lax.ppermute(to_west, "tile", beside(-1))
+    first, second, rows = call(edge_kernel, (strip, strip, strip), [VMEM_SPEC])(block)
+
+    def beside(odd):
+        pairs = [(i, i + 1) for i in range(odd, tiles - 1, 2) if i % TILE_ROWS != TILE_ROWS - 1]
+        return pairs + [(b, a) for a, b in pairs]
+
+    first_in = lax.ppermute(first, "tile", beside(0))
+    second_in = lax.ppermute(second, "tile", beside(1))
 
     def flat(x):
         return x.reshape(-1, cells_y)
@@ -425,7 +434,7 @@
         ),
         [VMEM_SPEC] * 6,
         [pltpu.VMEM((5, chans * 8, cells_y), F32)],
-    )(flat(rows), flat(from_west), flat(from_east), flat(to_west), flat(to_east), coef.T)
+    )(flat(rows), flat(first_in), flat(second_in), flat(first), flat(second), coef.T)
 
     def across(x, by):
         return lax.ppermute(x, "tile", [(i, (i + by) % tiles) for i in range(tiles)])

time: 37.1 us -> 35 us (0.943)
  the two profiles are of different devices: /device:TPU:8 before, /device:TPU:2 now
where the time goes in v9:
time: 35 us; the launch traced here: 34.8 us
  Pallas kernels  13.6 us (39%)
  starting transfers between devices  9.88 us (28%)
  waiting for transfers between devices  8.58 us (25%)
  local copies, waits for them, and re-layouts  2.31 us (7%)
    pallas_call x2, Pallas kernels, shards(): call(functools.partial(physics_kernel, n, chans=chans), (moved, sds((chan...  7.45 us
    ppermute x4, waiting for transfers between devices, swap(): return lax.ppermute(x, 'group', [(0, 1), (1, 0)])  6.52 us
    ppermute x4, starting transfers between devices, swap(): return lax.ppermute(x, 'group', [(0, 1), (1, 0)])  5.23 us
    pallas_call x2, Pallas kernels, transport(): call(functools.partial(transport_kernel, chans=chans, jobs=jobs, size=siz...  3.81 us
    ppermute x1, starting transfers between devices, across(): lax.ppermute(x, 'tile', [(i, (i + by) % tiles) for i in range(tiles)])  2.65 us
    ppermute x1, waiting for transfers between devices, shards(): second_in = lax.ppermute(second, 'tile', beside(1))  2.06 us
    ppermute x1, starting transfers between devices, shards(): second_in = lax.ppermute(second, 'tile', beside(1))  1.92 us
    unnamed x20, local copies, waits for them, and re-layouts  1.52 us
  transfers between devices with their start and end apart: 7, of which 4 were waited for; matrix products, arithmetic and copies ran while one was open for 3% of the time, Pallas kernels for 35%

profile of v9, /device:TPU:2, one launch (start us, length us, event | category | flops | bytes accessed | tf_op | source)
XLA Modules:
  0.0 34.8 jit_solution(12697442362857087122)
XLA Ops:
  0.0 0.0 copy-start
  0.0 1.3 %copy-done = f32[4,5,1,128,128]{4,3,2,1,0:T(8,128)S(1)} copy-done((f32[4,5,1,128,128]{4,3,2,1,0:T(8,128)S(1)}, f32[4,5,1,128,128]{4,3,2,1,0:T(8,128)}, u32[]{:S(2)}) %copy-start) | copy-done | bytes 1310744
  1.3 0.0 copy-start.6
  1.3 0.0 copy-start.5
  1.3 0.0 copy-start.4
  1.3 0.0 copy-start.3
  1.3 0.4 %shard_map.82 = (bf16[20,8,128]{2,1,0:T(8,128)(2,1)S(1)}, bf16[20,8,128]{2,1,0:T(8,128)(2,1)S(1)}, bf16[20,8,128]{2,1,0:T(8,128)(2,1)S(1)}) custom-call(f32[20,128,128]{2,1,0:T(8,128)S(1)} %bitcast.22), custom_call_target="tpu_custom_call" | custom-call | flops 1000000000 | bytes 1000000 | tf_op jit(solution)/shard_map/pallas_call | solution.py:403
  1.8 0.0 copy-start.7
  1.8 0.0 copy-start.8
  1.8 0.1 collective-permute-start
  1.9 1.9 %collective-permute-start.1 = (bf16[20,8,128]{2,1,0:T(8,128)(2,1)S(1)}, bf16[20,8,128]{2,1,0:T(8,128)(2,1)S(1)}, u32[]{:S(2)}, u32[]{:S(2)}) collective-permute-start(bf16[20,8,128]{2,1,0:T(8,128)(2,1)S(1)} %get-tuple-element.24), channel_id=1, source_target_pairs={{2,4},{6,8},{10,12},{18,20},{22,24},{26,28},{4,2},{8,6},{12,10},{2... | collective-permute-start | bytes 122888 | tf_op jit(solution)/shard_map/ppermute | solution.py:410
  3.8 0.0 copy-done.6
  3.8 0.0 copy-done.5
  3.8 0.0 copy-done.4
  3.9 0.1 copy.30
  4.0 0.0 copy-done.3
  4.0 0.1 reshape.181
  4.1 0.1 fusion
  4.2 0.0 copy-done.7
  4.2 0.0 copy-done.8
  4.2 0.1 broadcast_subtract_fusion
  4.3 0.1 sub.70
  4.4 0.1 sub.68
  4.5 0.1 add.33
  4.6 0.1 add.31
  4.6 0.1 sub.66
  4.8 0.1 copy.31
  4.9 0.1 copy.35
  5.0 0.1 copy.33.w1_ref
  5.1 0.0 collective-permute-done
  5.1 2.1 %collective-permute-done.1 = bf16[20,8,128]{2,1,0:T(8,128)(2,1)S(1)} collective-permute-done((bf16[20,8,128]{2,1,0:T(8,128)(2,1)S(1)}, bf16[20,8,128]{2,1,0:T(8,128)(2,1)S(1)}, u32[]{:S(2)}, u32[]{:S(2)}) %collective-permute-start.1) | collective-permute-done | bytes 40992 | tf_op jit(solution)/shard_map/ppermute | solution.py:410
  7.2 0.0 copy-start.1
  7.2 0.1 shard_map.83
  7.3 2.7 %collective-permute-start.2 = (bf16[160,128]{1,0:T(8,128)(2,1)S(1)}, bf16[160,128]{1,0:T(8,128)(2,1)S(1)}, u32[]{:S(2)}, u32[]{:S(2)}) collective-permute-start(bf16[160,128]{1,0:T(8,128)(2,1)S(1)} %get-tuple-element.27), channel_id=1, source_target_pairs={{0,16},{2,18},{4,20},{6,22},{8,24},{10,26},{12,28},{14,30},{16,0},... | collective-permute-start | bytes 122888 | tf_op jit(solution)/shard_map/ppermute | solution.py:440
  10.0 0.0 copy-done.1
  10.0 0.9 %shard_map.85 = bf16[800,128]{1,0:T(8,128)(2,1)S(1)} custom-call(f32[20,128,128]{2,1,0:T(8,128)S(1)} %bitcast.23, f32[5,20,128]{2,1,0:T(8,128)S(1)} %get-tuple-element.25.coef_ref, f32[10,20,128]{2,1,0:T(8,128)S(1)} %get-tuple-element.26.column_ref), custom_call_target="tpu_custom_call" | custom-call | flops 5000000000 | bytes 1000000 | tf_op jit(solution)/shard_map/pallas_call | solution.py:452
  10.9 0.0 copy-start.2
  10.9 1.6 %collective-permute-start.4 = (bf16[800,128]{1,0:T(8,128)(2,1)S(1)}, bf16[800,128]{1,0:T(8,128)(2,1)S(1)}, u32[]{:S(2)}, u32[]{:S(2)}) collective-permute-start(bf16[800,128]{1,0:T(8,128)(2,1)S(1)} %shard_map.85), channel_id=1, source_target_pairs={{0,1},{1,0},{2,3},{3,2},{4,5},{5,4},{6,7},{7,6},{8,9},{9,8},{10,11... | collective-permute-start | bytes 614408 | tf_op jit(solution)/shard_map/ppermute | solution.py:470
  12.5 0.0 collective-permute-done.2.rest_0_.rest_1_
  12.5 2.9 %shard_map.84 = (bf16[800,128]{1,0:T(8,128)(2,1)S(1)}, bf16[800,128]{1,0:T(8,128)(2,1)S(1)}, bf16[800,128]{1,0:T(8,128)(2,1)S(1)}, f32[640,128]{1,0:T(8,128)S(1)...) custom-call(f32[20,128,128]{2,1,0:T(8,128)S(1)} %bitcast.24, ...), custom_call_target="tpu_custom_call" | custom-call | flops 5000000000 | bytes 1000000 | tf_op jit(solution)/shard_map/pallas_call | solution.py:452
  15.4 1.4 %collective-permute-start.3 = (bf16[800,128]{1,0:T(8,128)(2,1)S(1)}, bf16[800,128]{1,0:T(8,128)(2,1)S(1)}, u32[]{:S(2)}, u32[]{:S(2)}) collective-permute-start(bf16[800,128]{1,0:T(8,128)(2,1)S(1)} %get-tuple-element.29), channel_id=1, source_target_pairs={{0,1},{1,0},{2,3},{3,2},{4,5},{5,4},{6,7},{7,6},{8,9},{9,8},{10,11... | collective-permute-start | bytes 614408 | tf_op jit(solution)/shard_map/ppermute | solution.py:470
  16.8 2.0 %collective-permute-done.4.got_ref = bf16[800,128]{1,0:T(8,128)(2,1)S(1)} collective-permute-done((bf16[800,128]{1,0:T(8,128)(2,1)S(1)}, bf16[800,128]{1,0:T(8,128)(2,1)S(1)}, u32[]{:S(2)}, u32[]{:S(2)}) %collective-permute-start.4) | collective-permute-done | bytes 204832 | tf_op jit(solution)/shard_map/ppermute | solution.py:470
  18.8 0.0 copy-done.2
  18.8 3.7 %shard_map.86 = (f32[640,128]{1,0:T(8,128)S(1)}, bf16[640,128]{1,0:T(8,128)(2,1)S(1)}) custom-call(s32[9,1,128,128]{3,2,1,0:T(8,128)S(1)} %copy-done.2, bf16[256,432]{1,0:T(8,128)(2,1)S(1)} %copy.33.w1_ref, bf16[256,256]{1,0:T(8,128)(2,1)S(1)} %multiply_bitcast_fusion.w2_ref, bf16[48,256]{1,0:T(8,128)(2,1)S(1)} %bitcast.19, ...), custom_call_target="tpu_custom_call" | custom-call | flops 7000000000 | bytes 1000000 | tf_op jit(solution)/shard_map/pallas_call | solution.py:492
  22.5 1.6 %collective-permute-start.6 = (bf16[640,128]{1,0:T(8,128)(2,1)S(1)}, bf16[640,128]{1,0:T(8,128)(2,1)S(1)}, u32[]{:S(2)}, u32[]{:S(2)}) collective-permute-start(bf16[640,128]{1,0:T(8,128)(2,1)S(1)} %get-tuple-element.36), channel_id=1, source_target_pairs={{0,1},{1,0},{2,3},{3,2},{4,5},{5,4},{6,7},{7,6},{8,9},{9,8},{10,11... | collective-permute-start | bytes 491528 | tf_op jit(solution)/shard_map/ppermute | solution.py:470
  24.1 0.0 collective-permute-done.3.got_ref
  24.1 3.7 %shard_map.87 = (f32[640,128]{1,0:T(8,128)S(1)}, bf16[640,128]{1,0:T(8,128)(2,1)S(1)}) custom-call(s32[9,1,128,128]{3,2,1,0:T(8,128)S(1)} %copy-done.2, bf16[256,432]{1,0:T(8,128)(2,1)S(1)} %copy.33.w1_ref, bf16[256,256]{1,0:T(8,128)(2,1)S(1)} %multiply_bitcast_fusion.w2_ref, bf16[48,256]{1,0:T(8,128)(2,1)S(1)} %bitcast.20, ...), custom_call_target="tpu_custom_call" | custom-call | flops 7000000000 | bytes 1000000 | tf_op jit(solution)/shard_map/pallas_call | solution.py:492
  27.8 0.7 %collective-permute-start.5 = (bf16[640,128]{1,0:T(8,128)(2,1)S(1)}, bf16[640,128]{1,0:T(8,128)(2,1)S(1)}, u32[]{:S(2)}, u32[]{:S(2)}) collective-permute-start(bf16[640,128]{1,0:T(8,128)(2,1)S(1)} %get-tuple-element.34), channel_id=1, source_target_pairs={{0,1},{1,0},{2,3},{3,2},{4,5},{5,4},{6,7},{7,6},{8,9},{9,8},{10,11... | collective-permute-start | bytes 491528 | tf_op jit(solution)/shard_map/ppermute | solution.py:470
  28.5 0.3 collective-permute-done.6.back_ref
  28.8 1.0 %shard_map.88.rest_0_ = f32[20,128,128]{2,1,0:T(8,128)} custom-call(bf16[640,128]{1,0:T(8,128)(2,1)S(1)} %collective-permute-done.6.back_ref, f32[640,128]{1,0:T(8,128)S(1)} %get-tuple-element.37.moved_ref, f32[20,32,128]{2,1,0:T(8,128)S(1)} %bitcast.29, f32[20,32,128]{2,1,0:T(8,128)S(1)} %bitcast.30), custom_call_target="tpu_custom_call" | custom-call | flops 1000000000 | bytes 1000000 | tf_op jit(solution)/shard_map/pallas_call | solution.py:513
  29.8 4.2 %collective-permute-done.5.back_ref = bf16[640,128]{1,0:T(8,128)(2,1)S(1)} collective-permute-done((bf16[640,128]{1,0:T(8,128)(2,1)S(1)}, bf16[640,128]{1,0:T(8,128)(2,1)S(1)}, u32[]{:S(2)}, u32[]{:S(2)}) %collective-permute-start.5) | collective-permute-done | bytes 163872 | tf_op jit(solution)/shard_map/ppermute | solution.py:470
  34.1 0.8 %shard_map.89 = f32[20,128,128]{2,1,0:T(8,128)} custom-call(bf16[640,128]{1,0:T(8,128)(2,1)S(1)} %collective-permute-done.5.back_ref, f32[640,128]{1,0:T(8,128)S(1)} %get-tuple-element.35.moved_ref, f32[20,128,128]{2,1,0:T(8,128)} %shard_map.88.rest_0_), custom_call_target="tpu_custom_call", output_to_operand_aliasing={{}: (2, {})} | custom-call | flops 1000000000 | bytes 1000000 | tf_op jit(solution)/shard_map/pallas_call | solution.py:521
  (9 shorter events, 0.1 us)
Async XLA Ops:
  0.0 1.3 %copy-start = (f32[4,5,1,128,128]{4,3,2,1,0:T(8,128)S(1)}, f32[4,5,1,128,128]{4,3,2,1,0:T(8,128)}, u32[]{:S(2)}) copy-start(f32[4,5,1,128,128]{4,3,2,1,0:T(8,128)} %param.8) | copy-start | bytes 3932164
  1.3 2.5 %copy-start.6 = (f32[5]{0:T(128)S(1)}, f32[5]{0:T(128)}, u32[]{:S(2)}) copy-start(f32[5]{0:T(128)} %param.11) | copy-start | bytes 64
  1.3 2.5 %copy-start.5 = (bf16[256,40]{0,1:T(8,128)(2,1)S(1)}, bf16[256,40]{0,1:T(8,128)(2,1)}, u32[]{:S(2)}) copy-start(bf16[256,40]{0,1:T(8,128)(2,1)} %param.15) | copy-start | bytes 61444
  1.3 2.5 %copy-start.4 = (bf16[256,256]{1,0:T(8,128)(2,1)S(1)}, bf16[256,256]{1,0:T(8,128)(2,1)}, u32[]{:S(2)}) copy-start(bf16[256,256]{1,0:T(8,128)(2,1)} %param.14) | copy-start | bytes 393220
  1.3 2.7 %copy-start.3 = (bf16[360,256]{1,0:T(8,128)(2,1)S(1)}, bf16[360,256]{1,0:T(8,128)(2,1)}, u32[]{:S(2)}) copy-start(bf16[360,256]{1,0:T(8,128)(2,1)} %param.13) | copy-start | bytes 552964
  1.8 2.4 %copy-start.7 = (f32[4]{0:T(128)S(1)}, f32[4]{0:T(128)}, u32[]{:S(2)}) copy-start(f32[4]{0:T(128)} %param.10) | copy-start | bytes 52
  1.8 2.4 %copy-start.8 = (f32[4]{0:T(128)S(1)}, f32[4]{0:T(128)}, u32[]{:S(2)}) copy-start(f32[4]{0:T(128)} %param.9) | copy-start | bytes 52
  1.8 3.3 %collective-permute-start = (bf16[20,8,128]{2,1,0:T(8,128)(2,1)S(1)}, bf16[20,8,128]{2,1,0:T(8,128)(2,1)S(1)}, u32[]{:S(2)}, u32[]{:S(2)}) collective-permute-start(bf16[20,8,128]{2,1,0:T(8,128)(2,1)S(1)} %get-tuple-element.23), channel_id=1, source_target_pairs={{0,2},{4,6},{8,10},{12,14},{16,18},{20,22},{24,26},{28,30},{2,0},{... | collective-permute-start | bytes 122888 | tf_op jit(solution)/shard_map/ppermute | solution.py:409
  1.9 5.3 %collective-permute-start.1 = (bf16[20,8,128]{2,1,0:T(8,128)(2,1)S(1)}, bf16[20,8,128]{2,1,0:T(8,128)(2,1)S(1)}, u32[]{:S(2)}, u32[]{:S(2)}) collective-permute-start(bf16[20,8,128]{2,1,0:T(8,128)(2,1)S(1)} %get-tuple-element.24), channel_id=1, source_target_pairs={{2,4},{6,8},{10,12},{18,20},{22,24},{26,28},{4,2},{8,6},{12,10},{2... | collective-permute-start | bytes 122888 | tf_op jit(solution)/shard_map/ppermute | solution.py:410
  7.2 2.8 %copy-start.1 = (f32[4,5,1,128,128]{4,3,2,1,0:T(8,128)S(1)}, f32[4,5,1,128,128]{4,3,2,1,0:T(8,128)}, u32[]{:S(2)}) copy-start(f32[4,5,1,128,128]{4,3,2,1,0:T(8,128)} %param.8) | copy-start | bytes 3932164
  7.3 5.2 %collective-permute-start.2 = (bf16[160,128]{1,0:T(8,128)(2,1)S(1)}, bf16[160,128]{1,0:T(8,128)(2,1)S(1)}, u32[]{:S(2)}, u32[]{:S(2)}) collective-permute-start(bf16[160,128]{1,0:T(8,128)(2,1)S(1)} %get-tuple-element.27), channel_id=1, source_target_pairs={{0,16},{2,18},{4,20},{6,22},{8,24},{10,26},{12,28},{14,30},{16,0},... | collective-permute-start | bytes 122888 | tf_op jit(solution)/shard_map/ppermute | solution.py:440
  10.9 7.9 %copy-start.2 = (s32[9,1,128,128]{3,2,1,0:T(8,128)S(1)}, s32[9,1,128,128]{3,2,1,0:T(8,128)}, u32[]{:S(2)}) copy-start(s32[9,1,128,128]{3,2,1,0:T(8,128)} %table_ref.3) | copy-start | bytes 1769476
  10.9 7.9 %collective-permute-start.4 = (bf16[800,128]{1,0:T(8,128)(2,1)S(1)}, bf16[800,128]{1,0:T(8,128)(2,1)S(1)}, u32[]{:S(2)}, u32[]{:S(2)}) collective-permute-start(bf16[800,128]{1,0:T(8,128)(2,1)S(1)} %shard_map.85), channel_id=1, source_target_pairs={{0,1},{1,0},{2,3},{3,2},{4,5},{5,4},{6,7},{7,6},{8,9},{9,8},{10,11... | collective-permute-start | bytes 614408 | tf_op jit(solution)/shard_map/ppermute | solution.py:470
  15.4 8.7 %collective-permute-start.3 = (bf16[800,128]{1,0:T(8,128)(2,1)S(1)}, bf16[800,128]{1,0:T(8,128)(2,1)S(1)}, u32[]{:S(2)}, u32[]{:S(2)}) collective-permute-start(bf16[800,128]{1,0:T(8,128)(2,1)S(1)} %get-tuple-element.29), channel_id=1, source_target_pairs={{0,1},{1,0},{2,3},{3,2},{4,5},{5,4},{6,7},{7,6},{8,9},{9,8},{10,11... | collective-permute-start | bytes 614408 | tf_op jit(solution)/shard_map/ppermute | solution.py:470
  22.5 6.3 %collective-permute-start.6 = (bf16[640,128]{1,0:T(8,128)(2,1)S(1)}, bf16[640,128]{1,0:T(8,128)(2,1)S(1)}, u32[]{:S(2)}, u32[]{:S(2)}) collective-permute-start(bf16[640,128]{1,0:T(8,128)(2,1)S(1)} %get-tuple-element.36), channel_id=1, source_target_pairs={{0,1},{1,0},{2,3},{3,2},{4,5},{5,4},{6,7},{7,6},{8,9},{9,8},{10,11... | collective-permute-start | bytes 491528 | tf_op jit(solution)/shard_map/ppermute | solution.py:470
  27.8 6.2 %collective-permute-start.5 = (bf16[640,128]{1,0:T(8,128)(2,1)S(1)}, bf16[640,128]{1,0:T(8,128)(2,1)S(1)}, u32[]{:S(2)}, u32[]{:S(2)}) collective-permute-start(bf16[640,128]{1,0:T(8,128)(2,1)S(1)} %get-tuple-element.34), channel_id=1, source_target_pairs={{0,1},{1,0},{2,3},{3,2},{4,5},{5,4},{6,7},{7,6},{8,9},{9,8},{10,11... | collective-permute-start | bytes 491528 | tf_op jit(solution)/shard_map/ppermute | solution.py:470

commit v10 on v9

--- a/solution.py
+++ b/solution.py
@@ -10,7 +10,7 @@
 
 TILE_ROWS = 8
 DEEP = 3
-EXTRA = 8
+EXTRAS = 3
 BLOCK_ROWS = 16
 MARGIN = 16
 GROUP = 4
@@ -100,9 +100,10 @@
     own = lax.axis_index("group")
     place = lax.axis_index("tile") % TILE_ROWS
     half_of = (own, 1 - own)
+    pad = -(-chans // 8) * 8
     base_of = [first_row(half_of[whose], n, size) for whose, n in jobs]
-    fetch = pltpu.make_async_copy(state_ref, raw_s.at[:, pl.ds(MARGIN, cells_x)], sem.at[0])
     if not ahead:
+        fetch = pltpu.make_async_copy(state_ref, raw_s.at[:, pl.ds(MARGIN, cells_x)], sem.at[0])
         fetch.start()
     matrix[...] = shift_matrix(width)
     lane = lanes_of((chans, width))
@@ -167,7 +168,12 @@
             row_of = lane - first_lane + at
             off = (row_of < 0) | (row_of >= cells_x)
             sides.append(jnp.where(off, roll(aux, by), roll(main, by)))
-        window[pl.ds(2, chans, stride=EXTRA + size), :] = jnp.where(low_lanes, *sides)
+        window[pl.ds(chans * size + 2 * pad, chans), :] = jnp.where(low_lanes, *sides)
+        for k in range(EXTRAS):
+            if pad > chans:
+                window[pl.ds(chans * size + k * pad + chans, pad - chans), :] = jnp.zeros(
+                    (pad - chans, width), F32
+                )
 
     rows = size + 16 if ahead else cells_x + 16
     origin = base_of[0] - 8 if ahead else -8
@@ -217,10 +223,10 @@
             c = base + g
             for window, row in zip(windows, base_of):
                 at = MARGIN + row
-                to = c * (EXTRA + size)
+                to = chans * size + c
                 window[pl.ds(to, 1), :] = last_s[c, pl.ds(at - 1, 1), :]
-                window[pl.ds(to + 1, 1), :] = last_s[c, pl.ds(at + size, 1), :]
-                window[pl.ds(to + EXTRA, size), :] = last_s[c, pl.ds(pl.multiple_of(at, 8), size), :]
+                window[pl.ds(to + pad, 1), :] = last_s[c, pl.ds(at + size, 1), :]
+                window[pl.ds(c * size, size), :] = last_s[c, pl.ds(pl.multiple_of(at, 8), size), :]
             for k, quarter in enumerate(quarters):
                 at = pl.multiple_of(MARGIN + first_row(half_of[k // 2], k % 2, size), 8)
                 quarter[pl.ds(c * size, size), :] = last_s[c, pl.ds(at, size), :]
@@ -241,9 +247,10 @@
 def physics_kernel(
     chunk, table_ref, w1_ref, w2_ref, w3_ref, mine_ref, got_ref, kept_ref, *rest, chans
 ):
-    own_ref, other_ref, wide, packed, mask, table, even, odd, terms, sem = rest[-10:]
+    own_ref, other_ref, wide, ends, packed, mask, table, even, odd, terms, sem = rest[-11:]
     size, width = table.shape[1:]
-    height = EXTRA + size
+    height = mine_ref.shape[0]
+    pitch = size + 8
     pad = -(-chans // 8) * 8
     both = 2 * pad
     top = first_row(lax.axis_index("group"), chunk, size)
@@ -260,18 +267,17 @@
     west = (k >= width) & (k < width + width // 2) & (n == 0)
     east = (k >= width + width // 2) & (n == 2 * width - 1)
     matrix = jnp.where(inner | west | east, 1.0, 0.0).astype(BF16)
-    slot = lax.broadcasted_iota(jnp.int32, (height, width), 0)
-    line = jnp.where(
-        slot >= EXTRA, slot - EXTRA + 1, jnp.where(slot == 0, 0, jnp.where(slot == 1, size + 1, -1))
-    )
-    diagonal = lanes_of((height, width)) % (width // 2) == line
+    lanes = lanes_of((size, width)) % (width // 2)
+    diagonal = lanes == lax.broadcasted_iota(jnp.int32, (size, width), 0) + 1
+    lane = lanes_of((pad, width)) % (width // 2)
+    end = chans * size
     for s, ref in enumerate((mine_ref, got_ref)):
         cells = ref[...]
         flat = cells.astype(F32)
-        wide[1, s, pl.ds(0, chans * height)] = flat
-        edges = [
-            jnp.where(diagonal, flat[c * height + 2 : c * height + 3], 0.0) for c in range(chans)
-        ]
+        sides = flat[end + 2 * pad : end + 3 * pad]
+        edges = [jnp.where(diagonal, sides[c : c + 1], 0.0) for c in range(chans)]
+        edges += [jnp.where(lane == 0, sides, 0.0), jnp.where(lane == size + 1, sides, 0.0)]
+        edges.append(jnp.zeros((height - end - 2 * pad, width), F32))
         edges = jnp.concatenate(edges, axis=0).astype(BF16)
         near = lax.dot_general(
             jnp.concatenate([cells, edges], axis=1),
@@ -279,18 +285,24 @@
             (((1,), (0,)), ((), ())),
             preferred_element_type=F32,
         )
-        wide[0, s, pl.ds(0, chans * height)] = near[:, :width]
-        wide[2, s, pl.ds(0, chans * height)] = near[:, width:]
-        if pad > chans:
-            for b in range(3):
-                wide[b, s, pl.ds(chans * height, (pad - chans) * height)] = jnp.zeros(
-                    ((pad - chans) * height, width), F32
+        for b, x in enumerate((near[:, :width], flat, near[:, width:])):
+            for c in range(chans):
+                wide[b, s, pl.ds(c * pitch, size)] = x[c * size : (c + 1) * size]
+            for k in range(2):
+                ends[b, s, k] = x[end + k * pad : end + (k + 1) * pad]
+            if pad > chans:
+                wide[b, s, pl.ds(chans * pitch, (pad - chans) * pitch)] = jnp.zeros(
+                    ((pad - chans) * pitch, width), F32
                 )
 
+    def cells_at(b, s, l):
+        if 0 <= l < size:
+            return wide[b, s, pl.ds(l, pad, stride=pitch), :]
+        return ends[b, s, int(l == size)]
+
     for l in range(-1, size + 1):
-        at = 0 if l < 0 else 1 if l == size else EXTRA + l
         for b in range(3):
-            pair = [wide[b, s, pl.ds(at, pad, stride=height), :] for s in range(2)]
+            pair = [cells_at(b, s, l) for s in range(2)]
             packed[b, l + 1] = jnp.concatenate(pair, axis=0).astype(BF16)
 
     for copy in copies:
@@ -342,8 +354,8 @@
         for u in range(rows_step):
             l = n * rows_step + u
             cols = slice(u * width, (u + 1) * width)
-            terms[0, pl.ds(l, chans, stride=size), :] = tend[0:chans, cols]
-            terms[1, pl.ds(l, chans, stride=size), :] = tend[pad : pad + chans, cols]
+            terms[0, pl.ds(l, chans, stride=pitch), :] = tend[0:chans, cols]
+            terms[1, pl.ds(l, chans, stride=pitch), :] = tend[pad : pad + chans, cols]
 
     steps = size // rows_step
     slots = (even, odd)
@@ -352,8 +364,10 @@
         if n + 1 < steps:
             stack(n + 1, slots[(n + 1) % 2])
         network(n, slots[n % 2])
-    other_ref[...] = terms[1].astype(BF16)
-    own_ref[...] = kept_ref[...] + terms[0]
+    for c in range(chans):
+        rows, line = pl.ds(c * size, size), pl.ds(c * pitch, size)
+        other_ref[rows] = terms[1, line].astype(BF16)
+        own_ref[rows] = kept_ref[rows] + terms[0, line]
 
 
 def finish_kernel(chunk, back_ref, moved_ref, *rest, parts):
@@ -444,7 +458,7 @@
 
     size = cells_x // 4
     tall = pltpu.VMEM((chans, cells_x + 2 * MARGIN, cells_y), F32)
-    height = chans * (EXTRA + size)
+    height = -(-(chans * size + EXTRAS * pad) // 16) * 16
     moved = sds((chans * size, cells_y), F32)
 
     def transport(jobs, *halos):
@@ -494,13 +508,14 @@
             (moved, sds((chans * size, cells_y), BF16)),
             [ANY_SPEC] + [VMEM_SPEC] * 6 + [ANY_SPEC] * n,
             [
-                pltpu.VMEM((3, 2, pad * (EXTRA + size), cells_y), F32),
+                pltpu.VMEM((3, 2, pad * (size + 8), cells_y), F32),
+                pltpu.VMEM((3, 2, 2, pad, cells_y), F32),
                 pltpu.VMEM((3, size + 2, both, cells_y), BF16),
                 pltpu.VMEM((3, size, cells_y), F32),
                 pltpu.VMEM((2, size, cells_y), jnp.int32),
                 blocks,
                 blocks,
-                pltpu.VMEM((2, chans * size, cells_y), F32),
+                pltpu.VMEM((2, chans * (size + 8), cells_y), F32),
                 pltpu.SemaphoreType.DMA((2,)),
             ],
             flops=7 * 10**9,

time: 35 us -> 33.7 us (0.963)
  waiting for transfers between devices: 8.58 us -> 7.88 us
  Pallas kernels: 13.6 us -> 12.9 us
    ppermute x4, waiting for transfers between devices: 6.52 us -> 5.82 us  [swap(): return lax.ppermute(x, 'group', [(0, 1), (1, 0)])]
    pallas_call x2, Pallas kernels: 7.45 us -> 6.82 us  [shards(): call(functools.partial(physics_kernel, n, chans=chans), (moved, sds((chan...]
where the time goes in v10:
time: 33.7 us; the launch traced here: 33.6 us
  Pallas kernels  12.9 us (38%)
  starting transfers between devices  9.97 us (30%)
  waiting for transfers between devices  7.88 us (23%)
  local copies, waits for them, and re-layouts  2.31 us (7%)
    pallas_call x2, Pallas kernels, shards(): call(functools.partial(physics_kernel, n, chans=chans), (moved, sds((chan...  6.82 us
    ppermute x4, waiting for transfers between devices, swap(): return lax.ppermute(x, 'group', [(0, 1), (1, 0)])  5.82 us
    ppermute x4, starting transfers between devices, swap(): return lax.ppermute(x, 'group', [(0, 1), (1, 0)])  5.32 us
    pallas_call x2, Pallas kernels, transport(): call(functools.partial(transport_kernel, chans=chans, jobs=jobs, size=siz...  3.8 us
    ppermute x1, starting transfers between devices, across(): lax.ppermute(x, 'tile', [(i, (i + by) % tiles) for i in range(tiles)])  2.65 us
    ppermute x1, waiting for transfers between devices, shards(): second_in = lax.ppermute(second, 'tile', beside(1))  2.06 us
    ppermute x1, starting transfers between devices, shards(): second_in = lax.ppermute(second, 'tile', beside(1))  1.92 us
    unnamed x20, local copies, waits for them, and re-layouts  1.52 us
  transfers between devices with their start and end apart: 7, of which 4 were waited for; matrix products, arithmetic and copies ran while one was open for 3% of the time, Pallas kernels for 35%

profile of v10, /device:TPU:2, one launch (start us, length us, event | category | flops | bytes accessed | tf_op | source)
XLA Modules:
  0.0 33.6 jit_solution(15275950140357517030)
XLA Ops:
  0.0 0.0 copy-start
  0.0 1.3 %copy-done = f32[4,5,1,128,128]{4,3,2,1,0:T(8,128)S(1)} copy-done((f32[4,5,1,128,128]{4,3,2,1,0:T(8,128)S(1)}, f32[4,5,1,128,128]{4,3,2,1,0:T(8,128)}, u32[]{:S(2)}) %copy-start) | copy-done | bytes 1310744
  1.3 0.0 copy-start.6
  1.3 0.0 copy-start.5
  1.3 0.0 copy-start.4
  1.3 0.0 copy-start.3
  1.3 0.4 %shard_map.82 = (bf16[20,8,128]{2,1,0:T(8,128)(2,1)S(1)}, bf16[20,8,128]{2,1,0:T(8,128)(2,1)S(1)}, bf16[20,8,128]{2,1,0:T(8,128)(2,1)S(1)}) custom-call(f32[20,128,128]{2,1,0:T(8,128)S(1)} %bitcast.22), custom_call_target="tpu_custom_call" | custom-call | flops 1000000000 | bytes 1000000 | tf_op jit(solution)/shard_map/pallas_call | solution.py:417
  1.8 0.0 copy-start.7
  1.8 0.0 copy-start.8
  1.8 0.1 collective-permute-start
  1.9 1.9 %collective-permute-start.1 = (bf16[20,8,128]{2,1,0:T(8,128)(2,1)S(1)}, bf16[20,8,128]{2,1,0:T(8,128)(2,1)S(1)}, u32[]{:S(2)}, u32[]{:S(2)}) collective-permute-start(bf16[20,8,128]{2,1,0:T(8,128)(2,1)S(1)} %get-tuple-element.24), channel_id=1, source_target_pairs={{2,4},{6,8},{10,12},{18,20},{22,24},{26,28},{4,2},{8,6},{12,10},{2... | collective-permute-start | bytes 122888 | tf_op jit(solution)/shard_map/ppermute | solution.py:424
  3.8 0.0 copy-done.6
  3.8 0.0 copy-done.5
  3.8 0.0 copy-done.4
  3.9 0.1 copy.30
  4.0 0.0 copy-done.3
  4.0 0.1 reshape.181
  4.1 0.1 fusion
  4.2 0.0 copy-done.7
  4.2 0.0 copy-done.8
  4.2 0.1 broadcast_subtract_fusion
  4.3 0.1 sub.70
  4.4 0.1 sub.68
  4.5 0.1 add.33
  4.6 0.1 add.31
  4.6 0.1 sub.66
  4.8 0.1 copy.31
  4.9 0.1 copy.35
  5.0 0.1 copy.33.w1_ref
  5.1 0.0 collective-permute-done
  5.1 2.1 %collective-permute-done.1 = bf16[20,8,128]{2,1,0:T(8,128)(2,1)S(1)} collective-permute-done((bf16[20,8,128]{2,1,0:T(8,128)(2,1)S(1)}, bf16[20,8,128]{2,1,0:T(8,128)(2,1)S(1)}, u32[]{:S(2)}, u32[]{:S(2)}) %collective-permute-start.1) | collective-permute-done | bytes 40992 | tf_op jit(solution)/shard_map/ppermute | solution.py:424
  7.2 0.0 copy-start.1
  7.2 0.1 shard_map.83
  7.3 2.7 %collective-permute-start.2 = (bf16[160,128]{1,0:T(8,128)(2,1)S(1)}, bf16[160,128]{1,0:T(8,128)(2,1)S(1)}, u32[]{:S(2)}, u32[]{:S(2)}) collective-permute-start(bf16[160,128]{1,0:T(8,128)(2,1)S(1)} %get-tuple-element.27), channel_id=1, source_target_pairs={{0,16},{2,18},{4,20},{6,22},{8,24},{10,26},{12,28},{14,30},{16,0},... | collective-permute-start | bytes 122888 | tf_op jit(solution)/shard_map/ppermute | solution.py:454
  10.0 0.0 copy-done.1
  10.0 0.9 %shard_map.85 = bf16[720,128]{1,0:T(8,128)(2,1)S(1)} custom-call(f32[20,128,128]{2,1,0:T(8,128)S(1)} %bitcast.23, f32[5,20,128]{2,1,0:T(8,128)S(1)} %get-tuple-element.25.coef_ref, f32[10,20,128]{2,1,0:T(8,128)S(1)} %get-tuple-element.26.column_ref), custom_call_target="tpu_custom_call" | custom-call | flops 5000000000 | bytes 1000000 | tf_op jit(solution)/shard_map/pallas_call | solution.py:466
  10.9 0.0 copy-start.2
  10.9 1.6 %collective-permute-start.4 = (bf16[720,128]{1,0:T(8,128)(2,1)S(1)}, bf16[720,128]{1,0:T(8,128)(2,1)S(1)}, u32[]{:S(2)}, u32[]{:S(2)}) collective-permute-start(bf16[720,128]{1,0:T(8,128)(2,1)S(1)} %shard_map.85), channel_id=1, source_target_pairs={{0,1},{1,0},{2,3},{3,2},{4,5},{5,4},{6,7},{7,6},{8,9},{9,8},{10,11... | collective-permute-start | bytes 552968 | tf_op jit(solution)/shard_map/ppermute | solution.py:484
  12.5 0.0 collective-permute-done.2.rest_0_.rest_1_
  12.5 2.9 %shard_map.84 = (bf16[720,128]{1,0:T(8,128)(2,1)S(1)}, bf16[720,128]{1,0:T(8,128)(2,1)S(1)}, bf16[720,128]{1,0:T(8,128)(2,1)S(1)}, f32[640,128]{1,0:T(8,128)S(1)...) custom-call(f32[20,128,128]{2,1,0:T(8,128)S(1)} %bitcast.24, ...), custom_call_target="tpu_custom_call" | custom-call | flops 5000000000 | bytes 1000000 | tf_op jit(solution)/shard_map/pallas_call | solution.py:466
  15.4 1.4 %collective-permute-start.3 = (bf16[720,128]{1,0:T(8,128)(2,1)S(1)}, bf16[720,128]{1,0:T(8,128)(2,1)S(1)}, u32[]{:S(2)}, u32[]{:S(2)}) collective-permute-start(bf16[720,128]{1,0:T(8,128)(2,1)S(1)} %get-tuple-element.29), channel_id=1, source_target_pairs={{0,1},{1,0},{2,3},{3,2},{4,5},{5,4},{6,7},{7,6},{8,9},{9,8},{10,11... | collective-permute-start | bytes 552968 | tf_op jit(solution)/shard_map/ppermute | solution.py:484
  16.8 1.6 %collective-permute-done.4.got_ref = bf16[720,128]{1,0:T(8,128)(2,1)S(1)} collective-permute-done((bf16[720,128]{1,0:T(8,128)(2,1)S(1)}, bf16[720,128]{1,0:T(8,128)(2,1)S(1)}, u32[]{:S(2)}, u32[]{:S(2)}) %collective-permute-start.4) | collective-permute-done | bytes 184352 | tf_op jit(solution)/shard_map/ppermute | solution.py:484
  18.4 0.0 copy-done.2
  18.4 3.4 %shard_map.86 = (f32[640,128]{1,0:T(8,128)S(1)}, bf16[640,128]{1,0:T(8,128)(2,1)S(1)}) custom-call(s32[9,1,128,128]{3,2,1,0:T(8,128)S(1)} %copy-done.2, bf16[256,432]{1,0:T(8,128)(2,1)S(1)} %copy.33.w1_ref, bf16[256,256]{1,0:T(8,128)(2,1)S(1)} %multiply_bitcast_fusion.w2_ref, bf16[48,256]{1,0:T(8,128)(2,1)S(1)} %bitcast.19, ...), custom_call_target="tpu_custom_call" | custom-call | flops 7000000000 | bytes 1000000 | tf_op jit(solution)/shard_map/pallas_call | solution.py:506
  21.8 1.6 %collective-permute-start.6 = (bf16[640,128]{1,0:T(8,128)(2,1)S(1)}, bf16[640,128]{1,0:T(8,128)(2,1)S(1)}, u32[]{:S(2)}, u32[]{:S(2)}) collective-permute-start(bf16[640,128]{1,0:T(8,128)(2,1)S(1)} %get-tuple-element.36), channel_id=1, source_target_pairs={{0,1},{1,0},{2,3},{3,2},{4,5},{5,4},{6,7},{7,6},{8,9},{9,8},{10,11... | collective-permute-start | bytes 491528 | tf_op jit(solution)/shard_map/ppermute | solution.py:484
  23.4 0.0 collective-permute-done.3.got_ref
  23.4 3.4 %shard_map.87 = (f32[640,128]{1,0:T(8,128)S(1)}, bf16[640,128]{1,0:T(8,128)(2,1)S(1)}) custom-call(s32[9,1,128,128]{3,2,1,0:T(8,128)S(1)} %copy-done.2, bf16[256,432]{1,0:T(8,128)(2,1)S(1)} %copy.33.w1_ref, bf16[256,256]{1,0:T(8,128)(2,1)S(1)} %multiply_bitcast_fusion.w2_ref, bf16[48,256]{1,0:T(8,128)(2,1)S(1)} %bitcast.20, ...), custom_call_target="tpu_custom_call" | custom-call | flops 7000000000 | bytes 1000000 | tf_op jit(solution)/shard_map/pallas_call | solution.py:506
  26.8 0.8 %collective-permute-start.5 = (bf16[640,128]{1,0:T(8,128)(2,1)S(1)}, bf16[640,128]{1,0:T(8,128)(2,1)S(1)}, u32[]{:S(2)}, u32[]{:S(2)}) collective-permute-start(bf16[640,128]{1,0:T(8,128)(2,1)S(1)} %get-tuple-element.34), channel_id=1, source_target_pairs={{0,1},{1,0},{2,3},{3,2},{4,5},{5,4},{6,7},{7,6},{8,9},{9,8},{10,11... | collective-permute-start | bytes 491528 | tf_op jit(solution)/shard_map/ppermute | solution.py:484
  27.6 0.5 %collective-permute-done.6.back_ref = bf16[640,128]{1,0:T(8,128)(2,1)S(1)} collective-permute-done((bf16[640,128]{1,0:T(8,128)(2,1)S(1)}, bf16[640,128]{1,0:T(8,128)(2,1)S(1)}, u32[]{:S(2)}, u32[]{:S(2)}) %collective-permute-start.6) | collective-permute-done | bytes 163872 | tf_op jit(solution)/shard_map/ppermute | solution.py:484
  28.1 1.0 %shard_map.88.rest_0_ = f32[20,128,128]{2,1,0:T(8,128)} custom-call(bf16[640,128]{1,0:T(8,128)(2,1)S(1)} %collective-permute-done.6.back_ref, f32[640,128]{1,0:T(8,128)S(1)} %get-tuple-element.37.moved_ref, f32[20,32,128]{2,1,0:T(8,128)S(1)} %bitcast.29, f32[20,32,128]{2,1,0:T(8,128)S(1)} %bitcast.30), custom_call_target="tpu_custom_call" | custom-call | flops 1000000000 | bytes 1000000 | tf_op jit(solution)/shard_map/pallas_call | solution.py:528
  29.1 3.7 %collective-permute-done.5.back_ref = bf16[640,128]{1,0:T(8,128)(2,1)S(1)} collective-permute-done((bf16[640,128]{1,0:T(8,128)(2,1)S(1)}, bf16[640,128]{1,0:T(8,128)(2,1)S(1)}, u32[]{:S(2)}, u32[]{:S(2)}) %collective-permute-start.5) | collective-permute-done | bytes 163872 | tf_op jit(solution)/shard_map/ppermute | solution.py:484
  32.8 0.8 %shard_map.89 = f32[20,128,128]{2,1,0:T(8,128)} custom-call(bf16[640,128]{1,0:T(8,128)(2,1)S(1)} %collective-permute-done.5.back_ref, f32[640,128]{1,0:T(8,128)S(1)} %get-tuple-element.35.moved_ref, f32[20,128,128]{2,1,0:T(8,128)} %shard_map.88.rest_0_), custom_call_target="tpu_custom_call", output_to_operand_aliasing={{}: (2, {})} | custom-call | flops 1000000000 | bytes 1000000 | tf_op jit(solution)/shard_map/pallas_call | solution.py:536
  (9 shorter events, 0.1 us)
Async XLA Ops:
  0.0 1.3 %copy-start = (f32[4,5,1,128,128]{4,3,2,1,0:T(8,128)S(1)}, f32[4,5,1,128,128]{4,3,2,1,0:T(8,128)}, u32[]{:S(2)}) copy-start(f32[4,5,1,128,128]{4,3,2,1,0:T(8,128)} %param.8) | copy-start | bytes 3932164
  1.3 2.5 %copy-start.6 = (f32[5]{0:T(128)S(1)}, f32[5]{0:T(128)}, u32[]{:S(2)}) copy-start(f32[5]{0:T(128)} %param.11) | copy-start | bytes 64
  1.3 2.5 %copy-start.5 = (bf16[256,40]{0,1:T(8,128)(2,1)S(1)}, bf16[256,40]{0,1:T(8,128)(2,1)}, u32[]{:S(2)}) copy-start(bf16[256,40]{0,1:T(8,128)(2,1)} %param.15) | copy-start | bytes 61444
  1.3 2.5 %copy-start.4 = (bf16[256,256]{1,0:T(8,128)(2,1)S(1)}, bf16[256,256]{1,0:T(8,128)(2,1)}, u32[]{:S(2)}) copy-start(bf16[256,256]{1,0:T(8,128)(2,1)} %param.14) | copy-start | bytes 393220
  1.3 2.7 %copy-start.3 = (bf16[360,256]{1,0:T(8,128)(2,1)S(1)}, bf16[360,256]{1,0:T(8,128)(2,1)}, u32[]{:S(2)}) copy-start(bf16[360,256]{1,0:T(8,128)(2,1)} %param.13) | copy-start | bytes 552964
  1.8 2.4 %copy-start.7 = (f32[4]{0:T(128)S(1)}, f32[4]{0:T(128)}, u32[]{:S(2)}) copy-start(f32[4]{0:T(128)} %param.10) | copy-start | bytes 52
  1.8 2.4 %copy-start.8 = (f32[4]{0:T(128)S(1)}, f32[4]{0:T(128)}, u32[]{:S(2)}) copy-start(f32[4]{0:T(128)} %param.9) | copy-start | bytes 52
  1.8 3.3 %collective-permute-start = (bf16[20,8,128]{2,1,0:T(8,128)(2,1)S(1)}, bf16[20,8,128]{2,1,0:T(8,128)(2,1)S(1)}, u32[]{:S(2)}, u32[]{:S(2)}) collective-permute-start(bf16[20,8,128]{2,1,0:T(8,128)(2,1)S(1)} %get-tuple-element.23), channel_id=1, source_target_pairs={{0,2},{4,6},{8,10},{12,14},{16,18},{20,22},{24,26},{28,30},{2,0},{... | collective-permute-start | bytes 122888 | tf_op jit(solution)/shard_map/ppermute | solution.py:423
  1.9 5.3 %collective-permute-start.1 = (bf16[20,8,128]{2,1,0:T(8,128)(2,1)S(1)}, bf16[20,8,128]{2,1,0:T(8,128)(2,1)S(1)}, u32[]{:S(2)}, u32[]{:S(2)}) collective-permute-start(bf16[20,8,128]{2,1,0:T(8,128)(2,1)S(1)} %get-tuple-element.24), channel_id=1, source_target_pairs={{2,4},{6,8},{10,12},{18,20},{22,24},{26,28},{4,2},{8,6},{12,10},{2... | collective-permute-start | bytes 122888 | tf_op jit(solution)/shard_map/ppermute | solution.py:424
  7.2 2.8 %copy-start.1 = (f32[4,5,1,128,128]{4,3,2,1,0:T(8,128)S(1)}, f32[4,5,1,128,128]{4,3,2,1,0:T(8,128)}, u32[]{:S(2)}) copy-start(f32[4,5,1,128,128]{4,3,2,1,0:T(8,128)} %param.8) | copy-start | bytes 3932164
  7.3 5.2 %collective-permute-start.2 = (bf16[160,128]{1,0:T(8,128)(2,1)S(1)}, bf16[160,128]{1,0:T(8,128)(2,1)S(1)}, u32[]{:S(2)}, u32[]{:S(2)}) collective-permute-start(bf16[160,128]{1,0:T(8,128)(2,1)S(1)} %get-tuple-element.27), channel_id=1, source_target_pairs={{0,16},{2,18},{4,20},{6,22},{8,24},{10,26},{12,28},{14,30},{16,0},... | collective-permute-start | bytes 122888 | tf_op jit(solution)/shard_map/ppermute | solution.py:454
  10.9 7.5 %copy-start.2 = (s32[9,1,128,128]{3,2,1,0:T(8,128)S(1)}, s32[9,1,128,128]{3,2,1,0:T(8,128)}, u32[]{:S(2)}) copy-start(s32[9,1,128,128]{3,2,1,0:T(8,128)} %table_ref.3) | copy-start | bytes 1769476
  10.9 7.4 %collective-permute-start.4 = (bf16[720,128]{1,0:T(8,128)(2,1)S(1)}, bf16[720,128]{1,0:T(8,128)(2,1)S(1)}, u32[]{:S(2)}, u32[]{:S(2)}) collective-permute-start(bf16[720,128]{1,0:T(8,128)(2,1)S(1)} %shard_map.85), channel_id=1, source_target_pairs={{0,1},{1,0},{2,3},{3,2},{4,5},{5,4},{6,7},{7,6},{8,9},{9,8},{10,11... | collective-permute-start | bytes 552968 | tf_op jit(solution)/shard_map/ppermute | solution.py:484
  15.4 8.0 %collective-permute-start.3 = (bf16[720,128]{1,0:T(8,128)(2,1)S(1)}, bf16[720,128]{1,0:T(8,128)(2,1)S(1)}, u32[]{:S(2)}, u32[]{:S(2)}) collective-permute-start(bf16[720,128]{1,0:T(8,128)(2,1)S(1)} %get-tuple-element.29), channel_id=1, source_target_pairs={{0,1},{1,0},{2,3},{3,2},{4,5},{5,4},{6,7},{7,6},{8,9},{9,8},{10,11... | collective-permute-start | bytes 552968 | tf_op jit(solution)/shard_map/ppermute | solution.py:484
  21.8 6.3 %collective-permute-start.6 = (bf16[640,128]{1,0:T(8,128)(2,1)S(1)}, bf16[640,128]{1,0:T(8,128)(2,1)S(1)}, u32[]{:S(2)}, u32[]{:S(2)}) collective-permute-start(bf16[640,128]{1,0:T(8,128)(2,1)S(1)} %get-tuple-element.36), channel_id=1, source_target_pairs={{0,1},{1,0},{2,3},{3,2},{4,5},{5,4},{6,7},{7,6},{8,9},{9,8},{10,11... | collective-permute-start | bytes 491528 | tf_op jit(solution)/shard_map/ppermute | solution.py:484
  26.8 6.0 %collective-permute-start.5 = (bf16[640,128]{1,0:T(8,128)(2,1)S(1)}, bf16[640,128]{1,0:T(8,128)(2,1)S(1)}, u32[]{:S(2)}, u32[]{:S(2)}) collective-permute-start(bf16[640,128]{1,0:T(8,128)(2,1)S(1)} %get-tuple-element.34), channel_id=1, source_target_pairs={{0,1},{1,0},{2,3},{3,2},{4,5},{5,4},{6,7},{7,6},{8,9},{9,8},{10,11... | collective-permute-start | bytes 491528 | tf_op jit(solution)/shard_map/ppermute | solution.py:484
